TPU v7x, 1024 devices: a whole 8x8x8 slice. The times are simulated.
1024 devices in a mesh: tile: 64 (over y_hi, x, core), node: 16 (over z, y_lo).
Axes of the slice: x: 8, y: 8 (y_hi: 4, y_lo: 2; y = y_hi * 2 + y_lo), z: 8, core: 2. Of those that a mesh axis runs over, the one named last changes fastest.
Arguments:
- mask_field: float32 [512, 8192], P(None, 'tile'), may hold values from -1 to 1
- kernel_taps: float32 [16, 8, 2, 48, 65], P('node'), may hold values from -0.5 to 0.5
- kernel_weights: float32 [16, 8], P('node'), may hold values from 0.02 to 0.2
- node_weights: float32 [16], replicated, may hold values from 0.03125 to 0.125
- node_index: int32 [16, 2], replicated, may hold values from 0 to 4
- freq_index: int32 [48], replicated, may hold values from -256 to 255, as said below
- chaos_weights: float32 [15], replicated, may hold values from 1 to 4
- target: bfloat16 [15, 512, 8192], P(None, None, 'tile'), may hold values from -3 to 3
Outputs:
- mask_gradient: float32 [512, 8192], P('node', 'tile')
Inputs may be any that keep to these rules, and one draw needn't show every extreme that they name: `freq_index`: 48 distinct frequencies.
All inputs are finite; a program needn't handle non-finite values.
Results may differ from a plain program's by a relative error of at most 0.00085.
Values may be sent and summed in bfloat16 or wider, within the bound.
No kernel may reach another device: no remote copies, remote signals or barrier semaphores. Data moves between devices by JAX's collectives and lax.ppermute only.
A program may use at most 64 MiB of HBM per device.

v0:
```python
import math

import jax
import jax.numpy as jnp
from jax import lax
from jax.sharding import PartitionSpec as P

LEVELS = 5


highest = lax.Precision.HIGHEST
resist_slope = 4.0
resist_level = 0.6


def with_halo(value, sides, width):
    for axis, dim in sides:
        size, length = (lax.axis_size(axis), value.shape[dim])
        up = [(i, (i + 1) % size) for i in range(size - 1)]
        down = [(j, i) for i, j in up]
        last = lax.slice_in_dim(value, length - width, length, axis=dim)
        initial = lax.slice_in_dim(value, 0, width, axis=dim)
        before = lax.ppermute(last, axis, up)
        after = lax.ppermute(initial, axis, down)
        value = jnp.concatenate([before, value, after], axis=dim)
    return value


def spectra_tables(freq_index, pixel_rows):
    row_line = jnp.arange(pixel_rows, dtype=jnp.int32)
    phase_angle = jnp.mod(freq_index[:, None] * row_line[None, :], pixel_rows).astype(
        jnp.float32
    ) * (2.0 * math.pi / pixel_rows)
    cosine_table = jnp.cos(phase_angle)
    sine_table = jnp.sin(phase_angle)
    forward = jnp.concatenate([cosine_table, -sine_table], 0) / math.sqrt(pixel_rows)
    freq_count = freq_index.shape[0]
    upper = jnp.concatenate([cosine_table.T, -sine_table.T], 1)
    lower = jnp.concatenate([sine_table.T, cosine_table.T], 1)
    inverse = jnp.concatenate([upper, lower], 0) / math.sqrt(freq_count)
    return (forward, inverse)


def legendre_set(coordinate):
    square = coordinate * coordinate
    return [
        jnp.ones_like(coordinate),
        coordinate,
        1.5 * square - 0.5,
        (2.5 * square - 1.5) * coordinate,
        (4.375 * square - 3.75) * square + 0.375,
    ]


def level_coords(node_index):
    return node_index.astype(jnp.float32) * (2.0 / (LEVELS - 1)) - 1.0


def chaos_basis(node_index):
    coords = level_coords(node_index)
    focus_poly = legendre_set(coords[:, 0])
    dose_poly = legendre_set(coords[:, 1])
    columns = []
    for degree in range(5):
        for focus_order in range(degree, -1, -1):
            columns.append(focus_poly[focus_order] * dose_poly[degree - focus_order])
    return jnp.stack(columns, 1)


def combined_taps(taps_node):
    taps_real = taps_node[:, 0]
    taps_imag = taps_node[:, 1]
    real_out = jnp.stack([taps_real, -taps_imag], 1)
    imag_out = jnp.stack([taps_imag, taps_real], 1)
    return jnp.stack([real_out, imag_out], 1)


def image_forward(spectrum, combined, weights_node, dose_scale, inverse, col_count, radius):
    kernel_count = combined.shape[0]
    freq_count = combined.shape[3]
    tap_count = 2 * radius + 1
    shifted = jnp.stack(
        [spectrum[:, offset : offset + col_count] for offset in range(tap_count)], 1
    )
    shifted = shifted.reshape(2, freq_count, tap_count, col_count)
    band = jnp.einsum("cfsx,kdcfs->kdfx", shifted, combined, precision=highest)
    band = band.reshape(kernel_count, 2 * freq_count, col_count)
    fields = jnp.einsum("yf,kfx->kyx", inverse, band, precision=highest)
    pixel_rows = inverse.shape[0] // 2
    halves = fields.reshape(kernel_count, 2, pixel_rows, col_count)
    powers = halves[:, 0] * halves[:, 0] + halves[:, 1] * halves[:, 1]
    intensity = jnp.einsum("k,kyx->yx", weights_node, powers, precision=highest)
    resist = jax.nn.sigmoid(resist_slope * (dose_scale * intensity - resist_level))
    return (resist, halves)


def image_backward(
    pressure, resist, halves, combined, weights_node, dose_scale, inverse, col_count, radius
):
    kernel_count = combined.shape[0]
    freq_count = combined.shape[3]
    pixel_rows = inverse.shape[0] // 2
    tap_count = 2 * radius + 1
    slope = pressure * resist * (1.0 - resist) * (resist_slope * dose_scale)
    dfields = (2.0 * weights_node)[:, None, None, None] * halves * slope[None, None]
    dfields = dfields.reshape(kernel_count, 2 * pixel_rows, col_count)
    dband = jnp.einsum("yf,kyx->kfx", inverse, dfields, precision=highest)
    dband = dband.reshape(kernel_count, 2, freq_count, col_count)
    spread = jnp.einsum("kdfx,kdcfs->cfsx", dband, combined, precision=highest)
    total = jnp.zeros((2, freq_count, col_count + 2 * radius), jnp.float32)
    for offset in range(tap_count):
        total = total + jnp.pad(
            spread[:, :, offset], ((0, 0), (0, 0), (offset, 2 * radius - offset))
        )
    return total.reshape(2 * freq_count, col_count + 2 * radius)


def local(
    mask_field,
    kernel_taps,
    kernel_weights,
    node_weights,
    node_index,
    freq_index,
    chaos_weights,
    target,
):
    pixel_rows, col_count = mask_field.shape
    radius = (kernel_taps.shape[-1] - 1) // 2
    node_count = lax.axis_size("node")
    node_id = lax.axis_index("node")
    row_share = pixel_rows // node_count
    first_row = node_id * row_share
    forward, inverse = spectra_tables(freq_index, pixel_rows)
    padded = with_halo(mask_field, (("tile", 1),), radius)
    spectrum = jnp.dot(forward, padded, precision=highest)
    node_basis = chaos_basis(node_index)
    own_basis = lax.dynamic_index_in_dim(node_basis, node_id, 0, keepdims=False)
    own_dose = 1.0 + 0.1 * lax.dynamic_index_in_dim(
        level_coords(node_index)[:, 1], node_id, 0, keepdims=False
    )
    own_weight = lax.dynamic_index_in_dim(node_weights, node_id, 0, keepdims=False)
    combined = combined_taps(kernel_taps[0])
    resist, halves = image_forward(
        spectrum, combined, kernel_weights[0], own_dose, inverse, col_count, radius
    )
    rounded = resist.astype(jnp.bfloat16)
    scaled = own_weight * own_basis
    coefficient = lax.psum_scatter(
        (scaled[:, None, None] * rounded.astype(jnp.float32)[None]).astype(jnp.bfloat16),
        "node",
        scatter_dimension=1,
        tiled=True,
    ).astype(jnp.float32)
    target_rows = lax.dynamic_slice_in_dim(target, first_row, row_share, 1).astype(jnp.float32)
    mixed_terms = lax.all_gather(
        chaos_weights[:, None, None] * jnp.tanh(coefficient - target_rows),
        "node",
        axis=1,
        tiled=True,
    )
    pressure = own_weight * jnp.einsum("j,jyx->yx", own_basis, mixed_terms, precision=highest)
    dspec = image_backward(
        pressure, resist, halves, combined, kernel_weights[0], own_dose, inverse, col_count, radius
    )
    summed = lax.psum_scatter(
        jnp.dot(forward.T, dspec, precision=highest), "node", scatter_dimension=0, tiled=True
    )
    edge_cols = jnp.concatenate([summed[:, :radius], summed[:, col_count + radius :]], 1)
    beyond = with_halo(edge_cols, (("tile", 1),), radius)
    interior = summed[:, radius : col_count + radius]
    left_in = jnp.pad(beyond[:, :radius], ((0, 0), (0, col_count - radius)))
    right_in = jnp.pad(beyond[:, 3 * radius :], ((0, 0), (col_count - radius, 0)))
    return interior + left_in + right_in


def solution(mesh):
    placed = (
        P(None, "tile"),
        P("node", None, None, None, None),
        P("node", None),
        P(),
        P(),
        P(),
        P(),
        P(None, None, "tile"),
    )
    return jax.shard_map(
        local, mesh=mesh, in_specs=placed, out_specs=P("node", "tile"), check_vma=False
    )
```

profile of v0, /device:TPU:47, one launch (start us, length us, event | category | flops | bytes accessed | tf_op | source)
XLA Modules:
  0.0 441.4 jit_solution(5803529019614546245)
XLA Ops:
  7.8 6.0 %collective-permute-start = (f32[512,32]{1,0:T(8,128)S(1)}, f32[512,32]{1,0:T(8,128)S(1)}, u32[]{:S(2)}, u32[]{:S(2)}) collective-permute-start(f32[512,32]{1,0:T(8,128)S(1)} %get-tuple-element.77), channel_id=1, source_target_pairs={{0,16},{16,32},{32,48},{48,64},{64,80},{80,96},{96,112},{112,128},... | collective-permute-start | bytes 196616 | tf_op jit(solution)/shard_map/ppermute | solution.py:23
  13.8 1.9 collective-permute-start.1
  16.9 1.9 fusion.46
  25.1 2.6 collective-permute-done.1
  72.7 13.1 %stack.300 = f32[2,48,65,128]{3,2,0,1:T(8,128)S(1)} concatenate(f32[2,48,1,128]{3,2,0,1:T(1,128)} %copy.146, f32[2,48,1,128]{3,2,0,1:T(1,128)} %copy.147, f32[2,48,1,128]{3,2,0,1:T(1,128)} %copy.148, f32[2,48,1,128]{3,2,0,1:T(1,128)} %copy.149, f32[2,48,1,128]{3,2,0,1:T(1,128)} %copy.150, f32[2,48,1,128]{3,2,0,1:T(1,128)} %copy.151, f32[2,48,1,128]{3,2,0,1:T(1,128)} %copy.152, ...), dimensions={2} | concatenate | bytes 6389760 | tf_op jit(solution)/shard_map/stack | solution.py:82
  85.8 4.3 fusion.12
  90.3 5.2 %convolution_bitcast_fusion = f32[8,1024,128]{1,2,0:T(8,128)} fusion(f32[8,96,128]{2,1,0:T(8,128)S(1)} %bitcast.333, f32[512,48]{0,1:T(8,128)S(1)} %copy-done.11, f32[512,48]{0,1:T(8,128)S(1)} %copy-done.9, f32[512,48]{0,1:T(8,128)S(1)} %copy-done.7), kind=kOutput, calls=%fused_computation.8 | convolution fusion | flops 1208352768 | bytes 4882432 | tf_op jit(solution)/shard_map/yf,kfx->kyx/dot_general | solution.py:88
  95.5 6.7 %reshape.167 = f32[8,2,512,128]{2,1,3,0:T(2,128)} reshape(f32[8,1024,128]{1,2,0:T(8,128)} %convolution_bitcast_fusion) | data formatting | bytes 8388608 | tf_op jit(solution)/shard_map/reshape | solution.py:90
  102.1 6.5 %fusion.7 = f32[8,1,512,128]{2,1,3,0:T(1,128)S(1)} fusion(f32[8,2,512,128]{2,1,3,0:T(2,128)} %reshape.167), kind=kLoop, calls=%fused_computation.10 | loop fusion | flops 1572864 | bytes 6291456 | tf_op jit(solution)/shard_map/add | solution.py:91
  108.6 3.3 copy.290
  112.0 3.4 fusion.8
  115.5 1.8 multiply_convert_fusion
  117.4 80.7 %reduce-scatter.3.cloned.1.call-done = bf16[15,32,128]{2,1,0:T(8,128)(2,1)} async-done(((bf16[15,512,128]{2,1,0:T(8,128)(2,1)}), bf16[15,32,128]{2,1,0:T(8,128)(2,1)}) %reduce-scatter.3.cloned.1.call-update) | async-done | bytes 122896 | tf_op jit(solution)/shard_map/reduce_scatter | solution.py:149
  198.1 1.7 tanh_multiply_fusion
  200.1 111.2 %all-gather.2.cloned.1.call-done = f32[15,512,128]{2,1,0:T(8,128)} async-done(((f32[15,32,128]{2,1,0:T(8,128)}), f32[15,512,128]{2,1,0:T(8,128)}) %all-gather.2.cloned.1.call-update) | async-done | bytes 3932176 | tf_op jit(solution)/shard_map/all_gather | solution.py:156
  311.3 6.2 %fusion = f32[1,512,128]{2,0,1:T(1,128)S(1)} fusion(f32[15,512,128]{2,1,0:T(8,128)} %all-gather.2.cloned.1.call-done, f32[15]{0:T(128)S(1)} %dynamic-slice_reduce_fusion), kind=kOutput, calls=%fused_computation | convolution fusion | flops 11796480 | bytes 4194364 | tf_op jit(solution)/shard_map/j,jyx->yx/dot_general | solution.py:162
  318.8 6.7 %fusion.2 = f32[8,128,96]{1,2,0:T(8,128)S(1)} fusion(f32[8,1024,128]{1,2,0:T(8,128)} %convolution_bitcast_fusion, f32[1024,128]{0,1:T(8,128)S(1)} %bitcast.331, f32[8]{0:T(128)S(1)} %bitcast_multiply_fusion, f32[512,48]{0,1:T(8,128)S(1)} %copy-done.12, f32[512,48]{0,1:T(8,128)S(1)} %copy-done.10, f32[512,48]{0,1:T(8,128)S(1)} %copy-done.8), kind=kOutput, calls=%fused_computation.2 | convolution fusion | flops 1210449920 | bytes 5406752 | tf_op jit(solution)/shard_map/yf,kyx->kfx/dot_general | solution.py:107
  325.5 5.9 %convolution_bitcast_fusion.1 = f32[2,48,65,128]{3,2,0,1:T(8,128)S(1)} fusion(f32[8,1,2,48,65]{4,0,2,1,3:T(8,128)S(1)} %copy-done.1, f32[8,1,2,48,65]{4,0,2,1,3:T(8,128)S(1)} %copy-done, f32[8,2,48,128,1]{3,2,1,0,4:T(8,128)S(1)} %bitcast.332), kind=kOutput, calls=%fused_computation.16 | convolution fusion | flops 153454080 | bytes 3987456 | tf_op jit(solution)/shard_map/kdfx,kdcfs->cfsx/dot_general | solution.py:109
  334.5 6.8 %pad_add_fusion = f32[2,48,192]{2,0,1:T(2,128)S(1)} fusion(f32[2,48,128]{2,0,1:T(2,128)S(1)} %bitcast.351, f32[2,48,128]{2,0,1:T(2,128)S(1)} %bitcast.352, f32[2,48,128]{2,0,1:T(2,128)S(1)} %bitcast.449, f32[2,48,128]{2,0,1:T(2,128)S(1)} %bitcast.450, f32[2,48,128]{2,0,1:T(2,128)S(1)} %bitcast.451, f32[2,48,128]{2,0,1:T(2,128)S(1)} %bitcast.452, ...), kind=kLoop, calls=%fused_computation.52 | loop fusion | flops 1179648 | bytes 3268608 | tf_op jit(solution)/shard_map/add | solution.py:112
  342.7 64.3 %reduce-scatter.5.cloned.1.call-done = f32[32,192]{1,0:T(8,128)} async-done(((f32[512,192]{1,0:T(8,128)}), f32[32,192]{1,0:T(8,128)}) %reduce-scatter.5.cloned.1.call-update) | async-done | bytes 24592 | tf_op jit(solution)/shard_map/reduce_scatter | solution.py:166
  407.8 16.1 %collective-permute-start.2 = (f32[32,32]{1,0:T(8,128)S(1)}, f32[32,32]{1,0:T(8,128)S(1)}, u32[]{:S(2)}, u32[]{:S(2)}) collective-permute-start(f32[32,32]{1,0:T(8,128)S(1)} %get-tuple-element.146), channel_id=1, source_target_pairs={{0,16},{16,32},{32,48},{48,64},{64,80},{80,96},{96,112},{112,128},... | collective-permute-start | bytes 12296 | tf_op jit(solution)/shard_map/ppermute | solution.py:23
  424.0 1.9 collective-permute-start.3
  425.9 7.3 %collective-permute-done.3 = f32[32,32]{1,0:T(8,128)S(1)} collective-permute-done((f32[32,32]{1,0:T(8,128)S(1)}, f32[32,32]{1,0:T(8,128)S(1)}, u32[]{:S(2)}, u32[]{:S(2)}) %collective-permute-start.3) | collective-permute-done | bytes 4128 | tf_op jit(solution)/shard_map/ppermute | solution.py:24
  433.2 1.4 fusion.47
  (136 shorter events, 59.9 us)
Async XLA Ops:
  6.5 21.2 %copy-start.2 = (f32[512,128]{1,0:T(8,128)S(1)}, f32[512,128]{1,0:T(8,128)}, u32[]{:S(2)}) copy-start(f32[512,128]{1,0:T(8,128)} %param.8) | copy-start | bytes 786436
  6.5 191.6 %reduce-scatter.3.cloned.1.call-start = ((), (), s32[]{:S(2)}) async-start(), calls=%async_computation.2 | async-start | bytes 2088960 | tf_op jit(solution)/shard_map/reduce_scatter | solution.py:149
  7.8 17.4 %collective-permute-start = (f32[512,32]{1,0:T(8,128)S(1)}, f32[512,32]{1,0:T(8,128)S(1)}, u32[]{:S(2)}, u32[]{:S(2)}) collective-permute-start(f32[512,32]{1,0:T(8,128)S(1)} %get-tuple-element.77), channel_id=1, source_target_pairs={{0,16},{16,32},{32,48},{48,64},{64,80},{80,96},{96,112},{112,128},... | collective-permute-start | bytes 196616 | tf_op jit(solution)/shard_map/ppermute | solution.py:23
  13.8 13.9 %collective-permute-start.1 = (f32[512,32]{1,0:T(8,128)S(1)}, f32[512,32]{1,0:T(8,128)S(1)}, u32[]{:S(2)}, u32[]{:S(2)}) collective-permute-start(f32[512,32]{1,0:T(8,128)S(1)} %get-tuple-element.78), channel_id=1, source_target_pairs={{16,0},{32,16},{48,32},{64,48},{80,64},{96,80},{112,96},{128,112},... | collective-permute-start | bytes 196616 | tf_op jit(solution)/shard_map/ppermute | solution.py:24
  16.8 12.1 %copy-start.3 = (f32[48,512]{1,0:T(8,128)}, f32[48,512]{1,0:T(8,128)S(1)}, u32[]{:S(2)}) copy-start(f32[48,512]{1,0:T(8,128)S(1)} %get-tuple-element.163) | copy-start | bytes 294916
  16.9 12.1 %copy-start.5 = (f32[48,512]{1,0:T(8,128)}, f32[48,512]{1,0:T(8,128)S(1)}, u32[]{:S(2)}) copy-start(f32[48,512]{1,0:T(8,128)S(1)} %get-tuple-element.164) | copy-start | bytes 294916
  85.8 4.5 %copy-start.7 = (f32[512,48]{0,1:T(8,128)S(1)}, f32[512,48]{0,1:T(8,128)}, u32[]{:S(2)}) copy-start(f32[512,48]{0,1:T(8,128)} %get-tuple-element.160) | copy-start | bytes 294916
  85.8 4.5 %copy-start.9 = (f32[512,48]{0,1:T(8,128)S(1)}, f32[512,48]{0,1:T(8,128)}, u32[]{:S(2)}) copy-start(f32[512,48]{0,1:T(8,128)} %get-tuple-element.161) | copy-start | bytes 294916
  85.8 4.5 %copy-start.11 = (f32[512,48]{0,1:T(8,128)S(1)}, f32[512,48]{0,1:T(8,128)}, u32[]{:S(2)}) copy-start(f32[512,48]{0,1:T(8,128)} %get-tuple-element.162) | copy-start | bytes 294916
  108.6 3.4 copy-start.13
  112.0 86.1 %copy-start.14 = (f32[15]{0:T(128)S(1)}, f32[15]{0:T(128)}, u32[]{:S(2)}) copy-start(f32[15]{0:T(128)} %param.14) | copy-start | bytes 184
  117.3 194.0 %all-gather.2.cloned.1.call-start = ((), (), s32[]{:S(2)}) async-start(), calls=%async_computation.3 | async-start | bytes 4177920 | tf_op jit(solution)/shard_map/all_gather | solution.py:156
  199.9 207.2 %reduce-scatter.5.cloned.1.call-start = ((), (), s32[]{:S(2)}) async-start(), calls=%async_computation.4 | async-start | bytes 557056 | tf_op jit(solution)/shard_map/reduce_scatter | solution.py:166
  200.1 118.7 %copy-start.8 = (f32[512,48]{0,1:T(8,128)S(1)}, f32[512,48]{0,1:T(8,128)}, u32[]{:S(2)}) copy-start(f32[512,48]{0,1:T(8,128)} %get-tuple-element.160) | copy-start | bytes 294916
  200.1 118.7 %copy-start.10 = (f32[512,48]{0,1:T(8,128)S(1)}, f32[512,48]{0,1:T(8,128)}, u32[]{:S(2)}) copy-start(f32[512,48]{0,1:T(8,128)} %get-tuple-element.161) | copy-start | bytes 294916
  200.1 118.7 %copy-start.12 = (f32[512,48]{0,1:T(8,128)S(1)}, f32[512,48]{0,1:T(8,128)}, u32[]{:S(2)}) copy-start(f32[512,48]{0,1:T(8,128)} %get-tuple-element.162) | copy-start | bytes 294916
  318.5 7.1 %copy-start = (f32[8,1,2,48,65]{4,0,2,1,3:T(8,128)S(1)}, f32[8,1,2,48,65]{4,0,2,1,3:T(8,128)}, u32[]{:S(2)}) copy-start(f32[8,1,2,48,65]{4,0,2,1,3:T(8,128)} %get-tuple-element.79) | copy-start | bytes 599044
  318.5 7.1 %copy-start.1 = (f32[8,1,2,48,65]{4,0,2,1,3:T(8,128)S(1)}, f32[8,1,2,48,65]{4,0,2,1,3:T(8,128)}, u32[]{:S(2)}) copy-start(f32[8,1,2,48,65]{4,0,2,1,3:T(8,128)} %get-tuple-element.80) | copy-start | bytes 599044
  333.3 8.0 %copy-start.4 = (f32[48,512]{1,0:T(8,128)S(1)}, f32[48,512]{1,0:T(8,128)}, u32[]{:S(2)}) copy-start(f32[48,512]{1,0:T(8,128)} %copy-done.3) | copy-start | bytes 294916
  333.3 8.0 %copy-start.6 = (f32[48,512]{1,0:T(8,128)S(1)}, f32[48,512]{1,0:T(8,128)}, u32[]{:S(2)}) copy-start(f32[48,512]{1,0:T(8,128)} %copy-done.5) | copy-start | bytes 294916
  407.8 18.1 %collective-permute-start.2 = (f32[32,32]{1,0:T(8,128)S(1)}, f32[32,32]{1,0:T(8,128)S(1)}, u32[]{:S(2)}, u32[]{:S(2)}) collective-permute-start(f32[32,32]{1,0:T(8,128)S(1)} %get-tuple-element.146), channel_id=1, source_target_pairs={{0,16},{16,32},{32,48},{48,64},{64,80},{80,96},{96,112},{112,128},... | collective-permute-start | bytes 12296 | tf_op jit(solution)/shard_map/ppermute | solution.py:23
  424.0 9.3 %collective-permute-start.3 = (f32[32,32]{1,0:T(8,128)S(1)}, f32[32,32]{1,0:T(8,128)S(1)}, u32[]{:S(2)}, u32[]{:S(2)}) collective-permute-start(f32[32,32]{1,0:T(8,128)S(1)} %get-tuple-element.147), channel_id=1, source_target_pairs={{16,0},{32,16},{48,32},{64,48},{80,64},{96,80},{112,96},{128,112},... | collective-permute-start | bytes 12296 | tf_op jit(solution)/shard_map/ppermute | solution.py:24
Sparse Core Ops, SparseCore 0:
  117.5 80.5 reduce-scatter.2
  201.1 110.1 all-gather.1
  342.9 64.1 reduce-scatter.4
where the time goes:
time: 448 us; the launch traced here: 441 us
  waiting for transfers between devices  266 us (59%)
  local copies, waits for them, and re-layouts  75.8 us (17%)
  matrix products  33.8 us (8%)
  starting transfers between devices  26.2 us (6%)
  other arithmetic  25 us (6%)
  between operations  14.5 us (3%)
    all_gather x1, waiting for transfers between devices, local(): lax.all_gather(chaos_weights[:, None, None] * jnp.tanh(coefficient - targ...  111 us
    reduce_scatter x1, waiting for transfers between devices, local(): lax.psum_scatter((scaled[:, None, None] * rounded.astype(jnp.float32)[Non...  80.7 us
    reduce_scatter x1, waiting for transfers between devices, local(): lax.psum_scatter(jnp.dot(forward.T, dspec, precision=highest), 'node', sc...  64.3 us
    another operation x66, local copies, waits for them, and re-layouts, image_forward(): jnp.stack([spectrum[:, offset:offset + col_count] for offset in range(tap...  56.3 us
    ppermute x2, starting transfers between devices, with_halo(): before = lax.ppermute(last, axis, up)  22.1 us
    ppermute x2, waiting for transfers between devices, with_halo(): after = lax.ppermute(initial, axis, down)  9.91 us
  transfers between devices with their start and end apart: 7, of which 5 were waited for; matrix products, arithmetic and copies ran while one was open for 2% of the time, Pallas kernels for 0%

commit v1 on v0

v1 whole, which is shorter than its diff:
```python
import functools
import math

import jax
import jax.numpy as jnp
import ml_dtypes
import numpy as np
from jax import lax
from jax.experimental import pallas as pl
from jax.experimental.pallas import tpu as pltpu
from jax.sharding import PartitionSpec as P

LEVELS = 5
resist_slope = 4.0
resist_level = 0.6
degrees = [(d - q, q) for d in range(5) for q in range(d + 1)]
f32, bf16 = jnp.float32, jnp.bfloat16
vmem = pl.BlockSpec(memory_space=pltpu.VMEM)
smem = pl.BlockSpec(memory_space=pltpu.SMEM)
params = pltpu.CompilerParams(vmem_limit_bytes=48 << 20)


def parts_of(value):
    high = value.astype(bf16)
    return high, (value - high.astype(f32)).astype(bf16)


def mm(a, b):
    return jnp.dot(a, b, preferred_element_type=f32)


def mm3(a, b):
    return mm(a[0], b[0]) + mm(a[0], b[1]) + mm(a[1], b[0])


def cosine(turn, period):
    turn = jnp.bitwise_and(turn, period - 1)
    half = jnp.minimum(turn, period - turn)
    far = half > period // 4
    angle = jnp.where(far, period // 2 - half, half).astype(f32) * (2.0 * math.pi / period)
    z = angle * angle
    poly = jnp.full_like(z, 1.0 / math.factorial(12))
    for order in (10, 8, 6, 4, 2, 0):
        sign = -1.0 if order % 4 == 2 else 1.0
        poly = poly * z + sign / math.factorial(order)
    return jnp.where(far, -poly, poly)


def column_waves(length):
    turn = (np.arange(length)[:, None] * np.arange(length)[None, :]) % length
    wave = np.concatenate([np.cos(2 * np.pi * turn / length), np.sin(2 * np.pi * turn / length)], 1)
    high = wave.astype(np.float32).astype(ml_dtypes.bfloat16)
    low = (wave - high.astype(np.float64)).astype(np.float32).astype(ml_dtypes.bfloat16)
    return high, low


def tables_kernel(freq, taps, weights, wave_hi, wave_lo, u_ref, fh_ref, fl_ref, gr_ref, gi_ref):
    rows = u_ref.shape[0]
    count = freq.shape[0]
    kernels, tap_count = taps.shape[1], taps.shape[4]
    span = wave_hi.shape[0]
    radius = (tap_count - 1) // 2
    f_row = lax.broadcasted_iota(jnp.int32, (2 * count, rows), 0)
    f_freq = jnp.zeros((2 * count, 128), jnp.int32)
    line = lax.broadcasted_iota(jnp.int32, (2 * count, 128), 0)
    u_freq = jnp.zeros((8, 128), jnp.int32)
    lane = lax.broadcasted_iota(jnp.int32, (8, 128), 1)
    for i in range(count):
        value = freq[i]
        f_freq = jnp.where((line == i) | (line == i + count), value, f_freq)
        u_freq = jnp.where((lane == i) | (lane == i + count), value, u_freq)
    y_lane = lax.broadcasted_iota(jnp.int32, (2 * count, rows), 1)
    f_full = jnp.concatenate([f_freq] * (rows // 128), 1)
    quarter = rows // 4
    f_table = cosine(f_full * y_lane + jnp.where(f_row >= count, quarter, 0), rows)
    fh_ref[...], fl_ref[...] = parts_of(f_table)
    u_full = jnp.concatenate([u_freq] * (rows // 8), 0)
    u_lane = lax.broadcasted_iota(jnp.int32, (rows, 128), 1)
    u_y = lax.broadcasted_iota(jnp.int32, (rows, 128), 0)
    u_table = cosine(u_full * u_y + jnp.where(u_lane >= count, quarter, 0), rows)
    u_table = jnp.where(u_lane < 2 * count, u_table, 0.0)
    high, low = parts_of(u_table)
    u_ref[:, 0:128] = high
    u_ref[:, 128:256] = high
    u_ref[:, 256:384] = low
    side = [jnp.concatenate([w[span - radius : span], w[0 : tap_count - radius]], 0) for w in (wave_hi, wave_lo)]
    scale = jnp.sqrt(weights[...]) * (1.0 / (span * math.sqrt(count)))
    for k in range(kernels):
        both = parts_of(taps[0, k].reshape(2 * count, tap_count))
        prod = mm3(both, side)
        amount = scale[0:1, k : k + 1]
        gr_ref[k] = (prod[:count, :span] - prod[count:, span:]) * amount
        gi_ref[k] = (prod[:count, span:] + prod[count:, :span]) * amount


def forward_kernel(
    radius, dose, mask, before, after, fh, fl, gr, gi, u, wave_hi, wave_lo,
    image_ref, slope_ref, fields_ref, bh, bl, r, total,
):
    rows, cols = mask.shape
    kernels, count, span = gr.shape
    lane = lax.broadcasted_iota(jnp.int32, (rows, cols), 1)
    beyond = jnp.where(lane < radius, after[...], jnp.where(lane >= cols - radius, before[...], 0.0))
    padded = jnp.concatenate([mask[...], beyond], 1)
    spectrum = mm3((fh[...], fl[...]), parts_of(padded)) * (1.0 / math.sqrt(rows))
    wave = (wave_hi[...], wave_lo[...])
    prod = mm3(parts_of(spectrum), wave)
    a_re = prod[:count, :span] + prod[count:, span:]
    a_im = prod[count:, :span] - prod[:count, span:]
    for k in range(kernels):
        b_re = gr[k] * a_re - gi[k] * a_im
        b_im = gr[k] * a_im + gi[k] * a_re
        for d, value in ((0, b_re), (1, b_im)):
            at = pl.ds((2 * k + d) * count, count)
            bh[at, :], bl[at, :] = parts_of(value)
    near = [jnp.concatenate([w[:, 0:cols], w[:, span : span + cols]], 1) for w in (wave_hi, wave_lo)]
    r[...] = jnp.zeros(r.shape, bf16)
    for k in range(kernels):
        at = pl.ds(2 * k * count, 2 * count)
        q = mm3((bh[at, :], bl[at, :]), near)
        band_re = q[:count, :cols] - q[count:, cols:]
        band_im = q[:count, cols:] + q[count:, :cols]
        top = parts_of(jnp.concatenate([band_re, band_im], 1))
        bottom = parts_of(jnp.concatenate([band_im, -band_re], 1))
        for place, part in ((0, 0), (128, 1), (256, 0)):
            r[k, place : place + count, :] = top[part]
            r[k, place + count : place + 2 * count, :] = bottom[part]
    total[...] = jnp.zeros(total.shape, f32)

    @pl.loop(0, kernels)
    def _(k):
        field = mm(u[...], r[k])
        fields_ref[k] = field
        square = field * field
        total[...] += square[:, :cols] + square[:, cols:]

    value = dose[0]
    resist = jax.nn.sigmoid(resist_slope * (value * total[...] - resist_level))
    image_ref[...] = resist.astype(bf16)
    slope_ref[...] = resist * (1.0 - resist) * (2.0 * resist_slope * value)


def middle_kernel(index, node_weights, chaos, start, images, target, pressure_ref, rows_ref, sem, table):
    nodes, share, cols = images.shape
    terms = len(degrees)
    at = pl.multiple_of(start[0], share)
    copy = pltpu.make_async_copy(target.at[:, pl.ds(at, share), :], rows_ref, sem)
    copy.start()
    for n in range(nodes):
        poly = []
        for axis in range(2):
            c = index[n, axis].astype(f32) * (2.0 / (LEVELS - 1)) - 1.0
            s = c * c
            poly.append([None, c, 1.5 * s - 0.5, (2.5 * s - 1.5) * c, (4.375 * s - 3.75) * s + 0.375])
        weight = node_weights[n]
        for j, (p, q) in enumerate(degrees):
            value = weight
            if p:
                value = value * poly[0][p]
            if q:
                value = value * poly[1][q]
            table[n, j] = value
    copy.wait()
    slab = 16
    for first in range(0, share, slab):
        image = [images[n, first : first + slab, :].astype(f32) for n in range(nodes)]
        pressure = [None] * nodes
        for j in range(terms):
            coefficient = table[0, j] * image[0]
            for n in range(1, nodes):
                coefficient = coefficient + table[n, j] * image[n]
            wanted = rows_ref[j, first : first + slab, :].astype(f32)
            mixed = chaos[j] * jnp.tanh(coefficient - wanted)
            for n in range(nodes):
                term = table[n, j] * mixed
                pressure[n] = term if j == 0 else pressure[n] + term
        for n in range(nodes):
            pressure_ref[n, first : first + slab, :] = pressure[n]


def backward_kernel(pressure, slope, fields, fh, fl, gr, gi, wave_hi, wave_lo, own_ref, beyond_ref, dh, dl, scale):
    kernels, count, span = gr.shape
    rows, cols = slope.shape
    scale[...] = slope[...] * pressure[...]

    @pl.loop(0, kernels)
    def _(k):
        factor = scale[...]
        high, low = parts_of(fields[k] * jnp.concatenate([factor, factor], 1))
        prod = mm(fh[...], high) + mm(fh[...], low) + mm(fl[...], high)
        at = pl.multiple_of(2 * k * count, 2 * count)
        dh[pl.ds(at, count), :], dl[pl.ds(at, count), :] = parts_of(prod[:count, :cols] - prod[count:, cols:])
        at = pl.multiple_of(at + count, count)
        dh[pl.ds(at, count), :], dl[pl.ds(at, count), :] = parts_of(prod[:count, cols:] + prod[count:, :cols])

    near = (wave_hi[0:cols, :], wave_lo[0:cols, :])
    a_re = jnp.zeros((count, span), f32)
    a_im = jnp.zeros((count, span), f32)
    for k in range(kernels):
        at = pl.ds(2 * k * count, 2 * count)
        q = mm3((dh[at, :], dl[at, :]), near)
        b_re = q[:count, :span] + q[count:, span:]
        b_im = q[count:, :span] - q[:count, span:]
        a_re = a_re + gr[k] * b_re + gi[k] * b_im
        a_im = a_im + gr[k] * b_im - gi[k] * b_re
    wave = (wave_hi[...], wave_lo[...])
    prod = mm3(parts_of(jnp.concatenate([a_re, a_im], 0)), wave)
    d_re = prod[:count, :span] - prod[count:, span:]
    d_im = prod[:count, span:] + prod[count:, :span]
    own_ref[...] = jnp.concatenate([d_re[:, :cols], d_im[:, :cols]], 0)
    beyond_ref[...] = jnp.concatenate([d_re[:, cols:], d_im[:, cols:]], 0)


def rows_kernel(radius, own, before, after, u, out_ref):
    count, cols = own.shape
    rows = u.shape[0]
    lane = lax.broadcasted_iota(jnp.int32, (count, cols), 1)
    whole = own[...] + jnp.where(lane < radius, before[...], jnp.where(lane >= cols - radius, after[...], 0.0))
    high, low = parts_of(whole)
    high, low = (jnp.concatenate([v, jnp.zeros((128 - count, cols), bf16)], 0) for v in (high, low))
    out_ref[...] = mm(u[...], jnp.concatenate([high, low, high], 0)) * (1.0 / math.sqrt(rows))


def shape_of(*shape, dtype=f32):
    return jax.ShapeDtypeStruct(shape, dtype)


def call(kernel, spaces, outs, scratch=()):
    return pl.pallas_call(
        kernel,
        in_specs=spaces,
        out_specs=[vmem] * len(outs),
        out_shape=list(outs),
        scratch_shapes=list(scratch),
        compiler_params=params,
    )


def local(mask, taps, weights, node_weights, node_index, freq, chaos, target):
    rows, cols = mask.shape
    kernels, count, tap_count = taps.shape[1], taps.shape[3], taps.shape[4]
    radius = (tap_count - 1) // 2
    span = 2 * cols
    nodes, tiles = lax.axis_size("node"), lax.axis_size("tile")
    node = lax.axis_index("node")
    share = rows // nodes
    up = [(i, i + 1) for i in range(tiles - 1)]
    down = [(i + 1, i) for i in range(tiles - 1)]
    wave_hi, wave_lo = (jnp.asarray(w) for w in column_waves(span))
    before = lax.ppermute(mask, "tile", up)
    after = lax.ppermute(mask, "tile", down)
    dose = 1.0 + 0.1 * (node_index[node, 1:2].astype(f32) * (2.0 / (LEVELS - 1)) - 1.0)
    u, fh, fl, gr, gi = call(
        tables_kernel,
        [smem] + [vmem] * 4,
        [
            shape_of(rows, 384, dtype=bf16),
            shape_of(2 * count, rows, dtype=bf16),
            shape_of(2 * count, rows, dtype=bf16),
            shape_of(kernels, count, span),
            shape_of(kernels, count, span),
        ],
    )(freq, taps, weights, wave_hi, wave_lo)
    image, slope, fields = call(
        functools.partial(forward_kernel, radius),
        [smem] + [vmem] * 10,
        [shape_of(rows, cols, dtype=bf16), shape_of(rows, cols), shape_of(kernels, rows, 2 * cols)],
        [
            pltpu.VMEM((2 * kernels * count, span), bf16),
            pltpu.VMEM((2 * kernels * count, span), bf16),
            pltpu.VMEM((kernels, 384, 2 * cols), bf16),
            pltpu.VMEM((rows, cols), f32),
        ],
    )(dose, mask, before, after, fh, fl, gr, gi, u, wave_hi, wave_lo)
    images = lax.all_to_all(image.reshape(nodes, share, cols), "node", 0, 0)
    (pressure,) = call(
        middle_kernel,
        [smem, smem, smem, smem, vmem, pl.BlockSpec(memory_space=pl.ANY)],
        [shape_of(nodes, share, cols)],
        [
            pltpu.VMEM((target.shape[0], share, cols), bf16),
            pltpu.SemaphoreType.DMA,
            pltpu.SMEM((nodes, len(degrees)), f32),
        ],
    )(node_index, node_weights, chaos, (node * share).reshape(1), images, target)
    pressure = lax.all_to_all(pressure, "node", 0, 0).reshape(rows, cols)
    own, beyond = call(
        backward_kernel,
        [vmem] * 9,
        [shape_of(2 * count, cols), shape_of(2 * count, cols)],
        [
            pltpu.VMEM((2 * kernels * count, cols), bf16),
            pltpu.VMEM((2 * kernels * count, cols), bf16),
            pltpu.VMEM((rows, cols), f32),
        ],
    )(pressure, slope, fields, fh, fl, gr, gi, wave_hi, wave_lo)
    from_left = lax.ppermute(beyond, "tile", up)
    from_right = lax.ppermute(beyond, "tile", down)
    (spread,) = call(functools.partial(rows_kernel, radius), [vmem] * 4, [shape_of(rows, cols)])(
        own, from_left, from_right, u
    )
    return lax.all_to_all(spread.reshape(nodes, share, cols), "node", 0, 0).sum(0)


def solution(mesh):
    placed = (
        P(None, "tile"),
        P("node", None, None, None, None),
        P("node", None),
        P(),
        P(),
        P(),
        P(),
        P(None, None, "tile"),
    )
    return jax.shard_map(local, mesh=mesh, in_specs=placed, out_specs=P("node", "tile"), check_vma=False)
```

time: 448 us -> 111 us (0.25); the launches traced: 441 us -> 111 us
  waiting for transfers between devices: 266 us -> 18.2 us
  local copies, waits for them, and re-layouts: 75.8 us -> 15.7 us
  matrix products: 33.8 us -> 0 us
  other arithmetic: 25 us -> 1.89 us
  blocking collectives: 0 us -> 22.5 us
  Pallas kernels: 0 us -> 15 us
  between operations: 14.5 us -> 0.81 us
  starting transfers between devices: 26.2 us -> 36.4 us
    reduce_scatter x2 -> x0, waiting for transfers between devices: 145 us -> none  [the longest x1 80.7 us: local(): lax.psum_scatter((scaled[:, None, None] * rounded.astype(jnp.float32)[Non...]
    all_gather x1 -> x0, waiting for transfers between devices: 111 us -> none  [local(): lax.all_gather(chaos_weights[:, None, None] * jnp.tanh(coefficient - targ...]
    another operation x68 -> x0, local copies, waits for them, and re-layouts: 56.4 us -> none  [the longest x66 56.3 us: image_forward(): jnp.stack([spectrum[:, offset:offset + col_count] for offset in range(tap...]
    dot_general x8 -> x0, matrix products: 33.8 us -> none  [the longest x1 6.7 us: image_backward(): dband = jnp.einsum('yf,kyx->kfx', inverse, dfields, precision=highest)]
    all_to_all x0 -> x2, blocking collectives: none -> 22.5 us  [the longest x1 11.4 us: local(): pressure = lax.all_to_all(pressure, 'node', 0, 0).reshape(rows, cols)]
    all_to_all x0 -> x1, starting transfers between devices: none -> 18.6 us  [local(): images = lax.all_to_all(image.reshape(nodes, share, cols), 'node', 0, 0)]
    pallas_call x0 -> x5, Pallas kernels: none -> 15 us  [the longest x1 5.68 us: local(): call(functools.partial(forward_kernel, radius), [smem] + [vmem] * 10, [sh...]
    add x4 -> x0, other arithmetic: 14.7 us -> none  [the longest x1 6.78 us: image_backward(): total + jnp.pad(spread[:, :, offset], ((0, 0), (0, 0), (offset, 2 * radiu...]
  transfers between devices with their start and end apart: 7 -> 5, of which waited for: 5 -> 3; matrix products, arithmetic and copies ran while one was open for 2% -> 2% of each run, Pallas kernels for 0% -> 2%
where the time goes in v1:
time: 111 us
  starting transfers between devices  36.4 us (33%)
  blocking collectives  22.5 us (20%)
  waiting for transfers between devices  18.2 us (16%)
  local copies, waits for them, and re-layouts  15.7 us (14%)
  Pallas kernels  15 us (14%)
  other arithmetic  1.89 us (2%)
    all_to_all x1, starting transfers between devices, local(): images = lax.all_to_all(image.reshape(nodes, share, cols), 'node', 0, 0)  18.6 us
    unnamed x49, local copies, waits for them, and re-layouts  15.7 us
    all_to_all x1, blocking collectives, local(): pressure = lax.all_to_all(pressure, 'node', 0, 0).reshape(rows, cols)  11.4 us
    all_to_all x1, blocking collectives, local(): lax.all_to_all(spread.reshape(nodes, share, cols), 'node', 0, 0).sum(0)  11.1 us
    ppermute x1, starting transfers between devices, local(): from_left = lax.ppermute(beyond, 'tile', up)  7.92 us
    ppermute x1, waiting for transfers between devices, local(): from_right = lax.ppermute(beyond, 'tile', down)  7.73 us
    all_to_all x1, waiting for transfers between devices, local(): images = lax.all_to_all(image.reshape(nodes, share, cols), 'node', 0, 0)  7.18 us
    ppermute x1, starting transfers between devices, local(): before = lax.ppermute(mask, 'tile', up)  6.01 us
  transfers between devices with their start and end apart: 5, of which 3 were waited for; matrix products, arithmetic and copies ran while one was open for 2% of the time, Pallas kernels for 2%

profile of v1, /device:TPU:47, one launch (start us, length us, event | category | flops | bytes accessed | tf_op | source)
XLA Modules:
  0.0 110.5 jit_solution(3969420934629624912)
XLA Ops:
  0.0 6.0 %collective-permute-start = (f32[512,128]{1,0:T(8,128)}, f32[512,128]{1,0:T(8,128)S(1)}, u32[]{:S(2)}, u32[]{:S(2)}) collective-permute-start(f32[512,128]{1,0:T(8,128)} %mask.1), channel_id=1, source_target_pairs={{0,16},{16,32},{32,48},{48,64},{64,80},{80,96},{96,112},{112,128},... | collective-permute-start | bytes 786440 | tf_op jit(solution)/shard_map/ppermute | solution.py:250
  6.0 1.9 %collective-permute-start.1 = (f32[512,128]{1,0:T(8,128)}, f32[512,128]{1,0:T(8,128)S(1)}, u32[]{:S(2)}, u32[]{:S(2)}) collective-permute-start(f32[512,128]{1,0:T(8,128)} %mask.1), channel_id=1, source_target_pairs={{16,0},{32,16},{48,32},{64,48},{80,64},{96,80},{112,96},{128,112},... | collective-permute-start | bytes 786440 | tf_op jit(solution)/shard_map/ppermute | solution.py:251
  8.0 1.3 %fusion = f32[1,1]{0,1:T(1,128)} fusion(s32[16,2]{0,1:T(2,128)} %param.14, s32[]{:T(128)S(6)} %select_n.3), kind=kLoop, calls=%fused_computation.1 | loop fusion | flops 1 | bytes 12 | tf_op jit(solution)/shard_map/convert_element_type | solution.py:252
  9.9 0.9 copy-done
  10.8 0.9 copy-done.3
  11.8 1.0 copy-done.11
  14.1 2.0 %shard_map.100 = (bf16[512,384]{1,0:T(8,128)(2,1)S(1)}, bf16[96,512]{1,0:T(8,128)(2,1)S(1)}, bf16[96,512]{1,0:T(8,128)(2,1)S(1)}, f32[8,48,256]{2,1,0:T(8,128)S(1)}, f32[8,48,256]{2,1,0:T(8,128)S(1)}) custom-call(s32[48]{0:T(128)S(1)} %copy-done.20, f32[1,8,2,48,65]{4,3,2,1,0:T(8,128)S(1)} %copy-done.11, f32[1,8]{1,0:T(1,128)S(1)} %copy-done.21, ...), custom_call_target="tpu_custom_call" | custom-call | tf_op jit(solution)/shard_map/pallas_call | solution.py:253
  16.9 3.3 %collective-permute-done.1.after = f32[512,128]{1,0:T(8,128)S(1)} collective-permute-done((f32[512,128]{1,0:T(8,128)}, f32[512,128]{1,0:T(8,128)S(1)}, u32[]{:S(2)}, u32[]{:S(2)}) %collective-permute-start.1) | collective-permute-done | bytes 262176 | tf_op jit(solution)/shard_map/ppermute | solution.py:251
  20.9 0.9 copy-done.1
  21.8 0.9 copy-done.4
  22.8 0.9 copy-done.12
  23.7 0.9 copy-done.14
  24.7 0.9 copy-done.16
  25.6 5.7 %shard_map.101 = (bf16[512,128]{1,0:T(8,128)(2,1)S(1)}, f32[512,128]{1,0:T(8,128)S(1)}, f32[8,512,256]{2,1,0:T(8,128)}) custom-call(f32[1]{0:T(128)} %bitcast.1.dose, f32[512,128]{1,0:T(8,128)S(1)} %copy-done.12, f32[512,128]{1,0:T(8,128)S(1)} %copy-done.14, f32[512,128]{1,0:T(8,128)S(1)} %copy-done.16, bf16[96,512]{1,0:T(8,128)(2,1)S(1)} %get-tuple-element.15.fh, ...), custom_call_target="tpu_custom_call" | custom-call | tf_op jit(solution)/shard_map/pallas_call | solution.py:264
  32.7 18.6 %all-to-all-start = ((bf16[16,32,128]{2,1,0:T(8,128)(2,1)}), bf16[16,32,128]{2,1,0:T(8,128)(2,1)S(1)}, u32[]{:S(2)}, u32[]{:S(2)}) async-start(bf16[16,32,128]{2,1,0:T(8,128)(2,1)} %bitcast.7), calls=%async_computation | async-start | bytes 262144 | tf_op jit(solution)/shard_map/all_to_all | solution.py:275
  52.1 7.2 %all-to-all-done.images = bf16[16,32,128]{2,1,0:T(8,128)(2,1)S(1)} async-done(((bf16[16,32,128]{2,1,0:T(8,128)(2,1)}), bf16[16,32,128]{2,1,0:T(8,128)(2,1)S(1)}, u32[]{:S(2)}, u32[]{:S(2)}) %all-to-all-start) | async-done | bytes 131104 | tf_op jit(solution)/shard_map/all_to_all | solution.py:275
  60.5 1.5 %shard_map.102 = f32[16,32,128]{2,1,0:T(8,128)S(1)} custom-call(s32[16,2]{1,0:T(8,128)S(1)} %copy.11.index, f32[16]{0:T(128)S(1)} %copy-done.22, f32[15]{0:T(128)S(1)} %copy-done.23, s32[1]{0:T(128)} %bitcast.start, bf16[16,32,128]{2,1,0:T(8,128)(2,1)S(1)} %all-to-all-done.images, bf16[15,512,128]{2,1,0:T(8,128)(2,1)S(1)} %copy-done.6), custom_call_target="tpu_custom_call" | custom-call | tf_op jit(solution)/shard_map/pallas_call | solution.py:276
  62.1 11.4 %all_to_all.15 = f32[16,32,128]{2,1,0:T(8,128)S(1)} all-to-all(f32[16,32,128]{2,1,0:T(8,128)S(1)} %shard_map.102), channel_id=1, replica_groups=mesh['tile'=64,'node'=16] {'node'}, dimensions={0} | all-to-all | bytes 524288 | tf_op jit(solution)/shard_map/all_to_all | solution.py:286
  74.4 0.9 copy-done.18
  75.3 5.6 %shard_map.103 = (f32[96,128]{1,0:T(8,128)S(1)}, f32[96,128]{1,0:T(8,128)S(1)}) custom-call(f32[512,128]{1,0:T(8,128)S(1)} %bitcast.5, f32[512,128]{1,0:T(8,128)S(1)} %copy-done.18, f32[8,512,256]{2,1,0:T(8,128)} %get-tuple-element.22.fields, bf16[96,512]{1,0:T(8,128)(2,1)S(1)} %get-tuple-element.15.fh, bf16[96,512]{1,0:T(8,128)(2,1)S(1)} %copy-done.10, ...), custom_call_target="tpu_custom_call" | custom-call | tf_op jit(solution)/shard_map/pallas_call | solution.py:287
  80.9 7.9 %collective-permute-start.2 = (f32[96,128]{1,0:T(8,128)S(1)}, f32[96,128]{1,0:T(8,128)S(1)}, u32[]{:S(2)}, u32[]{:S(2)}) collective-permute-start(f32[96,128]{1,0:T(8,128)S(1)} %get-tuple-element.24), channel_id=1, source_target_pairs={{0,16},{16,32},{32,48},{48,64},{64,80},{80,96},{96,112},{112,128},... | collective-permute-start | bytes 147464 | tf_op jit(solution)/shard_map/ppermute | solution.py:297
  88.8 1.9 %collective-permute-start.3 = (f32[96,128]{1,0:T(8,128)S(1)}, f32[96,128]{1,0:T(8,128)S(1)}, u32[]{:S(2)}, u32[]{:S(2)}) collective-permute-start(f32[96,128]{1,0:T(8,128)S(1)} %get-tuple-element.24), channel_id=1, source_target_pairs={{16,0},{32,16},{48,32},{64,48},{80,64},{96,80},{112,96},{128,112},... | collective-permute-start | bytes 147464 | tf_op jit(solution)/shard_map/ppermute | solution.py:298
  90.8 7.7 %collective-permute-done.3.after = f32[96,128]{1,0:T(8,128)S(1)} collective-permute-done((f32[96,128]{1,0:T(8,128)S(1)}, f32[96,128]{1,0:T(8,128)S(1)}, u32[]{:S(2)}, u32[]{:S(2)}) %collective-permute-start.3) | collective-permute-done | bytes 49184 | tf_op jit(solution)/shard_map/ppermute | solution.py:298
  98.8 11.1 %all_to_all.16 = f32[16,32,128]{2,1,0:T(8,128)S(1)} all-to-all(f32[16,32,128]{2,1,0:T(8,128)S(1)} %bitcast.6), channel_id=1, replica_groups=mesh['tile'=64,'node'=16] {'node'}, dimensions={0} | all-to-all | bytes 524288 | tf_op jit(solution)/shard_map/all_to_all | solution.py:302
  (44 shorter events, 8.0 us)
Async XLA Ops:
  0.0 16.1 %collective-permute-start = (f32[512,128]{1,0:T(8,128)}, f32[512,128]{1,0:T(8,128)S(1)}, u32[]{:S(2)}, u32[]{:S(2)}) collective-permute-start(f32[512,128]{1,0:T(8,128)} %mask.1), channel_id=1, source_target_pairs={{0,16},{16,32},{32,48},{48,64},{64,80},{80,96},{96,112},{112,128},... | collective-permute-start | bytes 786440 | tf_op jit(solution)/shard_map/ppermute | solution.py:250
  6.0 14.1 %collective-permute-start.1 = (f32[512,128]{1,0:T(8,128)}, f32[512,128]{1,0:T(8,128)S(1)}, u32[]{:S(2)}, u32[]{:S(2)}) collective-permute-start(f32[512,128]{1,0:T(8,128)} %mask.1), channel_id=1, source_target_pairs={{16,0},{32,16},{48,32},{64,48},{80,64},{96,80},{112,96},{128,112},... | collective-permute-start | bytes 786440 | tf_op jit(solution)/shard_map/ppermute | solution.py:251
  9.9 1.0 copy-start
  10.8 0.9 copy-start.3
  11.8 1.0 copy-start.11
  14.1 59.4 %copy-start.2 = (bf16[256,512]{1,0:T(8,128)(2,1)S(1)}, bf16[256,512]{1,0:T(8,128)(2,1)}, u32[]{:S(2)}) copy-start(bf16[256,512]{1,0:T(8,128)(2,1)} %constant.29.clone.wave_hi) | copy-start | bytes 786436
  14.1 59.4 %copy-start.5 = (bf16[256,512]{1,0:T(8,128)(2,1)S(1)}, bf16[256,512]{1,0:T(8,128)(2,1)}, u32[]{:S(2)}) copy-start(bf16[256,512]{1,0:T(8,128)(2,1)} %constant.30.clone.wave_lo) | copy-start | bytes 786436
  16.1 15.2 %copy-start.7 = (bf16[512,384]{1,0:T(8,128)(2,1)}, bf16[512,384]{1,0:T(8,128)(2,1)S(1)}, u32[]{:S(2)}) copy-start(bf16[512,384]{1,0:T(8,128)(2,1)S(1)} %get-tuple-element.19.u) | copy-start | bytes 1179652
  16.1 16.6 %copy-start.9 = (bf16[96,512]{1,0:T(8,128)(2,1)}, bf16[96,512]{1,0:T(8,128)(2,1)S(1)}, u32[]{:S(2)}) copy-start(bf16[96,512]{1,0:T(8,128)(2,1)S(1)} %get-tuple-element.16.fl) | copy-start | bytes 294916
  16.1 0.8 copy-start.13
  20.2 0.7 copy-start.15
  20.9 0.9 copy-start.1
  21.8 0.9 copy-start.4
  22.8 0.9 copy-start.12
  23.7 0.9 copy-start.14
  24.7 0.9 copy-start.16
  25.6 33.6 %copy-start.6 = (bf16[15,512,128]{2,1,0:T(8,128)(2,1)S(1)}, bf16[15,512,128]{2,1,0:T(8,128)(2,1)}, u32[]{:S(2)}) copy-start(bf16[15,512,128]{2,1,0:T(8,128)(2,1)} %target.1) | copy-start | bytes 5898244
  31.3 0.7 copy-start.17
  32.7 26.5 %all-to-all-start = ((bf16[16,32,128]{2,1,0:T(8,128)(2,1)}), bf16[16,32,128]{2,1,0:T(8,128)(2,1)S(1)}, u32[]{:S(2)}, u32[]{:S(2)}) async-start(bf16[16,32,128]{2,1,0:T(8,128)(2,1)} %bitcast.7), calls=%async_computation | async-start | bytes 262144 | tf_op jit(solution)/shard_map/all_to_all | solution.py:275
  60.5 37.9 %copy-start.8 = (bf16[512,384]{1,0:T(8,128)(2,1)S(1)}, bf16[512,384]{1,0:T(8,128)(2,1)}, u32[]{:S(2)}) copy-start(bf16[512,384]{1,0:T(8,128)(2,1)} %copy-done.7) | copy-start | bytes 1179652
  73.5 0.9 copy-start.10
  74.4 0.9 copy-start.18
  80.9 9.9 %collective-permute-start.2 = (f32[96,128]{1,0:T(8,128)S(1)}, f32[96,128]{1,0:T(8,128)S(1)}, u32[]{:S(2)}, u32[]{:S(2)}) collective-permute-start(f32[96,128]{1,0:T(8,128)S(1)} %get-tuple-element.24), channel_id=1, source_target_pairs={{0,16},{16,32},{32,48},{48,64},{64,80},{80,96},{96,112},{112,128},... | collective-permute-start | bytes 147464 | tf_op jit(solution)/shard_map/ppermute | solution.py:297
  88.8 9.7 %collective-permute-start.3 = (f32[96,128]{1,0:T(8,128)S(1)}, f32[96,128]{1,0:T(8,128)S(1)}, u32[]{:S(2)}, u32[]{:S(2)}) collective-permute-start(f32[96,128]{1,0:T(8,128)S(1)} %get-tuple-element.24), channel_id=1, source_target_pairs={{16,0},{32,16},{48,32},{64,48},{80,64},{96,80},{112,96},{128,112},... | collective-permute-start | bytes 147464 | tf_op jit(solution)/shard_map/ppermute | solution.py:298
  (5 other events, 3.3 us)

commit v2 on v1

--- a/solution.py
+++ b/solution.py
@@ -17,7 +17,7 @@
 f32, bf16 = jnp.float32, jnp.bfloat16
 vmem = pl.BlockSpec(memory_space=pltpu.VMEM)
 smem = pl.BlockSpec(memory_space=pltpu.SMEM)
-params = pltpu.CompilerParams(vmem_limit_bytes=48 << 20)
+hbm = pl.BlockSpec(memory_space=pltpu.HBM)
 
 
 def parts_of(value):
@@ -54,12 +54,36 @@
     return high, low
 
 
-def tables_kernel(freq, taps, weights, wave_hi, wave_lo, u_ref, fh_ref, fl_ref, gr_ref, gi_ref):
-    rows = u_ref.shape[0]
+def tables_kernel(
+    start, freq_in, index_in, node_weights_in, chaos_in, weights_in, taps_in, wave_hi_in, wave_lo_in, mask_in, target_in,
+    u_ref, fh_ref, fl_ref, gr_ref, gi_ref, wave_hi, wave_lo, spectrum_ref, wanted_ref, scalars_ref,
+    freq, index, node_weights, chaos, weights, taps, mask, sems,
+):
+    rows, cols = mask.shape
     count = freq.shape[0]
     kernels, tap_count = taps.shape[1], taps.shape[4]
     span = wave_hi.shape[0]
     radius = (tap_count - 1) // 2
+    nodes, share = index.shape[1], wanted_ref.shape[1]
+    own = start[0]
+    at = pl.multiple_of(own * share, share)
+    moves = [
+        (freq_in, freq),
+        (index_in, index),
+        (node_weights_in, node_weights),
+        (chaos_in, chaos),
+        (weights_in, weights),
+        (mask_in, mask),
+        (wave_hi_in, wave_hi),
+        (wave_lo_in, wave_lo),
+        (taps_in, taps),
+        (target_in.at[:, pl.ds(at, share), :], wanted_ref),
+    ]
+    copies = [pltpu.make_async_copy(source, goal, sems.at[i]) for i, (source, goal) in enumerate(moves)]
+    for copy in copies:
+        copy.start()
+    for copy in copies[:4]:
+        copy.wait()
     f_row = lax.broadcasted_iota(jnp.int32, (2 * count, rows), 0)
     f_freq = jnp.zeros((2 * count, 128), jnp.int32)
     line = lax.broadcasted_iota(jnp.int32, (2 * count, 128), 0)
@@ -73,7 +97,8 @@
     f_full = jnp.concatenate([f_freq] * (rows // 128), 1)
     quarter = rows // 4
     f_table = cosine(f_full * y_lane + jnp.where(f_row >= count, quarter, 0), rows)
-    fh_ref[...], fl_ref[...] = parts_of(f_table)
+    f_parts = parts_of(f_table)
+    fh_ref[...], fl_ref[...] = f_parts
     u_full = jnp.concatenate([u_freq] * (rows // 8), 0)
     u_lane = lax.broadcasted_iota(jnp.int32, (rows, 128), 1)
     u_y = lax.broadcasted_iota(jnp.int32, (rows, 128), 0)
@@ -83,6 +108,29 @@
     u_ref[:, 0:128] = high
     u_ref[:, 128:256] = high
     u_ref[:, 256:384] = low
+    for n in range(nodes):
+        poly = []
+        for axis in range(2):
+            c = index[axis, n].astype(f32) * (2.0 / (LEVELS - 1)) - 1.0
+            s = c * c
+            poly.append([None, c, 1.5 * s - 0.5, (2.5 * s - 1.5) * c, (4.375 * s - 3.75) * s + 0.375])
+        weight = node_weights[n]
+        for j, (p, q) in enumerate(degrees):
+            value = weight
+            if p:
+                value = value * poly[0][p]
+            if q:
+                value = value * poly[1][q]
+            scalars_ref[16 * n + j : 16 * n + j + 1, :] = jnp.full((1, 128), value, f32)
+    dose = 1.0 + 0.1 * (index[1, own].astype(f32) * (2.0 / (LEVELS - 1)) - 1.0)
+    scalars_ref[15:16, :] = jnp.full((1, 128), dose, f32)
+    for j in range(len(degrees)):
+        scalars_ref[16 * nodes + j : 16 * nodes + j + 1, :] = jnp.full((1, 128), chaos[j], f32)
+    for copy in copies[4:6]:
+        copy.wait()
+    spectrum_ref[...] = mm3(f_parts, parts_of(mask[...])) * (1.0 / math.sqrt(rows))
+    for copy in copies[6:9]:
+        copy.wait()
     side = [jnp.concatenate([w[span - radius : span], w[0 : tap_count - radius]], 0) for w in (wave_hi, wave_lo)]
     scale = jnp.sqrt(weights[...]) * (1.0 / (span * math.sqrt(count)))
     for k in range(kernels):
@@ -91,20 +139,20 @@
         amount = scale[0:1, k : k + 1]
         gr_ref[k] = (prod[:count, :span] - prod[count:, span:]) * amount
         gi_ref[k] = (prod[:count, span:] + prod[count:, :span]) * amount
+    copies[9].wait()
 
 
 def forward_kernel(
-    radius, dose, mask, before, after, fh, fl, gr, gi, u, wave_hi, wave_lo,
+    radius, scalars, spectrum, before, after, fh, fl, gr, gi, u, wave_hi, wave_lo,
     image_ref, slope_ref, fields_ref, bh, bl, r, total,
 ):
-    rows, cols = mask.shape
+    rows, cols = before.shape
     kernels, count, span = gr.shape
     lane = lax.broadcasted_iota(jnp.int32, (rows, cols), 1)
     beyond = jnp.where(lane < radius, after[...], jnp.where(lane >= cols - radius, before[...], 0.0))
-    padded = jnp.concatenate([mask[...], beyond], 1)
-    spectrum = mm3((fh[...], fl[...]), parts_of(padded)) * (1.0 / math.sqrt(rows))
+    outer = mm3((fh[...], fl[...]), parts_of(beyond)) * (1.0 / math.sqrt(rows))
     wave = (wave_hi[...], wave_lo[...])
-    prod = mm3(parts_of(spectrum), wave)
+    prod = mm3(parts_of(jnp.concatenate([spectrum[...], outer], 1)), wave)
     a_re = prod[:count, :span] + prod[count:, span:]
     a_im = prod[count:, :span] - prod[:count, span:]
     for k in range(kernels):
@@ -134,45 +182,27 @@
         square = field * field
         total[...] += square[:, :cols] + square[:, cols:]
 
-    value = dose[0]
+    value = scalars[15:16, :]
     resist = jax.nn.sigmoid(resist_slope * (value * total[...] - resist_level))
     image_ref[...] = resist.astype(bf16)
     slope_ref[...] = resist * (1.0 - resist) * (2.0 * resist_slope * value)
 
 
-def middle_kernel(index, node_weights, chaos, start, images, target, pressure_ref, rows_ref, sem, table):
+def middle_kernel(images, wanted, scalars, pressure_ref):
     nodes, share, cols = images.shape
-    terms = len(degrees)
-    at = pl.multiple_of(start[0], share)
-    copy = pltpu.make_async_copy(target.at[:, pl.ds(at, share), :], rows_ref, sem)
-    copy.start()
-    for n in range(nodes):
-        poly = []
-        for axis in range(2):
-            c = index[n, axis].astype(f32) * (2.0 / (LEVELS - 1)) - 1.0
-            s = c * c
-            poly.append([None, c, 1.5 * s - 0.5, (2.5 * s - 1.5) * c, (4.375 * s - 3.75) * s + 0.375])
-        weight = node_weights[n]
-        for j, (p, q) in enumerate(degrees):
-            value = weight
-            if p:
-                value = value * poly[0][p]
-            if q:
-                value = value * poly[1][q]
-            table[n, j] = value
-    copy.wait()
     slab = 16
     for first in range(0, share, slab):
         image = [images[n, first : first + slab, :].astype(f32) for n in range(nodes)]
         pressure = [None] * nodes
-        for j in range(terms):
-            coefficient = table[0, j] * image[0]
+        for j in range(len(degrees)):
+            weight = [scalars[16 * n + j : 16 * n + j + 1, :] for n in range(nodes)]
+            coefficient = weight[0] * image[0]
             for n in range(1, nodes):
-                coefficient = coefficient + table[n, j] * image[n]
-            wanted = rows_ref[j, first : first + slab, :].astype(f32)
-            mixed = chaos[j] * jnp.tanh(coefficient - wanted)
+                coefficient = coefficient + weight[n] * image[n]
+            goal = wanted[j, first : first + slab, :].astype(f32)
+            mixed = scalars[16 * nodes + j : 16 * nodes + j + 1, :] * jnp.tanh(coefficient - goal)
             for n in range(nodes):
-                term = table[n, j] * mixed
+                term = weight[n] * mixed
                 pressure[n] = term if j == 0 else pressure[n] + term
         for n in range(nodes):
             pressure_ref[n, first : first + slab, :] = pressure[n]
@@ -225,14 +255,14 @@
     return jax.ShapeDtypeStruct(shape, dtype)
 
 
-def call(kernel, spaces, outs, scratch=()):
+def call(kernel, mebibytes, spaces, outs, scratch=()):
     return pl.pallas_call(
         kernel,
         in_specs=spaces,
         out_specs=[vmem] * len(outs),
         out_shape=list(outs),
         scratch_shapes=list(scratch),
-        compiler_params=params,
+        compiler_params=pltpu.CompilerParams(vmem_limit_bytes=mebibytes << 20),
     )
 
 
@@ -249,21 +279,43 @@
     wave_hi, wave_lo = (jnp.asarray(w) for w in column_waves(span))
     before = lax.ppermute(mask, "tile", up)
     after = lax.ppermute(mask, "tile", down)
-    dose = 1.0 + 0.1 * (node_index[node, 1:2].astype(f32) * (2.0 / (LEVELS - 1)) - 1.0)
-    u, fh, fl, gr, gi = call(
+    u, fh, fl, gr, gi, wave_hi, wave_lo, spectrum, wanted, scalars = call(
         tables_kernel,
-        [smem] + [vmem] * 4,
+        16,
+        [smem] + [hbm] * 10,
         [
             shape_of(rows, 384, dtype=bf16),
             shape_of(2 * count, rows, dtype=bf16),
             shape_of(2 * count, rows, dtype=bf16),
             shape_of(kernels, count, span),
             shape_of(kernels, count, span),
+            shape_of(span, 2 * span, dtype=bf16),
+            shape_of(span, 2 * span, dtype=bf16),
+            shape_of(2 * count, cols),
+            shape_of(target.shape[0], share, cols, dtype=bf16),
+            shape_of(16 * nodes + 16, 128),
         ],
-    )(freq, taps, weights, wave_hi, wave_lo)
+        [
+            pltpu.SMEM(freq.shape, jnp.int32),
+            pltpu.SMEM((2, nodes), jnp.int32),
+            pltpu.SMEM((nodes,), f32),
+            pltpu.SMEM(chaos.shape, f32),
+            pltpu.VMEM(weights.shape, f32),
+            pltpu.VMEM(taps.shape, f32),
+            pltpu.VMEM(mask.shape, f32),
+            pltpu.SemaphoreType.DMA((10,)),
+        ],
+    )(
+        node.reshape(1),
+        *(
+            pltpu.with_memory_space_constraint(a, pltpu.HBM)
+            for a in (freq, node_index.T, node_weights, chaos, weights, taps, wave_hi, wave_lo, mask, target)
+        ),
+    )
     image, slope, fields = call(
         functools.partial(forward_kernel, radius),
-        [smem] + [vmem] * 10,
+        16,
+        [vmem] * 11,
         [shape_of(rows, cols, dtype=bf16), shape_of(rows, cols), shape_of(kernels, rows, 2 * cols)],
         [
             pltpu.VMEM((2 * kernels * count, span), bf16),
@@ -271,21 +323,13 @@
             pltpu.VMEM((kernels, 384, 2 * cols), bf16),
             pltpu.VMEM((rows, cols), f32),
         ],
-    )(dose, mask, before, after, fh, fl, gr, gi, u, wave_hi, wave_lo)
+    )(scalars, spectrum, before, after, fh, fl, gr, gi, u, wave_hi, wave_lo)
     images = lax.all_to_all(image.reshape(nodes, share, cols), "node", 0, 0)
-    (pressure,) = call(
-        middle_kernel,
-        [smem, smem, smem, smem, vmem, pl.BlockSpec(memory_space=pl.ANY)],
-        [shape_of(nodes, share, cols)],
-        [
-            pltpu.VMEM((target.shape[0], share, cols), bf16),
-            pltpu.SemaphoreType.DMA,
-            pltpu.SMEM((nodes, len(degrees)), f32),
-        ],
-    )(node_index, node_weights, chaos, (node * share).reshape(1), images, target)
+    (pressure,) = call(middle_kernel, 8, [vmem] * 3, [shape_of(nodes, share, cols)])(images, wanted, scalars)
     pressure = lax.all_to_all(pressure, "node", 0, 0).reshape(rows, cols)
     own, beyond = call(
         backward_kernel,
+        16,
         [vmem] * 9,
         [shape_of(2 * count, cols), shape_of(2 * count, cols)],
         [
@@ -296,7 +340,7 @@
     )(pressure, slope, fields, fh, fl, gr, gi, wave_hi, wave_lo)
     from_left = lax.ppermute(beyond, "tile", up)
     from_right = lax.ppermute(beyond, "tile", down)
-    (spread,) = call(functools.partial(rows_kernel, radius), [vmem] * 4, [shape_of(rows, cols)])(
+    (spread,) = call(functools.partial(rows_kernel, radius), 8, [vmem] * 4, [shape_of(rows, cols)])(
         own, from_left, from_right, u
     )
     return lax.all_to_all(spread.reshape(nodes, share, cols), "node", 0, 0).sum(0)

time: 111 us -> 94.8 us (0.85)
  the two profiles are of different devices: /device:TPU:47 before, /device:TPU:112 now
where the time goes in v2:
time: 94.8 us; the launch traced here: 93.9 us
  blocking collectives  56.3 us (59%)
  waiting for transfers between devices  14.4 us (15%)
  starting transfers between devices  11.8 us (12%)
  Pallas kernels  10.7 us (11%)
    all_to_all x1, blocking collectives, local(): images = lax.all_to_all(image.reshape(nodes, share, cols), 'node', 0, 0)  29.7 us
    all_to_all x1, blocking collectives, local(): lax.all_to_all(spread.reshape(nodes, share, cols), 'node', 0, 0).sum(0)  13.4 us
    all_to_all x1, blocking collectives, local(): pressure = lax.all_to_all(pressure, 'node', 0, 0).reshape(rows, cols)  13.2 us
    ppermute x1, waiting for transfers between devices, local(): before = lax.ppermute(mask, 'tile', up)  8.18 us
    ppermute x1, waiting for transfers between devices, local(): from_left = lax.ppermute(beyond, 'tile', up)  6.17 us
    ppermute x1, starting transfers between devices, local(): after = lax.ppermute(mask, 'tile', down)  5.55 us
    pallas_call x1, Pallas kernels, local(): call(functools.partial(forward_kernel, radius), 16, [vmem] * 11, [shape_o...  3.84 us
    pallas_call x1, Pallas kernels, local(): call(backward_kernel, 16, [vmem] * 9, [shape_of(2 * count, cols), shape_o...  3.49 us
  transfers between devices with their start and end apart: 4, of which 2 were waited for; matrix products, arithmetic and copies ran while one was open for 0% of the time, Pallas kernels for 3%

profile of v2, /device:TPU:112, one launch (start us, length us, event | category | flops | bytes accessed | tf_op | source)
XLA Modules:
  0.0 93.9 jit_solution(17089781588939902799)
XLA Ops:
  0.0 5.5 %collective-permute-start.1 = (f32[512,128]{1,0:T(8,128)}, f32[512,128]{1,0:T(8,128)S(1)}, u32[]{:S(2)}, u32[]{:S(2)}) collective-permute-start(f32[512,128]{1,0:T(8,128)} %mask_in.1), channel_id=1, source_target_pairs={{16,0},{32,16},{48,32},{64,48},{80,64},{96,80},{112,96},{128,112},... | collective-permute-start | bytes 786440 | tf_op jit(solution)/shard_map/ppermute | solution.py:281
  5.6 1.9 %collective-permute-start = (f32[512,128]{1,0:T(8,128)}, f32[512,128]{1,0:T(8,128)S(1)}, u32[]{:S(2)}, u32[]{:S(2)}) collective-permute-start(f32[512,128]{1,0:T(8,128)} %mask_in.1), channel_id=1, source_target_pairs={{0,16},{16,32},{32,48},{48,64},{64,80},{80,96},{96,112},{112,128},... | collective-permute-start | bytes 786440 | tf_op jit(solution)/shard_map/ppermute | solution.py:280
  7.5 2.5 %shard_map.100 = (bf16[512,384]{1,0:T(8,128)(2,1)S(1)}, bf16[96,512]{1,0:T(8,128)(2,1)S(1)}, bf16[96,512]{1,0:T(8,128)(2,1)S(1)}, f32[8,48,256]{2,1,0:T(8,128)S(...) custom-call(s32[1]{0:T(128)} %bitcast.start, ...), custom_call_target="tpu_custom_call" | custom-call | tf_op jit(solution)/shard_map/pallas_call | solution.py:282
  10.0 0.0 collective-permute-done.1.after
  10.0 8.2 %collective-permute-done.before = f32[512,128]{1,0:T(8,128)S(1)} collective-permute-done((f32[512,128]{1,0:T(8,128)}, f32[512,128]{1,0:T(8,128)S(1)}, u32[]{:S(2)}, u32[]{:S(2)}) %collective-permute-start) | collective-permute-done | bytes 262176 | tf_op jit(solution)/shard_map/ppermute | solution.py:280
  18.2 3.8 %shard_map.101 = (bf16[512,128]{1,0:T(8,128)(2,1)S(1)}, f32[512,128]{1,0:T(8,128)S(1)}, f32[8,512,256]{2,1,0:T(8,128)S(1)}) custom-call(f32[272,128]{1,0:T(8,128)S(1)} %get-tuple-element.20.scalars, f32[96,128]{1,0:T(8,128)S(1)} %get-tuple-element.21.spectrum, f32[512,128]{1,0:T(8,128)S(1)} %collective-permute-done.before, ...), custom_call_target="tpu_custom_call" | custom-call | tf_op jit(solution)/shard_map/pallas_call | solution.py:315
  22.1 29.7 %all_to_all.15.images = bf16[16,32,128]{2,1,0:T(8,128)(2,1)S(1)} all-to-all(bf16[16,32,128]{2,1,0:T(8,128)(2,1)S(1)} %bitcast.7), channel_id=1, replica_groups=mesh['tile'=64,'node'=16] {'node'}, dimensions={0} | all-to-all | bytes 262144 | tf_op jit(solution)/shard_map/all_to_all | solution.py:327
  51.8 0.6 shard_map.102
  52.4 13.2 %all_to_all.16 = f32[16,32,128]{2,1,0:T(8,128)S(1)} all-to-all(f32[16,32,128]{2,1,0:T(8,128)S(1)} %shard_map.102), channel_id=1, replica_groups=mesh['tile'=64,'node'=16] {'node'}, dimensions={0} | all-to-all | bytes 524288 | tf_op jit(solution)/shard_map/all_to_all | solution.py:329
  65.6 3.5 %shard_map.103 = (f32[96,128]{1,0:T(8,128)S(1)}, f32[96,128]{1,0:T(8,128)S(1)}) custom-call(f32[512,128]{1,0:T(8,128)S(1)} %bitcast.5, f32[512,128]{1,0:T(8,128)S(1)} %get-tuple-element.31.slope, f32[8,512,256]{2,1,0:T(8,128)S(1)} %get-tuple-element.32.fields, bf16[96,512]{1,0:T(8,128)(2,1)S(1)} %get-tuple-element.22.fh, ...), custom_call_target="tpu_custom_call" | custom-call | tf_op jit(solution)/shard_map/pallas_call | solution.py:330
  69.1 1.9 %collective-permute-start.3 = (f32[96,128]{1,0:T(8,128)S(1)}, f32[96,128]{1,0:T(8,128)S(1)}, u32[]{:S(2)}, u32[]{:S(2)}) collective-permute-start(f32[96,128]{1,0:T(8,128)S(1)} %get-tuple-element.34), channel_id=1, source_target_pairs={{16,0},{32,16},{48,32},{64,48},{80,64},{96,80},{112,96},{128,112},... | collective-permute-start | bytes 147464 | tf_op jit(solution)/shard_map/ppermute | solution.py:342
  71.0 2.4 %collective-permute-start.2 = (f32[96,128]{1,0:T(8,128)S(1)}, f32[96,128]{1,0:T(8,128)S(1)}, u32[]{:S(2)}, u32[]{:S(2)}) collective-permute-start(f32[96,128]{1,0:T(8,128)S(1)} %get-tuple-element.34), channel_id=1, source_target_pairs={{0,16},{16,32},{32,48},{48,64},{64,80},{80,96},{96,112},{112,128},... | collective-permute-start | bytes 147464 | tf_op jit(solution)/shard_map/ppermute | solution.py:341
  73.5 0.0 collective-permute-done.3.after
  73.5 6.2 %collective-permute-done.2.before = f32[96,128]{1,0:T(8,128)S(1)} collective-permute-done((f32[96,128]{1,0:T(8,128)S(1)}, f32[96,128]{1,0:T(8,128)S(1)}, u32[]{:S(2)}, u32[]{:S(2)}) %collective-permute-start.2) | collective-permute-done | bytes 49184 | tf_op jit(solution)/shard_map/ppermute | solution.py:341
  79.6 0.3 shard_map.104
  79.9 13.4 %all_to_all.17 = f32[16,32,128]{2,1,0:T(8,128)S(1)} all-to-all(f32[16,32,128]{2,1,0:T(8,128)S(1)} %bitcast.6), channel_id=1, replica_groups=mesh['tile'=64,'node'=16] {'node'}, dimensions={0} | all-to-all | bytes 524288 | tf_op jit(solution)/shard_map/all_to_all | solution.py:346
  93.3 0.6 reduce_sum.9
Async XLA Ops:
  0.0 10.0 %collective-permute-start.1 = (f32[512,128]{1,0:T(8,128)}, f32[512,128]{1,0:T(8,128)S(1)}, u32[]{:S(2)}, u32[]{:S(2)}) collective-permute-start(f32[512,128]{1,0:T(8,128)} %mask_in.1), channel_id=1, source_target_pairs={{16,0},{32,16},{48,32},{64,48},{80,64},{96,80},{112,96},{128,112},... | collective-permute-start | bytes 786440 | tf_op jit(solution)/shard_map/ppermute | solution.py:281
  5.6 12.7 %collective-permute-start = (f32[512,128]{1,0:T(8,128)}, f32[512,128]{1,0:T(8,128)S(1)}, u32[]{:S(2)}, u32[]{:S(2)}) collective-permute-start(f32[512,128]{1,0:T(8,128)} %mask_in.1), channel_id=1, source_target_pairs={{0,16},{16,32},{32,48},{48,64},{64,80},{80,96},{96,112},{112,128},... | collective-permute-start | bytes 786440 | tf_op jit(solution)/shard_map/ppermute | solution.py:280
  69.1 4.3 %collective-permute-start.3 = (f32[96,128]{1,0:T(8,128)S(1)}, f32[96,128]{1,0:T(8,128)S(1)}, u32[]{:S(2)}, u32[]{:S(2)}) collective-permute-start(f32[96,128]{1,0:T(8,128)S(1)} %get-tuple-element.34), channel_id=1, source_target_pairs={{16,0},{32,16},{48,32},{64,48},{80,64},{96,80},{112,96},{128,112},... | collective-permute-start | bytes 147464 | tf_op jit(solution)/shard_map/ppermute | solution.py:342
  71.0 8.6 %collective-permute-start.2 = (f32[96,128]{1,0:T(8,128)S(1)}, f32[96,128]{1,0:T(8,128)S(1)}, u32[]{:S(2)}, u32[]{:S(2)}) collective-permute-start(f32[96,128]{1,0:T(8,128)S(1)} %get-tuple-element.34), channel_id=1, source_target_pairs={{0,16},{16,32},{32,48},{48,64},{64,80},{80,96},{96,112},{112,128},... | collective-permute-start | bytes 147464 | tf_op jit(solution)/shard_map/ppermute | solution.py:341

commit v3 on v2

v3 whole, which is shorter than its diff:
```python
import functools
import math

import jax
import jax.numpy as jnp
import ml_dtypes
import numpy as np
from jax import lax
from jax.experimental import pallas as pl
from jax.experimental.pallas import tpu as pltpu
from jax.sharding import PartitionSpec as P

LEVELS = 5
resist_slope = 4.0
resist_level = 0.6
degrees = [(d - q, q) for d in range(5) for q in range(d + 1)]
f32, bf16 = jnp.float32, jnp.bfloat16
vmem = pl.BlockSpec(memory_space=pltpu.VMEM)
smem = pl.BlockSpec(memory_space=pltpu.SMEM)
hbm = pl.BlockSpec(memory_space=pltpu.HBM)


def parts_of(value):
    high = value.astype(bf16)
    return high, (value - high.astype(f32)).astype(bf16)


def mm(a, b):
    return jnp.dot(a, b, preferred_element_type=f32)


def mm3(a, b):
    return mm(a[0], b[0]) + mm(a[0], b[1]) + mm(a[1], b[0])


def cosine(turn, period):
    turn = jnp.bitwise_and(turn, period - 1)
    half = jnp.minimum(turn, period - turn)
    far = half > period // 4
    angle = jnp.where(far, period // 2 - half, half).astype(f32) * (2.0 * math.pi / period)
    z = angle * angle
    poly = jnp.full_like(z, 1.0 / math.factorial(12))
    for order in (10, 8, 6, 4, 2, 0):
        sign = -1.0 if order % 4 == 2 else 1.0
        poly = poly * z + sign / math.factorial(order)
    return jnp.where(far, -poly, poly)


def column_waves(length):
    turn = (np.arange(length)[:, None] * np.arange(length)[None, :]) % length
    wave = np.concatenate([np.cos(2 * np.pi * turn / length), np.sin(2 * np.pi * turn / length)], 1)
    high = wave.astype(np.float32).astype(ml_dtypes.bfloat16)
    low = (wave - high.astype(np.float64)).astype(np.float32).astype(ml_dtypes.bfloat16)
    return high, low


def lanes(shape):
    return lax.broadcasted_iota(jnp.int32, shape, len(shape) - 1)


def turned(value):
    return pltpu.roll(value, value.shape[-1] // 2, len(value.shape) - 1)


def outer_lanes(shape, radius):
    lane = lanes(shape)
    return (lane < radius) | (lane >= shape[-1] - radius)


def right_lanes(shape, radius):
    lane, half = lanes(shape), shape[-1] // 2
    return (lane < radius) | ((lane >= half) & (lane < half + radius))


def spectrum_kernel(radius, node, freq_in, mask_in, target_in, packed_ref, wanted_ref, fh_ref, fl_ref, freq, mask, raw, sems):
    rows, cols = mask.shape
    count = freq.shape[0]
    terms, share = raw.shape[0], raw.shape[1]
    own = node[0]
    mirrored = own >= rows // (2 * share)
    at = jnp.where(mirrored, rows + rows // 2 - share - own * share, own * share)
    at = pl.multiple_of(at, share)
    moves = [(freq_in, freq), (mask_in, mask), (target_in.at[:, pl.ds(at, share), :], raw)]
    copies = [pltpu.make_async_copy(source, goal, sems.at[i]) for i, (source, goal) in enumerate(moves)]
    for copy in copies:
        copy.start()
    copies[0].wait()
    line = lax.broadcasted_iota(jnp.int32, (2 * count, 128), 0)
    f_freq = jnp.zeros((2 * count, 128), jnp.int32)
    for i in range(count):
        f_freq = jnp.where((line == i) | (line == i + count), freq[i], f_freq)
    f_full = jnp.concatenate([f_freq] * (rows // 128), 1)
    f_row = lax.broadcasted_iota(jnp.int32, (2 * count, rows), 0)
    turn = f_full * (2 * lanes((2 * count, rows)) + 1) + jnp.where(f_row >= count, rows // 2, 0)
    f_parts = parts_of(cosine(turn, 2 * rows))
    fh_ref[...], fl_ref[...] = f_parts
    copies[2].wait()
    row = lax.broadcasted_iota(jnp.int32, (share, share), 0)
    chosen = jnp.where(mirrored, share - 1 - row, row) == lanes((share, share))
    order = jnp.where(chosen, 1.0, 0.0).astype(bf16)
    half = share // 2
    outer = outer_lanes((half, cols), radius)
    for j in range(terms):
        goal = mm(order, raw[j])
        wanted_ref[j] = goal.astype(bf16)
        edge = jnp.where(outer, goal[:half], turned(goal[half:]))
        packed_ref[4 * count + half * j : 4 * count + half * (j + 1), :] = edge.astype(bf16)
    copies[1].wait()
    high, low = parts_of(mm3(f_parts, parts_of(mask[...])) * (1.0 / math.sqrt(rows)))
    packed_ref[0 : 2 * count, :] = high
    packed_ref[2 * count : 4 * count, :] = low


def tables_kernel(
    node, freq_in, index_in, node_weights_in, chaos_in, weights_in, taps_in, wave_hi_in, wave_lo_in,
    u_ref, cs_ref, gr_ref, gi_ref, wave_hi, wave_lo, scalars_ref,
    freq, index, node_weights, chaos, weights, taps, sems,
):
    rows = u_ref.shape[0]
    count = freq.shape[0]
    kernels, tap_count = taps.shape[1], taps.shape[4]
    span = wave_hi.shape[0]
    radius = (tap_count - 1) // 2
    nodes = index.shape[1]
    moves = [
        (freq_in, freq),
        (index_in, index),
        (node_weights_in, node_weights),
        (chaos_in, chaos),
        (weights_in, weights),
        (wave_hi_in, wave_hi),
        (wave_lo_in, wave_lo),
        (taps_in, taps),
    ]
    copies = [pltpu.make_async_copy(source, goal, sems.at[i]) for i, (source, goal) in enumerate(moves)]
    for copy in copies:
        copy.start()
    for copy in copies[:4]:
        copy.wait()
    lane = lanes((8, 256))
    u_freq = jnp.zeros((8, 256), jnp.int32)
    for i in range(count):
        u_freq = jnp.where((lane == i) | (lane == i + count) | (lane == i + 2 * count), freq[i], u_freq)
    quarter = rows // 2
    full = jnp.concatenate([u_freq[:, :128]] * (rows // 8), 0)
    u_lane = lanes((rows, 128))
    u_y = lax.broadcasted_iota(jnp.int32, (rows, 128), 0)
    table = cosine(full * (2 * u_y + 1) + jnp.where(u_lane >= count, quarter, 0), 2 * rows)
    high, low = parts_of(jnp.where(u_lane < 2 * count, table, 0.0))
    u_ref[:, 0:128] = high
    u_ref[:, 128:256] = high
    u_ref[:, 256:384] = low
    full = jnp.concatenate([u_freq] * (rows // 8), 0)
    c_row = lax.broadcasted_iota(jnp.int32, (rows, 256), 0)
    sine = c_row >= rows // 2
    c_y = jnp.where(sine, c_row - rows // 2, c_row)
    table = cosine(full * (2 * c_y + 1) - jnp.where(sine, quarter, 0), 2 * rows)
    high, low = parts_of(table)
    both = jnp.where(lanes((rows, 256)) < 2 * count, high.astype(f32), low.astype(f32))
    cs_ref[...] = both[:, : 3 * count].astype(bf16)
    for n in range(nodes):
        poly = []
        for axis in range(2):
            c = index[axis, n].astype(f32) * (2.0 / (LEVELS - 1)) - 1.0
            s = c * c
            poly.append([None, c, 1.5 * s - 0.5, (2.5 * s - 1.5) * c, (4.375 * s - 3.75) * s + 0.375])
        weight = node_weights[n]
        for j, (p, q) in enumerate(degrees):
            value = weight
            if p:
                value = value * poly[0][p]
            if q:
                value = value * poly[1][q]
            scalars_ref[16 * n + j : 16 * n + j + 1, :] = jnp.full((1, 128), value, f32)
    dose = 1.0 + 0.1 * (index[1, node[0]].astype(f32) * (2.0 / (LEVELS - 1)) - 1.0)
    scalars_ref[15:16, :] = jnp.full((1, 128), dose, f32)
    for j in range(len(degrees)):
        scalars_ref[16 * nodes + j : 16 * nodes + j + 1, :] = jnp.full((1, 128), chaos[j], f32)
    for copy in copies[4:]:
        copy.wait()
    side = [jnp.concatenate([w[span - radius : span], w[0 : tap_count - radius]], 0) for w in (wave_hi, wave_lo)]
    scale = jnp.sqrt(weights[...]) * (1.0 / (span * math.sqrt(count)))
    for k in range(kernels):
        parts = parts_of(taps[0, k].reshape(2 * count, tap_count))
        prod = mm3(parts, side)
        amount = scale[0:1, k : k + 1]
        gr_ref[k] = (prod[:count, :span] - prod[count:, span:]) * amount
        gi_ref[k] = (prod[:count, span:] + prod[count:, :span]) * amount


def forward_kernel(
    radius, tiles, tile, scalars, packed, before, after, gr, gi, cs, wave_hi, wave_lo,
    image_ref, slope_ref, fields_ref, bh, bl, x, total,
):
    kernels, count, span = gr.shape
    nodes, slab, cols = image_ref.shape
    rows = slope_ref.shape[0]
    share = rows // nodes
    half = share // 2
    near = lanes((2 * count, cols)) < 2 * radius
    pair = []
    for part in range(2):
        at = pl.ds(2 * part * count, 2 * count)
        beyond = jnp.where(near, after[at, :].astype(f32), before[at, :].astype(f32))
        pair.append(jnp.concatenate([packed[at, :], beyond.astype(bf16)], 1))
    wave = (wave_hi[...], wave_lo[...])
    prod = mm3(pair, wave)
    a_re = prod[:count, :span] + prod[count:, span:]
    a_im = prod[count:, :span] - prod[:count, span:]
    for k in range(kernels):
        b_re = gr[k] * a_re - gi[k] * a_im
        b_im = gr[k] * a_im + gi[k] * a_re
        for d, value in ((0, b_re), (1, b_im)):
            at = pl.ds((2 * k + d) * count, count)
            bh[at, :], bl[at, :] = parts_of(value)
    outer = outer_lanes((count, cols), radius)
    for k in range(kernels):
        at = pl.ds(2 * k * count, 2 * count)
        q = mm3((bh[at, :], bl[at, :]), wave)
        re = q[:count, :span] - q[count:, span:]
        im = q[:count, span:] + q[count:, :span]
        edge = jnp.where(outer, re[:, cols:], turned(im[:, cols:]))
        cross = jnp.where(outer, im[:, cols:], -turned(re[:, cols:]))
        straight = jnp.concatenate([re[:, :cols], im[:, :cols], edge], 1)
        crossed = jnp.concatenate([im[:, :cols], -re[:, :cols], cross], 1)
        for d, value in ((0, straight), (1, crossed)):
            high, low = parts_of(value)
            for place, part in ((0, high), (1, low), (2, high)):
                x[k, d, place * count : (place + 1) * count, :] = part
    total[...] = jnp.zeros(total.shape, f32)

    @pl.loop(0, kernels)
    def _(k):
        even = mm(cs[: rows // 2, :], x[k, 0])
        odd = mm(cs[rows // 2 :, :], x[k, 1])
        for first, field in ((0, even - odd), (rows // 2, even + odd)):
            at = pl.ds(first, rows // 2)
            fields_ref[k, at, :] = field
            square = field * field
            total[at, :cols] += square[:, :cols] + square[:, cols : 2 * cols]
            total[at, cols:] += square[:, 2 * cols :]

    value = scalars[15:16, :]
    inner = total[:, :cols]
    edge = total[:, cols:]
    edge = edge + turned(edge)
    right = right_lanes((rows, cols), radius)
    inside = (right & (tile[0] < tiles - 1)) | (jnp.logical_not(right) & (tile[0] > 0))
    outer = outer_lanes((half, cols), radius)
    for place, intensity in ((0, inner), (1, edge)):
        resist = jax.nn.sigmoid(resist_slope * (value * intensity - resist_level))
        slope = resist * (1.0 - resist) * (2.0 * resist_slope * value)
        if place:
            slope = jnp.where(inside, slope, 0.0)
        slope_ref[:, place * cols : (place + 1) * cols] = slope
        for n in range(nodes):
            rows_n = resist[n * share : (n + 1) * share]
            if place:
                image_ref[n, share:slab, :] = jnp.where(outer, rows_n[:half], rows_n[half:]).astype(bf16)
            else:
                image_ref[n, 0:share, :] = rows_n.astype(bf16)


def middle_kernel(radius, offset, images, wanted, before, after, scalars, pressure_ref):
    nodes, slab, cols = images.shape
    share = wanted.shape[1]
    step = slab - share
    right = right_lanes((step, cols), radius)
    for first in range(0, slab, step):
        image = [images[n, first : first + step, :].astype(f32) for n in range(nodes)]
        pressure = [None] * nodes
        for j in range(len(degrees)):
            weight = [scalars[16 * n + j : 16 * n + j + 1, :] for n in range(nodes)]
            coefficient = weight[0] * image[0]
            for n in range(1, nodes):
                coefficient = coefficient + weight[n] * image[n]
            if first < share:
                goal = wanted[j, first : first + step, :].astype(f32)
            else:
                at = pl.ds(offset + j * step, step)
                goal = jnp.where(right, after[at, :].astype(f32), before[at, :].astype(f32))
            mixed = scalars[16 * nodes + j : 16 * nodes + j + 1, :] * jnp.tanh(coefficient - goal)
            for n in range(nodes):
                term = weight[n] * mixed
                pressure[n] = term if j == 0 else pressure[n] + term
        for n in range(nodes):
            pressure_ref[n, first : first + step, :] = pressure[n]


def backward_kernel(radius, pressure, slope, fields, fh, fl, gr, gi, u, wave_hi, wave_lo, out_ref, dh, dl, scale):
    kernels, count, span = gr.shape
    nodes, slab, cols = pressure.shape
    rows = slope.shape[0]
    share = rows // nodes
    half = share // 2
    outer = outer_lanes((half, cols), radius)
    for n in range(nodes):
        at = pl.ds(n * share, share)
        scale[at, :cols] = slope[at, :cols] * pressure[n, :share, :]
        edge = pressure[n, share:, :]
        back = turned(edge)
        top, bottom = pl.ds(n * share, half), pl.ds(n * share + half, half)
        scale[top, cols:] = slope[top, cols:] * jnp.where(outer, edge, back)
        scale[bottom, cols:] = slope[bottom, cols:] * jnp.where(outer, back, edge)
    table = []
    for first in (0, count):
        table.append(jnp.concatenate([fh[first : first + count, : rows // 2], fl[first : first + count, : rows // 2]], 0))
    outer = outer_lanes((count, cols), radius)

    @pl.loop(0, kernels)
    def _(k):
        halves = []
        for first in (0, rows // 2):
            at = pl.ds(first, rows // 2)
            inner, edge = scale[at, :cols], scale[at, cols:]
            halves.append(fields[k, at, :] * jnp.concatenate([inner, inner, edge], 1))
        grads = []
        for lhs, value in zip(table, (halves[0] + halves[1], halves[0] - halves[1])):
            high, low = parts_of(value)
            prod = mm(lhs, high)
            grads.append(prod[:count] + prod[count:] + mm(lhs[:count], low))
        straight, crossed = grads
        edge, cross = straight[:, 2 * cols :], crossed[:, 2 * cols :]
        re_edge = jnp.where(outer, edge - turned(cross), 0.0)
        im_edge = jnp.where(outer, cross + turned(edge), 0.0)
        re = jnp.concatenate([straight[:, :cols] - crossed[:, cols : 2 * cols], re_edge], 1)
        im = jnp.concatenate([straight[:, cols : 2 * cols] + crossed[:, :cols], im_edge], 1)
        at = pl.multiple_of(2 * k * count, 2 * count)
        dh[pl.ds(at, count), :], dl[pl.ds(at, count), :] = parts_of(re)
        at = pl.multiple_of(at + count, count)
        dh[pl.ds(at, count), :], dl[pl.ds(at, count), :] = parts_of(im)

    wave = (wave_hi[...], wave_lo[...])
    a_re = jnp.zeros((count, span), f32)
    a_im = jnp.zeros((count, span), f32)
    for k in range(kernels):
        at = pl.ds(2 * k * count, 2 * count)
        q = mm3((dh[at, :], dl[at, :]), wave)
        b_re = q[:count, :span] + q[count:, span:]
        b_im = q[count:, :span] - q[:count, span:]
        a_re = a_re + gr[k] * b_re + gi[k] * b_im
        a_im = a_im + gr[k] * b_im - gi[k] * b_re
    near = [jnp.concatenate([w[:, 0:cols], w[:, span : span + cols]], 1) for w in (wave_hi, wave_lo)]
    prod = mm3(parts_of(jnp.concatenate([a_re, a_im], 0)), near)
    d_re = prod[:count, :cols] - prod[count:, cols:]
    d_im = prod[:count, cols:] + prod[count:, :cols]
    rest = jnp.zeros((128 - 2 * count, cols), f32)
    high, low = parts_of(jnp.concatenate([d_re, d_im, rest], 0))
    out_ref[...] = mm(u[...], jnp.concatenate([high, low, high], 0)) * (1.0 / math.sqrt(rows))


def shape_of(*shape, dtype=f32):
    return jax.ShapeDtypeStruct(shape, dtype)


def call(kernel, mebibytes, spaces, outs, scratch=()):
    return pl.pallas_call(
        kernel,
        in_specs=spaces,
        out_specs=[vmem] * len(outs),
        out_shape=list(outs),
        scratch_shapes=list(scratch),
        compiler_params=pltpu.CompilerParams(vmem_limit_bytes=mebibytes << 20),
    )


def kept(*arrays):
    return [pltpu.with_memory_space_constraint(a, pltpu.HBM) for a in arrays]


def local(mask, taps, weights, node_weights, node_index, freq, chaos, target):
    rows, cols = mask.shape
    kernels, count, tap_count = taps.shape[1], taps.shape[3], taps.shape[4]
    terms = target.shape[0]
    radius = (tap_count - 1) // 2
    span = 2 * cols
    nodes, tiles = lax.axis_size("node"), lax.axis_size("tile")
    node, tile = lax.axis_index("node").reshape(1), lax.axis_index("tile").reshape(1)
    share = rows // nodes
    half = share // 2
    slab = share + half
    up = [(i, i + 1) for i in range(tiles - 1)]
    down = [(i + 1, i) for i in range(tiles - 1)]
    wave_hi, wave_lo = (jnp.asarray(w) for w in column_waves(span))
    packed, wanted, fh, fl = call(
        functools.partial(spectrum_kernel, radius),
        8,
        [smem] + [hbm] * 3,
        [
            shape_of(4 * count + half * terms, cols, dtype=bf16),
            shape_of(terms, share, cols, dtype=bf16),
            shape_of(2 * count, rows, dtype=bf16),
            shape_of(2 * count, rows, dtype=bf16),
        ],
        [
            pltpu.SMEM(freq.shape, jnp.int32),
            pltpu.VMEM(mask.shape, f32),
            pltpu.VMEM((terms, share, cols), bf16),
            pltpu.SemaphoreType.DMA((3,)),
        ],
    )(node, *kept(freq, mask, target))
    before = lax.ppermute(packed, "tile", up)
    after = lax.ppermute(packed, "tile", down)
    u, cs, gr, gi, wave_hi, wave_lo, scalars = call(
        tables_kernel,
        16,
        [smem] + [hbm] * 8,
        [
            shape_of(rows, 384, dtype=bf16),
            shape_of(rows, 3 * count, dtype=bf16),
            shape_of(kernels, count, span),
            shape_of(kernels, count, span),
            shape_of(span, 2 * span, dtype=bf16),
            shape_of(span, 2 * span, dtype=bf16),
            shape_of(16 * nodes + 16, 128),
        ],
        [
            pltpu.SMEM(freq.shape, jnp.int32),
            pltpu.SMEM((2, nodes), jnp.int32),
            pltpu.SMEM((nodes,), f32),
            pltpu.SMEM(chaos.shape, f32),
            pltpu.VMEM(weights.shape, f32),
            pltpu.VMEM(taps.shape, f32),
            pltpu.SemaphoreType.DMA((8,)),
        ],
    )(node, *kept(freq, node_index.T, node_weights, chaos, weights, taps, wave_hi, wave_lo))
    image, slope, fields = call(
        functools.partial(forward_kernel, radius, tiles),
        20,
        [smem] + [vmem] * 9,
        [
            shape_of(nodes, slab, cols, dtype=bf16),
            shape_of(rows, 2 * cols),
            shape_of(kernels, rows, 3 * cols),
        ],
        [
            pltpu.VMEM((2 * kernels * count, span), bf16),
            pltpu.VMEM((2 * kernels * count, span), bf16),
            pltpu.VMEM((kernels, 2, 3 * count, 3 * cols), bf16),
            pltpu.VMEM((rows, 2 * cols), f32),
        ],
    )(tile, scalars, packed, before, after, gr, gi, cs, wave_hi, wave_lo)
    images = lax.all_to_all(image, "node", 0, 0)
    (pressure,) = call(
        functools.partial(middle_kernel, radius, 4 * count), 8, [vmem] * 5, [shape_of(nodes, slab, cols)]
    )(images, wanted, before, after, scalars)
    pressure = lax.all_to_all((pressure * 8192.0).astype(jnp.float16), "node", 0, 0).astype(f32) * (1.0 / 8192.0)
    (spread,) = call(
        functools.partial(backward_kernel, radius),
        16,
        [vmem] * 10,
        [shape_of(rows, cols)],
        [
            pltpu.VMEM((2 * kernels * count, span), bf16),
            pltpu.VMEM((2 * kernels * count, span), bf16),
            pltpu.VMEM((rows, 2 * cols), f32),
        ],
    )(pressure, slope, fields, fh, fl, gr, gi, u, wave_hi, wave_lo)
    return lax.all_to_all(spread.reshape(nodes, share, cols), "node", 0, 0).sum(0)


def solution(mesh):
    placed = (
        P(None, "tile"),
        P("node", None, None, None, None),
        P("node", None),
        P(),
        P(),
        P(),
        P(),
        P(None, None, "tile"),
    )
    return jax.shard_map(local, mesh=mesh, in_specs=placed, out_specs=P("node", "tile"), check_vma=False)
```

time: 94.8 us -> 80.6 us (0.85)
  waiting for transfers between devices: 14.4 us -> 5.05 us
  starting transfers between devices: 11.8 us -> 7.48 us
  blocking collectives: 56.3 us -> 52 us
  Pallas kernels: 10.7 us -> 14.1 us
    ppermute x4 -> x2, waiting for transfers between devices: 14.4 us -> 5.05 us  [the longest x1 5.04 us: local(): before = lax.ppermute(packed, 'tile', up)]
    ppermute x4 -> x2, starting transfers between devices: 11.8 us -> 7.48 us  [the longest x1 5.56 us: local(): after = lax.ppermute(packed, 'tile', down)]
    all_to_all x2, blocking collectives: 43 us -> 39 us  [the longest x1 26.7 us: local(): images = lax.all_to_all(image, 'node', 0, 0)]
    pallas_call x5, Pallas kernels: 10.7 us -> 14.1 us  [the longest x1 4.92 us: local(): call(functools.partial(backward_kernel, radius), 16, [vmem] * 10, [shape_...]
  transfers between devices with their start and end apart: 4 -> 2, of which waited for: 2 -> 1; matrix products, arithmetic and copies ran while one was open for 0% -> 0% of each run, Pallas kernels for 3% -> 3%
where the time goes in v3:
time: 80.6 us; the launch traced here: 79.5 us
  blocking collectives  52 us (65%)
  Pallas kernels  14.1 us (17%)
  starting transfers between devices  7.48 us (9%)
  waiting for transfers between devices  5.05 us (6%)
    all_to_all x1, blocking collectives, local(): images = lax.all_to_all(image, 'node', 0, 0)  26.7 us
    all_to_all x1, blocking collectives, local(): lax.all_to_all(spread.reshape(nodes, share, cols), 'node', 0, 0).sum(0)  13 us
    all_to_all x1, blocking collectives, local(): lax.all_to_all((pressure * 8192.0).astype(jnp.float16), 'node', 0, 0)  12.3 us
    ppermute x1, starting transfers between devices, local(): after = lax.ppermute(packed, 'tile', down)  5.56 us
    ppermute x1, waiting for transfers between devices, local(): before = lax.ppermute(packed, 'tile', up)  5.04 us
    pallas_call x1, Pallas kernels, local(): call(functools.partial(backward_kernel, radius), 16, [vmem] * 10, [shape_...  4.92 us
    pallas_call x1, Pallas kernels, local(): call(functools.partial(forward_kernel, radius, tiles), 20, [smem] + [vmem...  4.33 us
    pallas_call x1, Pallas kernels, local(): call(tables_kernel, 16, [smem] + [hbm] * 8, [shape_of(rows, 384, dtype=bf...  2.59 us
  transfers between devices with their start and end apart: 2, of which 1 were waited for; matrix products, arithmetic and copies ran while one was open for 0% of the time, Pallas kernels for 3%

profile of v3, /device:TPU:112, one launch (start us, length us, event | category | flops | bytes accessed | tf_op | source)
XLA Modules:
  0.0 79.5 jit_solution(13068565354745813153)
XLA Ops:
  0.0 1.5 %shard_map.101 = (bf16[432,128]{1,0:T(8,128)(2,1)S(1)}, bf16[15,32,128]{2,1,0:T(8,128)(2,1)S(1)}, bf16[96,512]{1,0:T(8,128)(2,1)S(1)}, bf16[96,512]{1,0:T(8,128)(2,1)S(1)}) custom-call(s32[1]{0:T(128)} %bitcast.1.node, s32[48]{0:T(128)} %freq_in.3, f32[512,128]{1,0:T(8,128)} %mask_in.1, bf16[15,512,128]{2,1,0:T(8,128)(2,1)} %target_in.1), custom_call_target="tpu_custom_call" | custom-call | tf_op jit(solution)/shard_map/pallas_call | solution.py:385
  1.5 5.6 %collective-permute-start.1 = (bf16[432,128]{1,0:T(8,128)(2,1)S(1)}, bf16[432,128]{1,0:T(8,128)(2,1)S(1)}, u32[]{:S(2)}, u32[]{:S(2)}) collective-permute-start(bf16[432,128]{1,0:T(8,128)(2,1)S(1)} %get-tuple-element.20.packed), channel_id=1, source_target_pairs={{16,0},{32,16},{48,32},{64,48},{80,64},{96,80},{112,96},{128,112},... | collective-permute-start | bytes 331784 | tf_op jit(solution)/shard_map/ppermute | solution.py:403
  7.1 1.9 %collective-permute-start = (bf16[432,128]{1,0:T(8,128)(2,1)S(1)}, bf16[432,128]{1,0:T(8,128)(2,1)S(1)}, u32[]{:S(2)}, u32[]{:S(2)}) collective-permute-start(bf16[432,128]{1,0:T(8,128)(2,1)S(1)} %get-tuple-element.20.packed), channel_id=1, source_target_pairs={{0,16},{16,32},{32,48},{48,64},{64,80},{80,96},{96,112},{112,128},... | collective-permute-start | bytes 331784 | tf_op jit(solution)/shard_map/ppermute | solution.py:402
  9.0 2.6 %shard_map.100 = (bf16[512,384]{1,0:T(8,128)(2,1)S(1)}, bf16[512,144]{1,0:T(8,128)(2,1)S(1)}, f32[8,48,256]{2,1,0:T(8,128)S(1)}, f32[8,48,256]{2,1,0:T(8,128)S(1...) custom-call(s32[1]{0:T(128)} %bitcast.1.node, s32[48]{0:T(128)} %freq_in.3, ...), custom_call_target="tpu_custom_call" | custom-call | tf_op jit(solution)/shard_map/pallas_call | solution.py:404
  11.6 0.0 collective-permute-done.1.after
  11.6 5.0 %collective-permute-done.before = bf16[432,128]{1,0:T(8,128)(2,1)S(1)} collective-permute-done((bf16[432,128]{1,0:T(8,128)(2,1)S(1)}, bf16[432,128]{1,0:T(8,128)(2,1)S(1)}, u32[]{:S(2)}, u32[]{:S(2)}) %collective-permute-start) | collective-permute-done | bytes 110624 | tf_op jit(solution)/shard_map/ppermute | solution.py:402
  16.7 4.3 %shard_map.102 = (bf16[16,48,128]{2,1,0:T(8,128)(2,1)S(1)}, f32[512,256]{1,0:T(8,128)S(1)}, f32[8,512,384]{2,1,0:T(8,128)S(1)}) custom-call(s32[1]{0:T(128)} %bitcast.tile, f32[272,128]{1,0:T(8,128)S(1)} %get-tuple-element.19.scalars, bf16[432,128]{1,0:T(8,128)(2,1)S(1)} %get-tuple-element.20.packed, bf16[432,128]{1,0:T(8,128)(2,1)S(1)} %collective-permute-done.before, ...), custom_call_target="tpu_custom_call" | custom-call | tf_op jit(solution)/shard_map/pallas_call | solution.py:427
  21.0 26.7 %all_to_all.15.images = bf16[16,48,128]{2,1,0:T(8,128)(2,1)S(1)} all-to-all(bf16[16,48,128]{2,1,0:T(8,128)(2,1)S(1)} %get-tuple-element.26), channel_id=1, replica_groups=mesh['tile'=64,'node'=16] {'node'}, dimensions={0} | all-to-all | bytes 393216 | tf_op jit(solution)/shard_map/all_to_all | solution.py:443
  47.6 0.8 %shard_map.103 = f32[16,48,128]{2,1,0:T(8,128)S(1)} custom-call(bf16[16,48,128]{2,1,0:T(8,128)(2,1)S(1)} %all_to_all.15.images, bf16[15,32,128]{2,1,0:T(8,128)(2,1)S(1)} %get-tuple-element.27.wanted, bf16[432,128]{1,0:T(8,128)(2,1)S(1)} %collective-permute-done.before, bf16[432,128]{1,0:T(8,128)(2,1)S(1)} %collective-permute-done.1.after, ...), custom_call_target="tpu_custom_call" | custom-call | tf_op jit(solution)/shard_map/pallas_call | solution.py:444
  48.5 12.3 %all_to_all.16 = f16[16,48,128]{2,1,0:T(8,128)(2,1)S(1)} all-to-all(f16[16,48,128]{2,1,0:T(8,128)(2,1)S(1)} %multiply_convert_fusion), channel_id=1, replica_groups=mesh['tile'=64,'node'=16] {'node'}, dimensions={0} | all-to-all | bytes 393216 | tf_op jit(solution)/shard_map/all_to_all | solution.py:447
  60.9 4.9 %shard_map.104 = f32[512,128]{1,0:T(8,128)S(1)} custom-call(f32[16,48,128]{2,1,0:T(8,128)S(1)} %convert_multiply_fusion.pressure, f32[512,256]{1,0:T(8,128)S(1)} %get-tuple-element.28.slope, f32[8,512,384]{2,1,0:T(8,128)S(1)} %get-tuple-element.29.fields, bf16[96,512]{1,0:T(8,128)(2,1)S(1)} %get-tuple-element.30.fh, ...), custom_call_target="tpu_custom_call" | custom-call | tf_op jit(solution)/shard_map/pallas_call | solution.py:448
  65.8 13.0 %all_to_all.17 = f32[16,32,128]{2,1,0:T(8,128)S(1)} all-to-all(f32[16,32,128]{2,1,0:T(8,128)S(1)} %bitcast.4), channel_id=1, replica_groups=mesh['tile'=64,'node'=16] {'node'}, dimensions={0} | all-to-all | bytes 524288 | tf_op jit(solution)/shard_map/all_to_all | solution.py:459
  78.8 0.6 reduce_sum.9
  (2 shorter events, 0.1 us)
Async XLA Ops:
  1.5 10.1 %collective-permute-start.1 = (bf16[432,128]{1,0:T(8,128)(2,1)S(1)}, bf16[432,128]{1,0:T(8,128)(2,1)S(1)}, u32[]{:S(2)}, u32[]{:S(2)}) collective-permute-start(bf16[432,128]{1,0:T(8,128)(2,1)S(1)} %get-tuple-element.20.packed), channel_id=1, source_target_pairs={{16,0},{32,16},{48,32},{64,48},{80,64},{96,80},{112,96},{128,112},... | collective-permute-start | bytes 331784 | tf_op jit(solution)/shard_map/ppermute | solution.py:403
  7.1 9.6 %collective-permute-start = (bf16[432,128]{1,0:T(8,128)(2,1)S(1)}, bf16[432,128]{1,0:T(8,128)(2,1)S(1)}, u32[]{:S(2)}, u32[]{:S(2)}) collective-permute-start(bf16[432,128]{1,0:T(8,128)(2,1)S(1)} %get-tuple-element.20.packed), channel_id=1, source_target_pairs={{0,16},{16,32},{32,48},{48,64},{64,80},{80,96},{96,112},{112,128},... | collective-permute-start | bytes 331784 | tf_op jit(solution)/shard_map/ppermute | solution.py:402

commit v4 on v3

--- a/solution.py
+++ b/solution.py
@@ -30,7 +30,7 @@
 
 
 def mm3(a, b):
-    return mm(a[0], b[0]) + mm(a[0], b[1]) + mm(a[1], b[0])
+    return mm(jnp.concatenate([a[0], a[0], a[1]], 1), jnp.concatenate([b[0], b[1], b[0]], 0))
 
 
 def cosine(turn, period):
@@ -189,7 +189,7 @@
 
 
 def forward_kernel(
-    radius, tiles, tile, scalars, packed, before, after, gr, gi, cs, wave_hi, wave_lo,
+    radius, tiles, tile, scalars, packed, after, before, gr, gi, cs, wave_hi, wave_lo,
     image_ref, slope_ref, fields_ref, bh, bl, x, total,
 ):
     kernels, count, span = gr.shape
@@ -215,8 +215,10 @@
             bh[at, :], bl[at, :] = parts_of(value)
     outer = outer_lanes((count, cols), radius)
     for k in range(kernels):
-        at = pl.ds(2 * k * count, 2 * count)
-        q = mm3((bh[at, :], bl[at, :]), wave)
+        if k % 2 == 0:
+            at = pl.ds(2 * k * count, 2 * 2 * count)
+            qq = mm3((bh[at, :], bl[at, :]), wave)
+        q = qq[(k % 2) * 2 * count : (k % 2 + 1) * 2 * count]
         re = q[:count, :span] - q[count:, span:]
         im = q[:count, span:] + q[count:, :span]
         edge = jnp.where(outer, re[:, cols:], turned(im[:, cols:]))
@@ -229,7 +231,7 @@
                 x[k, d, place * count : (place + 1) * count, :] = part
     total[...] = jnp.zeros(total.shape, f32)
 
-    @pl.loop(0, kernels)
+    @pl.loop(0, kernels, unroll=True)
     def _(k):
         even = mm(cs[: rows // 2, :], x[k, 0])
         odd = mm(cs[rows // 2 :, :], x[k, 1])
@@ -261,7 +263,7 @@
                 image_ref[n, 0:share, :] = rows_n.astype(bf16)
 
 
-def middle_kernel(radius, offset, images, wanted, before, after, scalars, pressure_ref):
+def middle_kernel(radius, offset, images, wanted, after, before, scalars, pressure_ref):
     nodes, slab, cols = images.shape
     share = wanted.shape[1]
     step = slab - share
@@ -307,7 +309,7 @@
         table.append(jnp.concatenate([fh[first : first + count, : rows // 2], fl[first : first + count, : rows // 2]], 0))
     outer = outer_lanes((count, cols), radius)
 
-    @pl.loop(0, kernels)
+    @pl.loop(0, kernels, unroll=True)
     def _(k):
         halves = []
         for first in (0, rows // 2):
@@ -334,8 +336,10 @@
     a_re = jnp.zeros((count, span), f32)
     a_im = jnp.zeros((count, span), f32)
     for k in range(kernels):
-        at = pl.ds(2 * k * count, 2 * count)
-        q = mm3((dh[at, :], dl[at, :]), wave)
+        if k % 2 == 0:
+            at = pl.ds(2 * k * count, 2 * 2 * count)
+            qq = mm3((dh[at, :], dl[at, :]), wave)
+        q = qq[(k % 2) * 2 * count : (k % 2 + 1) * 2 * count]
         b_re = q[:count, :span] + q[count:, span:]
         b_im = q[count:, :span] - q[:count, span:]
         a_re = a_re + gr[k] * b_re + gi[k] * b_im
@@ -399,8 +403,8 @@
             pltpu.SemaphoreType.DMA((3,)),
         ],
     )(node, *kept(freq, mask, target))
+    after = lax.ppermute(packed, "tile", down)
     before = lax.ppermute(packed, "tile", up)
-    after = lax.ppermute(packed, "tile", down)
     u, cs, gr, gi, wave_hi, wave_lo, scalars = call(
         tables_kernel,
         16,
@@ -439,11 +443,11 @@
             pltpu.VMEM((kernels, 2, 3 * count, 3 * cols), bf16),
             pltpu.VMEM((rows, 2 * cols), f32),
         ],
-    )(tile, scalars, packed, before, after, gr, gi, cs, wave_hi, wave_lo)
+    )(tile, scalars, packed, after, before, gr, gi, cs, wave_hi, wave_lo)
     images = lax.all_to_all(image, "node", 0, 0)
     (pressure,) = call(
         functools.partial(middle_kernel, radius, 4 * count), 8, [vmem] * 5, [shape_of(nodes, slab, cols)]
-    )(images, wanted, before, after, scalars)
+    )(images, wanted, after, before, scalars)
     pressure = lax.all_to_all((pressure * 8192.0).astype(jnp.float16), "node", 0, 0).astype(f32) * (1.0 / 8192.0)
     (spread,) = call(
         functools.partial(backward_kernel, radius),

time: 80.6 us -> 73.9 us (0.917)
  the two profiles are of different devices: /device:TPU:112 before, /device:TPU:4 now
where the time goes in v4:
time: 73.9 us; the launch traced here: 73.6 us
  blocking collectives  56.9 us (77%)
  Pallas kernels  10.4 us (14%)
  starting transfers between devices  5.56 us (8%)
    all_to_all x1, blocking collectives, local(): images = lax.all_to_all(image, 'node', 0, 0)  28.4 us
    all_to_all x1, blocking collectives, local(): lax.all_to_all(spread.reshape(nodes, share, cols), 'node', 0, 0).sum(0)  14.4 us
    all_to_all x1, blocking collectives, local(): lax.all_to_all((pressure * 8192.0).astype(jnp.float16), 'node', 0, 0)  14.2 us
    ppermute x1, starting transfers between devices, local(): after = lax.ppermute(packed, 'tile', down)  3.64 us
    pallas_call x1, Pallas kernels, local(): call(functools.partial(backward_kernel, radius), 16, [vmem] * 10, [shape_...  3.23 us
    pallas_call x1, Pallas kernels, local(): call(functools.partial(forward_kernel, radius, tiles), 20, [smem] + [vmem...  2.51 us
    pallas_call x1, Pallas kernels, local(): call(tables_kernel, 16, [smem] + [hbm] * 8, [shape_of(rows, 384, dtype=bf...  2.31 us
    ppermute x1, starting transfers between devices, local(): before = lax.ppermute(packed, 'tile', up)  1.92 us
  transfers between devices with their start and end apart: 2, of which 0 were waited for; matrix products, arithmetic and copies ran while one was open for 0% of the time, Pallas kernels for 3%

profile of v4, /device:TPU:4, one launch (start us, length us, event | category | flops | bytes accessed | tf_op | source)
XLA Modules:
  0.0 73.6 jit_solution(2069962110044732155)
XLA Ops:
  0.0 1.5 %shard_map.101 = (bf16[432,128]{1,0:T(8,128)(2,1)S(1)}, bf16[15,32,128]{2,1,0:T(8,128)(2,1)S(1)}, bf16[96,512]{1,0:T(8,128)(2,1)S(1)}, bf16[96,512]{1,0:T(8,128)(2,1)S(1)}) custom-call(s32[1]{0:T(128)} %bitcast.1.node, s32[48]{0:T(128)} %freq_in.3, f32[512,128]{1,0:T(8,128)} %mask_in.1, bf16[15,512,128]{2,1,0:T(8,128)(2,1)} %target_in.1), custom_call_target="tpu_custom_call" | custom-call | tf_op jit(solution)/shard_map/pallas_call | solution.py:389
  1.5 1.9 %collective-permute-start.1 = (bf16[432,128]{1,0:T(8,128)(2,1)S(1)}, bf16[432,128]{1,0:T(8,128)(2,1)S(1)}, u32[]{:S(2)}, u32[]{:S(2)}) collective-permute-start(bf16[432,128]{1,0:T(8,128)(2,1)S(1)} %get-tuple-element.20.packed), channel_id=1, source_target_pairs={{0,16},{16,32},{32,48},{48,64},{64,80},{80,96},{96,112},{112,128},... | collective-permute-start | bytes 331784 | tf_op jit(solution)/shard_map/ppermute | solution.py:407
  3.4 3.6 %collective-permute-start = (bf16[432,128]{1,0:T(8,128)(2,1)S(1)}, bf16[432,128]{1,0:T(8,128)(2,1)S(1)}, u32[]{:S(2)}, u32[]{:S(2)}) collective-permute-start(bf16[432,128]{1,0:T(8,128)(2,1)S(1)} %get-tuple-element.20.packed), channel_id=1, source_target_pairs={{16,0},{32,16},{48,32},{64,48},{80,64},{96,80},{112,96},{128,112},... | collective-permute-start | bytes 331784 | tf_op jit(solution)/shard_map/ppermute | solution.py:406
  7.1 2.3 %shard_map.100 = (bf16[512,384]{1,0:T(8,128)(2,1)S(1)}, bf16[512,144]{1,0:T(8,128)(2,1)S(1)}, f32[8,48,256]{2,1,0:T(8,128)S(1)}, f32[8,48,256]{2,1,0:T(8,128)S(1...) custom-call(s32[1]{0:T(128)} %bitcast.1.node, s32[48]{0:T(128)} %freq_in.3, ...), custom_call_target="tpu_custom_call" | custom-call | tf_op jit(solution)/shard_map/pallas_call | solution.py:408
  9.4 0.0 collective-permute-done.1.before
  9.4 0.0 collective-permute-done.after
  9.4 2.5 %shard_map.102 = (bf16[16,48,128]{2,1,0:T(8,128)(2,1)S(1)}, f32[512,256]{1,0:T(8,128)S(1)}, f32[8,512,384]{2,1,0:T(8,128)S(1)}) custom-call(s32[1]{0:T(128)} %bitcast.tile, f32[272,128]{1,0:T(8,128)S(1)} %get-tuple-element.19.scalars, bf16[432,128]{1,0:T(8,128)(2,1)S(1)} %get-tuple-element.20.packed, bf16[432,128]{1,0:T(8,128)(2,1)S(1)} %collective-permute-done.after, ...), custom_call_target="tpu_custom_call" | custom-call | tf_op jit(solution)/shard_map/pallas_call | solution.py:431
  11.9 28.4 %all_to_all.15.images = bf16[16,48,128]{2,1,0:T(8,128)(2,1)S(1)} all-to-all(bf16[16,48,128]{2,1,0:T(8,128)(2,1)S(1)} %get-tuple-element.26), channel_id=1, replica_groups=mesh['tile'=64,'node'=16] {'node'}, dimensions={0} | all-to-all | bytes 393216 | tf_op jit(solution)/shard_map/all_to_all | solution.py:447
  40.3 0.8 %shard_map.103 = f32[16,48,128]{2,1,0:T(8,128)S(1)} custom-call(bf16[16,48,128]{2,1,0:T(8,128)(2,1)S(1)} %all_to_all.15.images, bf16[15,32,128]{2,1,0:T(8,128)(2,1)S(1)} %get-tuple-element.27.wanted, bf16[432,128]{1,0:T(8,128)(2,1)S(1)} %collective-permute-done.after, bf16[432,128]{1,0:T(8,128)(2,1)S(1)} %collective-permute-done.1.before, ...), custom_call_target="tpu_custom_call" | custom-call | tf_op jit(solution)/shard_map/pallas_call | solution.py:448
  41.2 14.2 %all_to_all.16 = f16[16,48,128]{2,1,0:T(8,128)(2,1)S(1)} all-to-all(f16[16,48,128]{2,1,0:T(8,128)(2,1)S(1)} %multiply_convert_fusion), channel_id=1, replica_groups=mesh['tile'=64,'node'=16] {'node'}, dimensions={0} | all-to-all | bytes 393216 | tf_op jit(solution)/shard_map/all_to_all | solution.py:451
  55.4 3.2 %shard_map.104 = f32[512,128]{1,0:T(8,128)S(1)} custom-call(f32[16,48,128]{2,1,0:T(8,128)S(1)} %convert_multiply_fusion.pressure, f32[512,256]{1,0:T(8,128)S(1)} %get-tuple-element.28.slope, f32[8,512,384]{2,1,0:T(8,128)S(1)} %get-tuple-element.29.fields, bf16[96,512]{1,0:T(8,128)(2,1)S(1)} %get-tuple-element.30.fh, ...), custom_call_target="tpu_custom_call" | custom-call | tf_op jit(solution)/shard_map/pallas_call | solution.py:452
  58.7 14.4 %all_to_all.17 = f32[16,32,128]{2,1,0:T(8,128)S(1)} all-to-all(f32[16,32,128]{2,1,0:T(8,128)S(1)} %bitcast.4), channel_id=1, replica_groups=mesh['tile'=64,'node'=16] {'node'}, dimensions={0} | all-to-all | bytes 524288 | tf_op jit(solution)/shard_map/all_to_all | solution.py:463
  73.0 0.6 reduce_sum.9
  (2 shorter events, 0.1 us)
Async XLA Ops:
  1.5 7.9 %collective-permute-start.1 = (bf16[432,128]{1,0:T(8,128)(2,1)S(1)}, bf16[432,128]{1,0:T(8,128)(2,1)S(1)}, u32[]{:S(2)}, u32[]{:S(2)}) collective-permute-start(bf16[432,128]{1,0:T(8,128)(2,1)S(1)} %get-tuple-element.20.packed), channel_id=1, source_target_pairs={{0,16},{16,32},{32,48},{48,64},{64,80},{80,96},{96,112},{112,128},... | collective-permute-start | bytes 331784 | tf_op jit(solution)/shard_map/ppermute | solution.py:407
  3.4 6.0 %collective-permute-start = (bf16[432,128]{1,0:T(8,128)(2,1)S(1)}, bf16[432,128]{1,0:T(8,128)(2,1)S(1)}, u32[]{:S(2)}, u32[]{:S(2)}) collective-permute-start(bf16[432,128]{1,0:T(8,128)(2,1)S(1)} %get-tuple-element.20.packed), channel_id=1, source_target_pairs={{16,0},{32,16},{48,32},{64,48},{80,64},{96,80},{112,96},{128,112},... | collective-permute-start | bytes 331784 | tf_op jit(solution)/shard_map/ppermute | solution.py:406

commit v5 on v4

--- a/solution.py
+++ b/solution.py
@@ -189,7 +189,7 @@
 
 
 def forward_kernel(
-    radius, tiles, tile, scalars, packed, after, before, gr, gi, cs, wave_hi, wave_lo,
+    radius, tiles, tile, scalars, packed, twin, border, gr, gi, cs, wave_hi, wave_lo,
     image_ref, slope_ref, fields_ref, bh, bl, x, total,
 ):
     kernels, count, span = gr.shape
@@ -197,11 +197,12 @@
     rows = slope_ref.shape[0]
     share = rows // nodes
     half = share // 2
-    near = lanes((2 * count, cols)) < 2 * radius
+    even = lax.rem(tile[0], 2) == 0
+    near = (lanes((2 * count, cols)) < 2 * radius) == even
     pair = []
     for part in range(2):
         at = pl.ds(2 * part * count, 2 * count)
-        beyond = jnp.where(near, after[at, :].astype(f32), before[at, :].astype(f32))
+        beyond = jnp.where(near, twin[at, :].astype(f32), border[at, :].astype(f32))
         pair.append(jnp.concatenate([packed[at, :], beyond.astype(bf16)], 1))
     wave = (wave_hi[...], wave_lo[...])
     prod = mm3(pair, wave)
@@ -263,11 +264,11 @@
                 image_ref[n, 0:share, :] = rows_n.astype(bf16)
 
 
-def middle_kernel(radius, offset, images, wanted, after, before, scalars, pressure_ref):
+def middle_kernel(radius, offset, tile, images, wanted, twin, border, scalars, pressure_ref):
     nodes, slab, cols = images.shape
     share = wanted.shape[1]
     step = slab - share
-    right = right_lanes((step, cols), radius)
+    near = right_lanes((step, cols), radius) == (lax.rem(tile[0], 2) == 0)
     for first in range(0, slab, step):
         image = [images[n, first : first + step, :].astype(f32) for n in range(nodes)]
         pressure = [None] * nodes
@@ -280,7 +281,7 @@
                 goal = wanted[j, first : first + step, :].astype(f32)
             else:
                 at = pl.ds(offset + j * step, step)
-                goal = jnp.where(right, after[at, :].astype(f32), before[at, :].astype(f32))
+                goal = jnp.where(near, twin[at, :].astype(f32), border[at, :].astype(f32))
             mixed = scalars[16 * nodes + j : 16 * nodes + j + 1, :] * jnp.tanh(coefficient - goal)
             for n in range(nodes):
                 term = weight[n] * mixed
@@ -383,8 +384,8 @@
     share = rows // nodes
     half = share // 2
     slab = share + half
-    up = [(i, i + 1) for i in range(tiles - 1)]
-    down = [(i + 1, i) for i in range(tiles - 1)]
+    inside = [(i, i ^ 1) for i in range(tiles) if i ^ 1 < tiles]
+    across = [(i, ((i + 1) ^ 1) - 1) for i in range(tiles) if 0 <= ((i + 1) ^ 1) - 1 < tiles]
     wave_hi, wave_lo = (jnp.asarray(w) for w in column_waves(span))
     packed, wanted, fh, fl = call(
         functools.partial(spectrum_kernel, radius),
@@ -403,8 +404,8 @@
             pltpu.SemaphoreType.DMA((3,)),
         ],
     )(node, *kept(freq, mask, target))
-    after = lax.ppermute(packed, "tile", down)
-    before = lax.ppermute(packed, "tile", up)
+    border = lax.ppermute(packed, "tile", across)
+    twin = lax.ppermute(packed, "tile", inside)
     u, cs, gr, gi, wave_hi, wave_lo, scalars = call(
         tables_kernel,
         16,
@@ -443,11 +444,11 @@
             pltpu.VMEM((kernels, 2, 3 * count, 3 * cols), bf16),
             pltpu.VMEM((rows, 2 * cols), f32),
         ],
-    )(tile, scalars, packed, after, before, gr, gi, cs, wave_hi, wave_lo)
+    )(tile, scalars, packed, twin, border, gr, gi, cs, wave_hi, wave_lo)
     images = lax.all_to_all(image, "node", 0, 0)
     (pressure,) = call(
-        functools.partial(middle_kernel, radius, 4 * count), 8, [vmem] * 5, [shape_of(nodes, slab, cols)]
-    )(images, wanted, after, before, scalars)
+        functools.partial(middle_kernel, radius, 4 * count), 8, [smem] + [vmem] * 5, [shape_of(nodes, slab, cols)]
+    )(tile, images, wanted, twin, border, scalars)
     pressure = lax.all_to_all((pressure * 8192.0).astype(jnp.float16), "node", 0, 0).astype(f32) * (1.0 / 8192.0)
     (spread,) = call(
         functools.partial(backward_kernel, radius),

time: 73.9 us -> 75 us (1.015)
  the two profiles are of different devices: /device:TPU:4 before, /device:TPU:112 now
where the time goes in v5:
time: 75 us; the launch traced here: 74.1 us
  blocking collectives  55.5 us (74%)
  Pallas kernels  10.3 us (14%)
  starting transfers between devices  7.48 us (10%)
    all_to_all x1, blocking collectives, local(): images = lax.all_to_all(image, 'node', 0, 0)  28.2 us
    all_to_all x1, blocking collectives, local(): lax.all_to_all(spread.reshape(nodes, share, cols), 'node', 0, 0).sum(0)  14 us
    all_to_all x1, blocking collectives, local(): lax.all_to_all((pressure * 8192.0).astype(jnp.float16), 'node', 0, 0)  13.3 us
    ppermute x1, starting transfers between devices, local(): border = lax.ppermute(packed, 'tile', across)  5.56 us
    pallas_call x1, Pallas kernels, local(): call(functools.partial(backward_kernel, radius), 16, [vmem] * 10, [shape_...  3.22 us
    pallas_call x1, Pallas kernels, local(): call(functools.partial(forward_kernel, radius, tiles), 20, [smem] + [vmem...  2.51 us
    pallas_call x1, Pallas kernels, local(): call(tables_kernel, 16, [smem] + [hbm] * 8, [shape_of(rows, 384, dtype=bf...  2.31 us
    ppermute x1, starting transfers between devices, local(): twin = lax.ppermute(packed, 'tile', inside)  1.92 us
  transfers between devices with their start and end apart: 2, of which 0 were waited for; matrix products, arithmetic and copies ran while one was open for 0% of the time, Pallas kernels for 3%

profile of v5, /device:TPU:112, one launch (start us, length us, event | category | flops | bytes accessed | tf_op | source)
XLA Modules:
  0.0 74.1 jit_solution(5632994744694570724)
XLA Ops:
  0.0 1.5 %shard_map.101 = (bf16[432,128]{1,0:T(8,128)(2,1)S(1)}, bf16[15,32,128]{2,1,0:T(8,128)(2,1)S(1)}, bf16[96,512]{1,0:T(8,128)(2,1)S(1)}, bf16[96,512]{1,0:T(8,128)(2,1)S(1)}) custom-call(s32[1]{0:T(128)} %bitcast.1.node, s32[48]{0:T(128)} %freq_in.3, f32[512,128]{1,0:T(8,128)} %mask_in.1, bf16[15,512,128]{2,1,0:T(8,128)(2,1)} %target_in.1), custom_call_target="tpu_custom_call" | custom-call | tf_op jit(solution)/shard_map/pallas_call | solution.py:390
  1.5 5.6 %collective-permute-start.1 = (bf16[432,128]{1,0:T(8,128)(2,1)S(1)}, bf16[432,128]{1,0:T(8,128)(2,1)S(1)}, u32[]{:S(2)}, u32[]{:S(2)}) collective-permute-start(bf16[432,128]{1,0:T(8,128)(2,1)S(1)} %get-tuple-element.20.packed), channel_id=1, source_target_pairs={{16,32},{32,16},{48,64},{64,48},{80,96},{96,80},{112,128},{128,112... | collective-permute-start | bytes 331784 | tf_op jit(solution)/shard_map/ppermute | solution.py:407
  7.1 1.9 %collective-permute-start = (bf16[432,128]{1,0:T(8,128)(2,1)S(1)}, bf16[432,128]{1,0:T(8,128)(2,1)S(1)}, u32[]{:S(2)}, u32[]{:S(2)}) collective-permute-start(bf16[432,128]{1,0:T(8,128)(2,1)S(1)} %get-tuple-element.20.packed), channel_id=1, source_target_pairs={{0,16},{16,0},{32,48},{48,32},{64,80},{80,64},{96,112},{112,96},{1... | collective-permute-start | bytes 331784 | tf_op jit(solution)/shard_map/ppermute | solution.py:408
  9.0 2.3 %shard_map.100 = (bf16[512,384]{1,0:T(8,128)(2,1)S(1)}, bf16[512,144]{1,0:T(8,128)(2,1)S(1)}, f32[8,48,256]{2,1,0:T(8,128)S(1)}, f32[8,48,256]{2,1,0:T(8,128)S(1...) custom-call(s32[1]{0:T(128)} %bitcast.1.node, s32[48]{0:T(128)} %freq_in.3, ...), custom_call_target="tpu_custom_call" | custom-call | tf_op jit(solution)/shard_map/pallas_call | solution.py:409
  11.3 0.0 collective-permute-done.1.border
  11.3 0.0 collective-permute-done.twin
  11.3 2.5 %shard_map.102 = (bf16[16,48,128]{2,1,0:T(8,128)(2,1)S(1)}, f32[512,256]{1,0:T(8,128)S(1)}, f32[8,512,384]{2,1,0:T(8,128)S(1)}) custom-call(s32[1]{0:T(128)} %bitcast.tile, f32[272,128]{1,0:T(8,128)S(1)} %get-tuple-element.19.scalars, bf16[432,128]{1,0:T(8,128)(2,1)S(1)} %get-tuple-element.20.packed, bf16[432,128]{1,0:T(8,128)(2,1)S(1)} %collective-permute-done.twin, ...), custom_call_target="tpu_custom_call" | custom-call | tf_op jit(solution)/shard_map/pallas_call | solution.py:432
  13.9 28.2 %all_to_all.15.images = bf16[16,48,128]{2,1,0:T(8,128)(2,1)S(1)} all-to-all(bf16[16,48,128]{2,1,0:T(8,128)(2,1)S(1)} %get-tuple-element.26), channel_id=1, replica_groups=mesh['tile'=64,'node'=16] {'node'}, dimensions={0} | all-to-all | bytes 393216 | tf_op jit(solution)/shard_map/all_to_all | solution.py:448
  42.1 0.8 %shard_map.103 = f32[16,48,128]{2,1,0:T(8,128)S(1)} custom-call(s32[1]{0:T(128)} %bitcast.tile, bf16[16,48,128]{2,1,0:T(8,128)(2,1)S(1)} %all_to_all.15.images, bf16[15,32,128]{2,1,0:T(8,128)(2,1)S(1)} %get-tuple-element.27.wanted, bf16[432,128]{1,0:T(8,128)(2,1)S(1)} %collective-permute-done.twin, bf16[432,128]{1,0:T(8,128)(2,1)S(1)} %collective-permute-done.1.border, ...), custom_call_target="tpu_custom_call" | custom-call | tf_op jit(solution)/shard_map/pallas_call | solution.py:449
  42.9 13.3 %all_to_all.16 = f16[16,48,128]{2,1,0:T(8,128)(2,1)S(1)} all-to-all(f16[16,48,128]{2,1,0:T(8,128)(2,1)S(1)} %multiply_convert_fusion), channel_id=1, replica_groups=mesh['tile'=64,'node'=16] {'node'}, dimensions={0} | all-to-all | bytes 393216 | tf_op jit(solution)/shard_map/all_to_all | solution.py:452
  56.3 3.2 %shard_map.104 = f32[512,128]{1,0:T(8,128)S(1)} custom-call(f32[16,48,128]{2,1,0:T(8,128)S(1)} %convert_multiply_fusion.pressure, f32[512,256]{1,0:T(8,128)S(1)} %get-tuple-element.28.slope, f32[8,512,384]{2,1,0:T(8,128)S(1)} %get-tuple-element.29.fields, bf16[96,512]{1,0:T(8,128)(2,1)S(1)} %get-tuple-element.30.fh, ...), custom_call_target="tpu_custom_call" | custom-call | tf_op jit(solution)/shard_map/pallas_call | solution.py:453
  59.5 14.0 %all_to_all.17 = f32[16,32,128]{2,1,0:T(8,128)S(1)} all-to-all(f32[16,32,128]{2,1,0:T(8,128)S(1)} %bitcast.4), channel_id=1, replica_groups=mesh['tile'=64,'node'=16] {'node'}, dimensions={0} | all-to-all | bytes 524288 | tf_op jit(solution)/shard_map/all_to_all | solution.py:464
  73.5 0.6 reduce_sum.9
  (2 shorter events, 0.1 us)
Async XLA Ops:
  1.5 9.8 %collective-permute-start.1 = (bf16[432,128]{1,0:T(8,128)(2,1)S(1)}, bf16[432,128]{1,0:T(8,128)(2,1)S(1)}, u32[]{:S(2)}, u32[]{:S(2)}) collective-permute-start(bf16[432,128]{1,0:T(8,128)(2,1)S(1)} %get-tuple-element.20.packed), channel_id=1, source_target_pairs={{16,32},{32,16},{48,64},{64,48},{80,96},{96,80},{112,128},{128,112... | collective-permute-start | bytes 331784 | tf_op jit(solution)/shard_map/ppermute | solution.py:407
  7.1 4.3 %collective-permute-start = (bf16[432,128]{1,0:T(8,128)(2,1)S(1)}, bf16[432,128]{1,0:T(8,128)(2,1)S(1)}, u32[]{:S(2)}, u32[]{:S(2)}) collective-permute-start(bf16[432,128]{1,0:T(8,128)(2,1)S(1)} %get-tuple-element.20.packed), channel_id=1, source_target_pairs={{0,16},{16,0},{32,48},{48,32},{64,80},{80,64},{96,112},{112,96},{1... | collective-permute-start | bytes 331784 | tf_op jit(solution)/shard_map/ppermute | solution.py:408

commit v6 on v5

--- a/solution.py
+++ b/solution.py
@@ -72,92 +72,49 @@
     return (lane < radius) | ((lane >= half) & (lane < half + radius))
 
 
-def spectrum_kernel(radius, node, freq_in, mask_in, target_in, packed_ref, wanted_ref, fh_ref, fl_ref, freq, mask, raw, sems):
+def first_kernel(
+    radius, node, freq_in, index_in, node_weights_in, chaos_in, target_in, mask_in, wave_hi_in, wave_lo_in, taps_in, weights_in,
+    packed_ref, wanted_ref, fh_ref, fl_ref, freq_ref, scalars_ref, wave_hi, wave_lo, taps, weights,
+    freq, index, node_weights, chaos, raw, mask, sems,
+):
     rows, cols = mask.shape
     count = freq.shape[0]
     terms, share = raw.shape[0], raw.shape[1]
+    nodes = index.shape[1]
     own = node[0]
     mirrored = own >= rows // (2 * share)
     at = jnp.where(mirrored, rows + rows // 2 - share - own * share, own * share)
     at = pl.multiple_of(at, share)
-    moves = [(freq_in, freq), (mask_in, mask), (target_in.at[:, pl.ds(at, share), :], raw)]
-    copies = [pltpu.make_async_copy(source, goal, sems.at[i]) for i, (source, goal) in enumerate(moves)]
-    for copy in copies:
-        copy.start()
-    copies[0].wait()
-    line = lax.broadcasted_iota(jnp.int32, (2 * count, 128), 0)
-    f_freq = jnp.zeros((2 * count, 128), jnp.int32)
-    for i in range(count):
-        f_freq = jnp.where((line == i) | (line == i + count), freq[i], f_freq)
-    f_full = jnp.concatenate([f_freq] * (rows // 128), 1)
-    f_row = lax.broadcasted_iota(jnp.int32, (2 * count, rows), 0)
-    turn = f_full * (2 * lanes((2 * count, rows)) + 1) + jnp.where(f_row >= count, rows // 2, 0)
-    f_parts = parts_of(cosine(turn, 2 * rows))
-    fh_ref[...], fl_ref[...] = f_parts
-    copies[2].wait()
-    row = lax.broadcasted_iota(jnp.int32, (share, share), 0)
-    chosen = jnp.where(mirrored, share - 1 - row, row) == lanes((share, share))
-    order = jnp.where(chosen, 1.0, 0.0).astype(bf16)
-    half = share // 2
-    outer = outer_lanes((half, cols), radius)
-    for j in range(terms):
-        goal = mm(order, raw[j])
-        wanted_ref[j] = goal.astype(bf16)
-        edge = jnp.where(outer, goal[:half], turned(goal[half:]))
-        packed_ref[4 * count + half * j : 4 * count + half * (j + 1), :] = edge.astype(bf16)
-    copies[1].wait()
-    high, low = parts_of(mm3(f_parts, parts_of(mask[...])) * (1.0 / math.sqrt(rows)))
-    packed_ref[0 : 2 * count, :] = high
-    packed_ref[2 * count : 4 * count, :] = low
-
-
-def tables_kernel(
-    node, freq_in, index_in, node_weights_in, chaos_in, weights_in, taps_in, wave_hi_in, wave_lo_in,
-    u_ref, cs_ref, gr_ref, gi_ref, wave_hi, wave_lo, scalars_ref,
-    freq, index, node_weights, chaos, weights, taps, sems,
-):
-    rows = u_ref.shape[0]
-    count = freq.shape[0]
-    kernels, tap_count = taps.shape[1], taps.shape[4]
-    span = wave_hi.shape[0]
-    radius = (tap_count - 1) // 2
-    nodes = index.shape[1]
     moves = [
         (freq_in, freq),
         (index_in, index),
         (node_weights_in, node_weights),
         (chaos_in, chaos),
-        (weights_in, weights),
+        (target_in.at[:, pl.ds(at, share), :], raw),
+        (mask_in, mask),
         (wave_hi_in, wave_hi),
         (wave_lo_in, wave_lo),
         (taps_in, taps),
+        (weights_in, weights),
     ]
     copies = [pltpu.make_async_copy(source, goal, sems.at[i]) for i, (source, goal) in enumerate(moves)]
     for copy in copies:
         copy.start()
     for copy in copies[:4]:
         copy.wait()
+    line = lax.broadcasted_iota(jnp.int32, (2 * count, 128), 0)
+    f_freq = jnp.zeros((2 * count, 128), jnp.int32)
     lane = lanes((8, 256))
     u_freq = jnp.zeros((8, 256), jnp.int32)
     for i in range(count):
+        f_freq = jnp.where((line == i) | (line == i + count), freq[i], f_freq)
         u_freq = jnp.where((lane == i) | (lane == i + count) | (lane == i + 2 * count), freq[i], u_freq)
+    f_full = jnp.concatenate([f_freq] * (rows // 128), 1)
+    f_row = lax.broadcasted_iota(jnp.int32, (2 * count, rows), 0)
     quarter = rows // 2
-    full = jnp.concatenate([u_freq[:, :128]] * (rows // 8), 0)
-    u_lane = lanes((rows, 128))
-    u_y = lax.broadcasted_iota(jnp.int32, (rows, 128), 0)
-    table = cosine(full * (2 * u_y + 1) + jnp.where(u_lane >= count, quarter, 0), 2 * rows)
-    high, low = parts_of(jnp.where(u_lane < 2 * count, table, 0.0))
-    u_ref[:, 0:128] = high
-    u_ref[:, 128:256] = high
-    u_ref[:, 256:384] = low
-    full = jnp.concatenate([u_freq] * (rows // 8), 0)
-    c_row = lax.broadcasted_iota(jnp.int32, (rows, 256), 0)
-    sine = c_row >= rows // 2
-    c_y = jnp.where(sine, c_row - rows // 2, c_row)
-    table = cosine(full * (2 * c_y + 1) - jnp.where(sine, quarter, 0), 2 * rows)
-    high, low = parts_of(table)
-    both = jnp.where(lanes((rows, 256)) < 2 * count, high.astype(f32), low.astype(f32))
-    cs_ref[...] = both[:, : 3 * count].astype(bf16)
+    turn = f_full * (2 * lanes((2 * count, rows)) + 1) + jnp.where(f_row >= count, quarter, 0)
+    f_parts = parts_of(cosine(turn, 2 * rows))
+    fh_ref[...], fl_ref[...] = f_parts
     for n in range(nodes):
         poly = []
         for axis in range(2):
@@ -172,12 +129,64 @@
             if q:
                 value = value * poly[1][q]
             scalars_ref[16 * n + j : 16 * n + j + 1, :] = jnp.full((1, 128), value, f32)
-    dose = 1.0 + 0.1 * (index[1, node[0]].astype(f32) * (2.0 / (LEVELS - 1)) - 1.0)
+    dose = 1.0 + 0.1 * (index[1, own].astype(f32) * (2.0 / (LEVELS - 1)) - 1.0)
     scalars_ref[15:16, :] = jnp.full((1, 128), dose, f32)
     for j in range(len(degrees)):
         scalars_ref[16 * nodes + j : 16 * nodes + j + 1, :] = jnp.full((1, 128), chaos[j], f32)
-    for copy in copies[4:]:
+    freq_ref[...] = u_freq
+    copies[4].wait()
+    row = lax.broadcasted_iota(jnp.int32, (share, share), 0)
+    chosen = jnp.where(mirrored, share - 1 - row, row) == lanes((share, share))
+    order = jnp.where(chosen, 1.0, 0.0).astype(bf16)
+    half = share // 2
+    outer = outer_lanes((half, cols), radius)
+    for j in range(terms):
+        goal = mm(order, raw[j])
+        wanted_ref[j] = goal.astype(bf16)
+        edge = jnp.where(outer, goal[:half], turned(goal[half:]))
+        packed_ref[4 * count + half * j : 4 * count + half * (j + 1), :] = edge.astype(bf16)
+    copies[5].wait()
+    high, low = parts_of(mm3(f_parts, parts_of(mask[...])) * (1.0 / math.sqrt(rows)))
+    packed_ref[0 : 2 * count, :] = high
+    packed_ref[2 * count : 4 * count, :] = low
+    for copy in copies[6:]:
         copy.wait()
+
+
+def taps_kernel(freq, weights, taps, wave_hi, wave_lo, u_ref, cs_ref, gr_ref, gi_ref):
+    kernels, count, span = gr_ref.shape
+    tap_count = taps.shape[4]
+    radius = (tap_count - 1) // 2
+    rows = u_ref.shape[0]
+    quarter = rows // 2
+    steps = lax.broadcasted_iota(jnp.int32, (8, 256), 0)
+
+    def spread_out(frequency, first, lead):
+        width = frequency.shape[1]
+        full = jnp.concatenate([frequency] * (first // 8), 0)
+        turn = full * (2 * lax.broadcasted_iota(jnp.int32, (first, width), 0) + 1) + lead
+        jump = frequency * (2 * first * steps[:, :width])
+        return [cosine(t, 2 * rows) for t in (turn, turn - quarter, jump, jump - quarter)]
+
+    first = rows // 8
+    lane = lanes((first, 128))
+    c, s, step_c, step_s = spread_out(freq[:, :128], first, jnp.where(lane >= count, quarter, 0))
+    for i in range(8):
+        table = c * step_c[i : i + 1, :] - s * step_s[i : i + 1, :]
+        high, low = parts_of(jnp.where(lane < 2 * count, table, 0.0))
+        at = pl.ds(i * first, first)
+        u_ref[at, 0:128] = high
+        u_ref[at, 128:256] = high
+        u_ref[at, 256:384] = low
+    first = rows // 16
+    lane = lanes((first, 256))
+    c, s, step_c, step_s = spread_out(freq[...], first, 0)
+    for i in range(8):
+        by_c, by_s = step_c[i : i + 1, :], step_s[i : i + 1, :]
+        for start, table in ((0, c * by_c - s * by_s), (rows // 2, s * by_c + c * by_s)):
+            high, low = parts_of(table)
+            both = jnp.where(lane < 2 * count, high.astype(f32), low.astype(f32))
+            cs_ref[start + i * first : start + (i + 1) * first, :] = both[:, : 3 * count].astype(bf16)
     side = [jnp.concatenate([w[span - radius : span], w[0 : tap_count - radius]], 0) for w in (wave_hi, wave_lo)]
     scale = jnp.sqrt(weights[...]) * (1.0 / (span * math.sqrt(count)))
     for k in range(kernels):
@@ -351,7 +360,13 @@
     d_im = prod[:count, cols:] + prod[count:, :cols]
     rest = jnp.zeros((128 - 2 * count, cols), f32)
     high, low = parts_of(jnp.concatenate([d_re, d_im, rest], 0))
-    out_ref[...] = mm(u[...], jnp.concatenate([high, low, high], 0)) * (1.0 / math.sqrt(rows))
+    spread = mm(u[...], jnp.concatenate([high, low, high], 0)) * (1.0 / math.sqrt(rows))
+    largest = jnp.max(jnp.abs(spread), axis=0, keepdims=True)
+    power = jnp.ceil(jnp.log2(jnp.maximum(largest, 1e-30)))
+    spread = spread * jnp.exp2(-power)
+    for n in range(nodes):
+        out_ref[n, :share, :] = spread[n * share : (n + 1) * share]
+        out_ref[n, share:, :] = jnp.broadcast_to(power, (out_ref.shape[1] - share, cols))
 
 
 def shape_of(*shape, dtype=f32):
@@ -387,48 +402,45 @@
     inside = [(i, i ^ 1) for i in range(tiles) if i ^ 1 < tiles]
     across = [(i, ((i + 1) ^ 1) - 1) for i in range(tiles) if 0 <= ((i + 1) ^ 1) - 1 < tiles]
     wave_hi, wave_lo = (jnp.asarray(w) for w in column_waves(span))
-    packed, wanted, fh, fl = call(
-        functools.partial(spectrum_kernel, radius),
-        8,
-        [smem] + [hbm] * 3,
+    packed, wanted, fh, fl, turns, scalars, wave_hi, wave_lo, staged, loads = call(
+        functools.partial(first_kernel, radius),
+        16,
+        [smem] + [hbm] * 10,
         [
             shape_of(4 * count + half * terms, cols, dtype=bf16),
             shape_of(terms, share, cols, dtype=bf16),
             shape_of(2 * count, rows, dtype=bf16),
             shape_of(2 * count, rows, dtype=bf16),
+            shape_of(8, 256, dtype=jnp.int32),
+            shape_of(16 * nodes + 16, 128),
+            shape_of(span, 2 * span, dtype=bf16),
+            shape_of(span, 2 * span, dtype=bf16),
+            shape_of(*taps.shape),
+            shape_of(*weights.shape),
         ],
         [
             pltpu.SMEM(freq.shape, jnp.int32),
+            pltpu.SMEM((2, nodes), jnp.int32),
+            pltpu.SMEM((nodes,), f32),
+            pltpu.SMEM(chaos.shape, f32),
+            pltpu.VMEM((terms, share, cols), bf16),
             pltpu.VMEM(mask.shape, f32),
-            pltpu.VMEM((terms, share, cols), bf16),
-            pltpu.SemaphoreType.DMA((3,)),
-        ],
-    )(node, *kept(freq, mask, target))
+            pltpu.SemaphoreType.DMA((10,)),
+        ],
+    )(node, *kept(freq, node_index.T, node_weights, chaos, target, mask, wave_hi, wave_lo, taps, weights))
     border = lax.ppermute(packed, "tile", across)
     twin = lax.ppermute(packed, "tile", inside)
-    u, cs, gr, gi, wave_hi, wave_lo, scalars = call(
-        tables_kernel,
-        16,
-        [smem] + [hbm] * 8,
+    u, cs, gr, gi = call(
+        taps_kernel,
+        8,
+        [vmem] * 5,
         [
             shape_of(rows, 384, dtype=bf16),
             shape_of(rows, 3 * count, dtype=bf16),
             shape_of(kernels, count, span),
             shape_of(kernels, count, span),
-            shape_of(span, 2 * span, dtype=bf16),
-            shape_of(span, 2 * span, dtype=bf16),
-            shape_of(16 * nodes + 16, 128),
-        ],
-        [
-            pltpu.SMEM(freq.shape, jnp.int32),
-            pltpu.SMEM((2, nodes), jnp.int32),
-            pltpu.SMEM((nodes,), f32),
-            pltpu.SMEM(chaos.shape, f32),
-            pltpu.VMEM(weights.shape, f32),
-            pltpu.VMEM(taps.shape, f32),
-            pltpu.SemaphoreType.DMA((8,)),
-        ],
-    )(node, *kept(freq, node_index.T, node_weights, chaos, weights, taps, wave_hi, wave_lo))
+        ],
+    )(turns, loads, staged, wave_hi, wave_lo)
     image, slope, fields = call(
         functools.partial(forward_kernel, radius, tiles),
         20,
@@ -454,14 +466,15 @@
         functools.partial(backward_kernel, radius),
         16,
         [vmem] * 10,
-        [shape_of(rows, cols)],
+        [shape_of(nodes, share + 8, cols)],
         [
             pltpu.VMEM((2 * kernels * count, span), bf16),
             pltpu.VMEM((2 * kernels * count, span), bf16),
             pltpu.VMEM((rows, 2 * cols), f32),
         ],
     )(pressure, slope, fields, fh, fl, gr, gi, u, wave_hi, wave_lo)
-    return lax.all_to_all(spread.reshape(nodes, share, cols), "node", 0, 0).sum(0)
+    spread = lax.all_to_all(spread.astype(jnp.float16), "node", 0, 0).astype(f32)
+    return (spread[:, :share] * jnp.exp2(spread[:, share : share + 1])).sum(0)
 
 
 def solution(mesh):

time: 75 us -> 72.8 us (0.971)
  blocking collectives: 55.5 us -> 52.8 us
  waiting for transfers between devices: 0.01 us -> 1.38 us
  Pallas kernels: 10.3 us -> 9.14 us
    pallas_call x2, Pallas kernels: 3.79 us -> 2.42 us  [the longest x1 1.72 us: local(): call(functools.partial(first_kernel, radius), 16, [smem] + [hbm] * 10, [s...]
    ppermute x1, waiting for transfers between devices: 0.01 us -> 1.38 us  [local(): border = lax.ppermute(packed, 'tile', across)]
    all_to_all x1, blocking collectives: 28.2 us -> 26.8 us  [local(): images = lax.all_to_all(image, 'node', 0, 0)]
    all_to_all x1, blocking collectives: 14 us -> 12.9 us  [local(): lax.all_to_all(spread.astype(jnp.float16), 'node', 0, 0).astype(f32)]
  transfers between devices with their start and end apart: 2 -> 2, of which waited for: 0 -> 1; matrix products, arithmetic and copies ran while one was open for 0% -> 0% of each run, Pallas kernels for 3% -> 1%
where the time goes in v6:
time: 72.8 us; the launch traced here: 71.7 us
  blocking collectives  52.8 us (73%)
  Pallas kernels  9.14 us (13%)
  starting transfers between devices  7.48 us (10%)
  waiting for transfers between devices  1.38 us (2%)
  other arithmetic  0.78 us (1%)
    all_to_all x1, blocking collectives, local(): images = lax.all_to_all(image, 'node', 0, 0)  26.8 us
    all_to_all x1, blocking collectives, local(): lax.all_to_all((pressure * 8192.0).astype(jnp.float16), 'node', 0, 0)  13.1 us
    all_to_all x1, blocking collectives, local(): lax.all_to_all(spread.astype(jnp.float16), 'node', 0, 0).astype(f32)  12.9 us
    ppermute x1, starting transfers between devices, local(): border = lax.ppermute(packed, 'tile', across)  5.56 us
    pallas_call x1, Pallas kernels, local(): call(functools.partial(backward_kernel, radius), 16, [vmem] * 10, [shape_...  3.31 us
    pallas_call x1, Pallas kernels, local(): call(functools.partial(forward_kernel, radius, tiles), 20, [smem] + [vmem...  2.59 us
    ppermute x1, starting transfers between devices, local(): twin = lax.ppermute(packed, 'tile', inside)  1.92 us
    pallas_call x1, Pallas kernels, local(): call(functools.partial(first_kernel, radius), 16, [smem] + [hbm] * 10, [s...  1.72 us
  transfers between devices with their start and end apart: 2, of which 1 were waited for; matrix products, arithmetic and copies ran while one was open for 0% of the time, Pallas kernels for 1%

profile of v6, /device:TPU:112, one launch (start us, length us, event | category | flops | bytes accessed | tf_op | source)
XLA Modules:
  0.0 71.7 jit_solution(337814516314457261)
XLA Ops:
  0.0 1.7 %shard_map.100 = (bf16[432,128]{1,0:T(8,128)(2,1)S(1)}, bf16[15,32,128]{2,1,0:T(8,128)(2,1)S(1)}, bf16[96,512]{1,0:T(8,128)(2,1)S(1)}, bf16[96,512]{1,0:T(8,128)...) custom-call(s32[1]{0:T(128)} %bitcast.1.node, ...), custom_call_target="tpu_custom_call" | custom-call | tf_op jit(solution)/shard_map/pallas_call | solution.py:405
  1.7 5.6 %collective-permute-start.1 = (bf16[432,128]{1,0:T(8,128)(2,1)S(1)}, bf16[432,128]{1,0:T(8,128)(2,1)S(1)}, u32[]{:S(2)}, u32[]{:S(2)}) collective-permute-start(bf16[432,128]{1,0:T(8,128)(2,1)S(1)} %get-tuple-element.23.packed), channel_id=1, source_target_pairs={{16,32},{32,16},{48,64},{64,48},{80,96},{96,80},{112,128},{128,112... | collective-permute-start | bytes 331784 | tf_op jit(solution)/shard_map/ppermute | solution.py:431
  7.3 1.9 %collective-permute-start = (bf16[432,128]{1,0:T(8,128)(2,1)S(1)}, bf16[432,128]{1,0:T(8,128)(2,1)S(1)}, u32[]{:S(2)}, u32[]{:S(2)}) collective-permute-start(bf16[432,128]{1,0:T(8,128)(2,1)S(1)} %get-tuple-element.23.packed), channel_id=1, source_target_pairs={{0,16},{16,0},{32,48},{48,32},{64,80},{80,64},{96,112},{112,96},{1... | collective-permute-start | bytes 331784 | tf_op jit(solution)/shard_map/ppermute | solution.py:432
  9.2 0.7 shard_map.101
  9.9 1.4 %collective-permute-done.1.border = bf16[432,128]{1,0:T(8,128)(2,1)S(1)} collective-permute-done((bf16[432,128]{1,0:T(8,128)(2,1)S(1)}, bf16[432,128]{1,0:T(8,128)(2,1)S(1)}, u32[]{:S(2)}, u32[]{:S(2)}) %collective-permute-start.1) | collective-permute-done | bytes 110624 | tf_op jit(solution)/shard_map/ppermute | solution.py:431
  11.3 0.0 collective-permute-done.twin
  11.3 2.6 %shard_map.102 = (bf16[16,48,128]{2,1,0:T(8,128)(2,1)S(1)}, f32[512,256]{1,0:T(8,128)S(1)}, f32[8,512,384]{2,1,0:T(8,128)S(1)}) custom-call(s32[1]{0:T(128)} %bitcast.tile, f32[272,128]{1,0:T(8,128)S(1)} %get-tuple-element.22.scalars, bf16[432,128]{1,0:T(8,128)(2,1)S(1)} %get-tuple-element.23.packed, bf16[432,128]{1,0:T(8,128)(2,1)S(1)} %collective-permute-done.twin, ...), custom_call_target="tpu_custom_call" | custom-call | tf_op jit(solution)/shard_map/pallas_call | solution.py:444
  13.9 26.8 %all_to_all.15.images = bf16[16,48,128]{2,1,0:T(8,128)(2,1)S(1)} all-to-all(bf16[16,48,128]{2,1,0:T(8,128)(2,1)S(1)} %get-tuple-element.32), channel_id=1, replica_groups=mesh['tile'=64,'node'=16] {'node'}, dimensions={0} | all-to-all | bytes 393216 | tf_op jit(solution)/shard_map/all_to_all | solution.py:460
  40.8 0.8 %shard_map.103 = f32[16,48,128]{2,1,0:T(8,128)S(1)} custom-call(s32[1]{0:T(128)} %bitcast.tile, bf16[16,48,128]{2,1,0:T(8,128)(2,1)S(1)} %all_to_all.15.images, bf16[15,32,128]{2,1,0:T(8,128)(2,1)S(1)} %get-tuple-element.33.wanted, bf16[432,128]{1,0:T(8,128)(2,1)S(1)} %collective-permute-done.twin, bf16[432,128]{1,0:T(8,128)(2,1)S(1)} %collective-permute-done.1.border, ...), custom_call_target="tpu_custom_call" | custom-call | tf_op jit(solution)/shard_map/pallas_call | solution.py:461
  41.6 13.1 %all_to_all.16 = f16[16,48,128]{2,1,0:T(8,128)(2,1)S(1)} all-to-all(f16[16,48,128]{2,1,0:T(8,128)(2,1)S(1)} %multiply_convert_fusion), channel_id=1, replica_groups=mesh['tile'=64,'node'=16] {'node'}, dimensions={0} | all-to-all | bytes 393216 | tf_op jit(solution)/shard_map/all_to_all | solution.py:464
  54.8 3.3 %shard_map.104 = f32[16,40,128]{2,1,0:T(8,128)S(1)} custom-call(f32[16,48,128]{2,1,0:T(8,128)S(1)} %convert_multiply_fusion.pressure, f32[512,256]{1,0:T(8,128)S(1)} %get-tuple-element.34.slope, f32[8,512,384]{2,1,0:T(8,128)S(1)} %get-tuple-element.35.fields, bf16[96,512]{1,0:T(8,128)(2,1)S(1)} %get-tuple-element.36.fh, ...), custom_call_target="tpu_custom_call" | custom-call | tf_op jit(solution)/shard_map/pallas_call | solution.py:465
  58.1 12.9 %all_to_all.17 = f16[16,40,128]{2,1,0:T(8,128)(2,1)S(1)} all-to-all(f16[16,40,128]{2,1,0:T(8,128)(2,1)S(1)} %convert_element_type.14), channel_id=1, replica_groups=mesh['tile'=64,'node'=16] {'node'}, dimensions={0} | all-to-all | bytes 327680 | tf_op jit(solution)/shard_map/all_to_all | solution.py:476
  71.1 0.6 fusion
  (5 shorter events, 0.1 us)
Async XLA Ops:
  1.7 9.6 %collective-permute-start.1 = (bf16[432,128]{1,0:T(8,128)(2,1)S(1)}, bf16[432,128]{1,0:T(8,128)(2,1)S(1)}, u32[]{:S(2)}, u32[]{:S(2)}) collective-permute-start(bf16[432,128]{1,0:T(8,128)(2,1)S(1)} %get-tuple-element.23.packed), channel_id=1, source_target_pairs={{16,32},{32,16},{48,64},{64,48},{80,96},{96,80},{112,128},{128,112... | collective-permute-start | bytes 331784 | tf_op jit(solution)/shard_map/ppermute | solution.py:431
  7.3 4.0 %collective-permute-start = (bf16[432,128]{1,0:T(8,128)(2,1)S(1)}, bf16[432,128]{1,0:T(8,128)(2,1)S(1)}, u32[]{:S(2)}, u32[]{:S(2)}) collective-permute-start(bf16[432,128]{1,0:T(8,128)(2,1)S(1)} %get-tuple-element.23.packed), channel_id=1, source_target_pairs={{0,16},{16,0},{32,48},{48,32},{64,80},{80,64},{96,112},{112,96},{1... | collective-permute-start | bytes 331784 | tf_op jit(solution)/shard_map/ppermute | solution.py:432

commit v7 on v5

--- a/solution.py
+++ b/solution.py
@@ -138,26 +138,38 @@
     for copy in copies[:4]:
         copy.wait()
     lane = lanes((8, 256))
-    u_freq = jnp.zeros((8, 256), jnp.int32)
+    turns = jnp.zeros((8, 256), jnp.int32)
     for i in range(count):
-        u_freq = jnp.where((lane == i) | (lane == i + count) | (lane == i + 2 * count), freq[i], u_freq)
+        turns = jnp.where((lane == i) | (lane == i + count) | (lane == i + 2 * count), freq[i], turns)
     quarter = rows // 2
-    full = jnp.concatenate([u_freq[:, :128]] * (rows // 8), 0)
-    u_lane = lanes((rows, 128))
-    u_y = lax.broadcasted_iota(jnp.int32, (rows, 128), 0)
-    table = cosine(full * (2 * u_y + 1) + jnp.where(u_lane >= count, quarter, 0), 2 * rows)
-    high, low = parts_of(jnp.where(u_lane < 2 * count, table, 0.0))
-    u_ref[:, 0:128] = high
-    u_ref[:, 128:256] = high
-    u_ref[:, 256:384] = low
-    full = jnp.concatenate([u_freq] * (rows // 8), 0)
-    c_row = lax.broadcasted_iota(jnp.int32, (rows, 256), 0)
-    sine = c_row >= rows // 2
-    c_y = jnp.where(sine, c_row - rows // 2, c_row)
-    table = cosine(full * (2 * c_y + 1) - jnp.where(sine, quarter, 0), 2 * rows)
-    high, low = parts_of(table)
-    both = jnp.where(lanes((rows, 256)) < 2 * count, high.astype(f32), low.astype(f32))
-    cs_ref[...] = both[:, : 3 * count].astype(bf16)
+    steps = lax.broadcasted_iota(jnp.int32, (8, 256), 0)
+
+    def spread_out(frequency, first, lead):
+        width = frequency.shape[1]
+        full = jnp.concatenate([frequency] * (first // 8), 0)
+        turn = full * (2 * lax.broadcasted_iota(jnp.int32, (first, width), 0) + 1) + lead
+        jump = frequency * (2 * first * steps[:, :width])
+        return [cosine(t, 2 * rows) for t in (turn, turn - quarter, jump, jump - quarter)]
+
+    first = rows // 8
+    lane = lanes((first, 128))
+    c, s, step_c, step_s = spread_out(turns[:, :128], first, jnp.where(lane >= count, quarter, 0))
+    for i in range(8):
+        table = c * step_c[i : i + 1, :] - s * step_s[i : i + 1, :]
+        high, low = parts_of(jnp.where(lane < 2 * count, table, 0.0))
+        at = pl.ds(i * first, first)
+        u_ref[at, 0:128] = high
+        u_ref[at, 128:256] = high
+        u_ref[at, 256:384] = low
+    first = rows // 16
+    lane = lanes((first, 256))
+    c, s, step_c, step_s = spread_out(turns, first, 0)
+    for i in range(8):
+        by_c, by_s = step_c[i : i + 1, :], step_s[i : i + 1, :]
+        for start, table in ((0, c * by_c - s * by_s), (rows // 2, s * by_c + c * by_s)):
+            high, low = parts_of(table)
+            both = jnp.where(lane < 2 * count, high.astype(f32), low.astype(f32))
+            cs_ref[start + i * first : start + (i + 1) * first, :] = both[:, : 3 * count].astype(bf16)
     for n in range(nodes):
         poly = []
         for axis in range(2):
@@ -228,20 +240,24 @@
         crossed = jnp.concatenate([im[:, :cols], -re[:, :cols], cross], 1)
         for d, value in ((0, straight), (1, crossed)):
             high, low = parts_of(value)
+            at = 3 * cols * (k % 2)
             for place, part in ((0, high), (1, low), (2, high)):
-                x[k, d, place * count : (place + 1) * count, :] = part
-    total[...] = jnp.zeros(total.shape, f32)
-
-    @pl.loop(0, kernels, unroll=True)
-    def _(k):
-        even = mm(cs[: rows // 2, :], x[k, 0])
-        odd = mm(cs[rows // 2 :, :], x[k, 1])
-        for first, field in ((0, even - odd), (rows // 2, even + odd)):
+                x[k // 2, d, place * count : (place + 1) * count, at : at + 3 * cols] = part
+    for pair in range(kernels // 2):
+        even_part = mm(cs[: rows // 2, :], x[pair, 0])
+        odd_part = mm(cs[rows // 2 :, :], x[pair, 1])
+        for first, field in ((0, even_part - odd_part), (rows // 2, even_part + odd_part)):
             at = pl.ds(first, rows // 2)
-            fields_ref[k, at, :] = field
+            fields_ref[2 * pair, at, :] = field[:, : 3 * cols]
+            fields_ref[2 * pair + 1, at, :] = field[:, 3 * cols :]
             square = field * field
-            total[at, :cols] += square[:, :cols] + square[:, cols : 2 * cols]
-            total[at, cols:] += square[:, 2 * cols :]
+            inner = square[:, :cols] + square[:, cols : 2 * cols]
+            inner = inner + (square[:, 3 * cols : 4 * cols] + square[:, 4 * cols : 5 * cols])
+            edge = square[:, 2 * cols : 3 * cols] + square[:, 5 * cols :]
+            if pair:
+                inner, edge = inner + total[at, :cols], edge + total[at, cols:]
+            total[at, :cols] = inner
+            total[at, cols:] = edge
 
     value = scalars[15:16, :]
     inner = total[:, :cols]
@@ -310,28 +326,28 @@
         table.append(jnp.concatenate([fh[first : first + count, : rows // 2], fl[first : first + count, : rows // 2]], 0))
     outer = outer_lanes((count, cols), radius)
 
-    @pl.loop(0, kernels, unroll=True)
-    def _(k):
+    for pair in range(0, kernels, 2):
         halves = []
         for first in (0, rows // 2):
             at = pl.ds(first, rows // 2)
             inner, edge = scale[at, :cols], scale[at, cols:]
-            halves.append(fields[k, at, :] * jnp.concatenate([inner, inner, edge], 1))
+            both = jnp.concatenate([fields[pair, at, :], fields[pair + 1, at, :]], 1)
+            halves.append(both * jnp.concatenate([inner, inner, edge] * 2, 1))
         grads = []
         for lhs, value in zip(table, (halves[0] + halves[1], halves[0] - halves[1])):
             high, low = parts_of(value)
             prod = mm(lhs, high)
             grads.append(prod[:count] + prod[count:] + mm(lhs[:count], low))
-        straight, crossed = grads
-        edge, cross = straight[:, 2 * cols :], crossed[:, 2 * cols :]
-        re_edge = jnp.where(outer, edge - turned(cross), 0.0)
-        im_edge = jnp.where(outer, cross + turned(edge), 0.0)
-        re = jnp.concatenate([straight[:, :cols] - crossed[:, cols : 2 * cols], re_edge], 1)
-        im = jnp.concatenate([straight[:, cols : 2 * cols] + crossed[:, :cols], im_edge], 1)
-        at = pl.multiple_of(2 * k * count, 2 * count)
-        dh[pl.ds(at, count), :], dl[pl.ds(at, count), :] = parts_of(re)
-        at = pl.multiple_of(at + count, count)
-        dh[pl.ds(at, count), :], dl[pl.ds(at, count), :] = parts_of(im)
+        for k in (pair, pair + 1):
+            straight, crossed = (g[:, 3 * cols * (k - pair) : 3 * cols * (k - pair + 1)] for g in grads)
+            edge, cross = straight[:, 2 * cols :], crossed[:, 2 * cols :]
+            re_edge = jnp.where(outer, edge - turned(cross), 0.0)
+            im_edge = jnp.where(outer, cross + turned(edge), 0.0)
+            re = jnp.concatenate([straight[:, :cols] - crossed[:, cols : 2 * cols], re_edge], 1)
+            im = jnp.concatenate([straight[:, cols : 2 * cols] + crossed[:, :cols], im_edge], 1)
+            for d, value in ((0, re), (1, im)):
+                at = pl.ds((2 * k + d) * count, count)
+                dh[at, :], dl[at, :] = parts_of(value)
 
     wave = (wave_hi[...], wave_lo[...])
     a_re = jnp.zeros((count, span), f32)
@@ -351,7 +367,13 @@
     d_im = prod[:count, cols:] + prod[count:, :cols]
     rest = jnp.zeros((128 - 2 * count, cols), f32)
     high, low = parts_of(jnp.concatenate([d_re, d_im, rest], 0))
-    out_ref[...] = mm(u[...], jnp.concatenate([high, low, high], 0)) * (1.0 / math.sqrt(rows))
+    spread = mm(u[...], jnp.concatenate([high, low, high], 0)) * (1.0 / math.sqrt(rows))
+    largest = jnp.max(jnp.abs(spread), axis=0, keepdims=True)
+    power = jnp.ceil(jnp.log2(jnp.maximum(largest, 1e-30)))
+    spread = spread * jnp.exp2(-power)
+    for n in range(nodes):
+        out_ref[n, :share, :] = spread[n * share : (n + 1) * share]
+        out_ref[n, share:, :] = jnp.broadcast_to(power, (out_ref.shape[1] - share, cols))
 
 
 def shape_of(*shape, dtype=f32):
@@ -405,7 +427,6 @@
         ],
     )(node, *kept(freq, mask, target))
     border = lax.ppermute(packed, "tile", across)
-    twin = lax.ppermute(packed, "tile", inside)
     u, cs, gr, gi, wave_hi, wave_lo, scalars = call(
         tables_kernel,
         16,
@@ -429,6 +450,8 @@
             pltpu.SemaphoreType.DMA((8,)),
         ],
     )(node, *kept(freq, node_index.T, node_weights, chaos, weights, taps, wave_hi, wave_lo))
+    ready, scalars = lax.optimization_barrier((packed, scalars))
+    twin = lax.ppermute(ready, "tile", inside)
     image, slope, fields = call(
         functools.partial(forward_kernel, radius, tiles),
         20,
@@ -441,7 +464,7 @@
         [
             pltpu.VMEM((2 * kernels * count, span), bf16),
             pltpu.VMEM((2 * kernels * count, span), bf16),
-            pltpu.VMEM((kernels, 2, 3 * count, 3 * cols), bf16),
+            pltpu.VMEM((kernels // 2, 2, 3 * count, 6 * cols), bf16),
             pltpu.VMEM((rows, 2 * cols), f32),
         ],
     )(tile, scalars, packed, twin, border, gr, gi, cs, wave_hi, wave_lo)
@@ -454,14 +477,15 @@
         functools.partial(backward_kernel, radius),
         16,
         [vmem] * 10,
-        [shape_of(rows, cols)],
+        [shape_of(nodes, share + 8, cols)],
         [
             pltpu.VMEM((2 * kernels * count, span), bf16),
             pltpu.VMEM((2 * kernels * count, span), bf16),
             pltpu.VMEM((rows, 2 * cols), f32),
         ],
     )(pressure, slope, fields, fh, fl, gr, gi, u, wave_hi, wave_lo)
-    return lax.all_to_all(spread.reshape(nodes, share, cols), "node", 0, 0).sum(0)
+    spread = lax.all_to_all(spread.astype(jnp.float16), "node", 0, 0).astype(f32)
+    return (spread[:, :share] * jnp.exp2(spread[:, share : share + 1])).sum(0)
 
 
 def solution(mesh):

time: 75 us -> 73.2 us (0.976)
  blocking collectives: 55.5 us -> 53.6 us
  waiting for transfers between devices: 0.01 us -> 1.28 us
    all_to_all x1, blocking collectives: 14 us -> 12.5 us  [local(): lax.all_to_all(spread.astype(jnp.float16), 'node', 0, 0).astype(f32)]
    ppermute x1, waiting for transfers between devices: 0.01 us -> 1.03 us  [local(): twin = lax.ppermute(ready, 'tile', inside)]
  transfers between devices with their start and end apart: 2 -> 2, of which waited for: 0 -> 2; matrix products, arithmetic and copies ran while one was open for 0% -> 0% of each run, Pallas kernels for 3% -> 3%
where the time goes in v7:
time: 73.2 us; the launch traced here: 72.9 us
  blocking collectives  53.6 us (73%)
  Pallas kernels  9.66 us (13%)
  starting transfers between devices  7.48 us (10%)
  waiting for transfers between devices  1.28 us (2%)
  other arithmetic  0.78 us (1%)
    all_to_all x1, blocking collectives, local(): images = lax.all_to_all(image, 'node', 0, 0)  27.9 us
    all_to_all x1, blocking collectives, local(): lax.all_to_all((pressure * 8192.0).astype(jnp.float16), 'node', 0, 0)  13.2 us
    all_to_all x1, blocking collectives, local(): lax.all_to_all(spread.astype(jnp.float16), 'node', 0, 0).astype(f32)  12.5 us
    ppermute x1, starting transfers between devices, local(): border = lax.ppermute(packed, 'tile', across)  5.56 us
    pallas_call x1, Pallas kernels, local(): call(functools.partial(backward_kernel, radius), 16, [vmem] * 10, [shape_...  3.13 us
    pallas_call x1, Pallas kernels, local(): call(functools.partial(forward_kernel, radius, tiles), 20, [smem] + [vmem...  2.4 us
    ppermute x1, starting transfers between devices, local(): twin = lax.ppermute(ready, 'tile', inside)  1.92 us
    pallas_call x1, Pallas kernels, local(): call(tables_kernel, 16, [smem] + [hbm] * 8, [shape_of(rows, 384, dtype=bf...  1.83 us
  transfers between devices with their start and end apart: 2, of which 2 were waited for; matrix products, arithmetic and copies ran while one was open for 0% of the time, Pallas kernels for 3%

profile of v7, /device:TPU:112, one launch (start us, length us, event | category | flops | bytes accessed | tf_op | source)
XLA Modules:
  0.0 72.9 jit_solution(7785628788508242649)
XLA Ops:
  0.0 1.5 %shard_map.100 = (bf16[432,128]{1,0:T(8,128)(2,1)S(1)}, bf16[15,32,128]{2,1,0:T(8,128)(2,1)S(1)}, bf16[96,512]{1,0:T(8,128)(2,1)S(1)}, bf16[96,512]{1,0:T(8,128)(2,1)S(1)}) custom-call(s32[1]{0:T(128)} %bitcast.1.node, s32[48]{0:T(128)} %freq_in.3, f32[512,128]{1,0:T(8,128)} %mask_in.1, bf16[15,512,128]{2,1,0:T(8,128)(2,1)} %target_in.1), custom_call_target="tpu_custom_call" | custom-call | tf_op jit(solution)/shard_map/pallas_call | solution.py:412
  1.5 5.6 %collective-permute-start.1 = (bf16[432,128]{1,0:T(8,128)(2,1)S(1)}, bf16[432,128]{1,0:T(8,128)(2,1)S(1)}, u32[]{:S(2)}, u32[]{:S(2)}) collective-permute-start(bf16[432,128]{1,0:T(8,128)(2,1)S(1)} %get-tuple-element.24.packed), channel_id=1, source_target_pairs={{16,32},{32,16},{48,64},{64,48},{80,96},{96,80},{112,128},{128,112... | collective-permute-start | bytes 331784 | tf_op jit(solution)/shard_map/ppermute | solution.py:429
  7.1 1.8 %shard_map.101 = (bf16[512,384]{1,0:T(8,128)(2,1)S(1)}, bf16[512,144]{1,0:T(8,128)(2,1)S(1)}, f32[8,48,256]{2,1,0:T(8,128)S(1)}, f32[8,48,256]{2,1,0:T(8,128)S(1...) custom-call(s32[1]{0:T(128)} %bitcast.1.node, s32[48]{0:T(128)} %freq_in.3, ...), custom_call_target="tpu_custom_call" | custom-call | tf_op jit(solution)/shard_map/pallas_call | solution.py:430
  8.9 1.9 %collective-permute-start = (bf16[432,128]{1,0:T(8,128)(2,1)S(1)}, bf16[432,128]{1,0:T(8,128)(2,1)S(1)}, u32[]{:S(2)}, u32[]{:S(2)}) collective-permute-start(bf16[432,128]{1,0:T(8,128)(2,1)S(1)} %get-tuple-element.24.packed), channel_id=1, source_target_pairs={{0,16},{16,0},{32,48},{48,32},{64,80},{80,64},{96,112},{112,96},{1... | collective-permute-start | bytes 331784 | tf_op jit(solution)/shard_map/ppermute | solution.py:454
  10.8 0.2 collective-permute-done.1.border
  11.1 1.0 %collective-permute-done.twin = bf16[432,128]{1,0:T(8,128)(2,1)S(1)} collective-permute-done((bf16[432,128]{1,0:T(8,128)(2,1)S(1)}, bf16[432,128]{1,0:T(8,128)(2,1)S(1)}, u32[]{:S(2)}, u32[]{:S(2)}) %collective-permute-start) | collective-permute-done | bytes 110624 | tf_op jit(solution)/shard_map/ppermute | solution.py:454
  12.1 2.4 %shard_map.102 = (bf16[16,48,128]{2,1,0:T(8,128)(2,1)S(1)}, f32[512,256]{1,0:T(8,128)S(1)}, f32[8,512,384]{2,1,0:T(8,128)S(1)}) custom-call(s32[1]{0:T(128)} %bitcast.tile, f32[272,128]{1,0:T(8,128)S(1)} %get-tuple-element.23.scalars, bf16[432,128]{1,0:T(8,128)(2,1)S(1)} %get-tuple-element.24.packed, bf16[432,128]{1,0:T(8,128)(2,1)S(1)} %collective-permute-done.twin, ...), custom_call_target="tpu_custom_call" | custom-call | tf_op jit(solution)/shard_map/pallas_call | solution.py:455
  14.5 27.9 %all_to_all.15.images = bf16[16,48,128]{2,1,0:T(8,128)(2,1)S(1)} all-to-all(bf16[16,48,128]{2,1,0:T(8,128)(2,1)S(1)} %get-tuple-element.30), channel_id=1, replica_groups=mesh['tile'=64,'node'=16] {'node'}, dimensions={0} | all-to-all | bytes 393216 | tf_op jit(solution)/shard_map/all_to_all | solution.py:471
  42.4 0.8 %shard_map.103 = f32[16,48,128]{2,1,0:T(8,128)S(1)} custom-call(s32[1]{0:T(128)} %bitcast.tile, bf16[16,48,128]{2,1,0:T(8,128)(2,1)S(1)} %all_to_all.15.images, bf16[15,32,128]{2,1,0:T(8,128)(2,1)S(1)} %get-tuple-element.31.wanted, bf16[432,128]{1,0:T(8,128)(2,1)S(1)} %collective-permute-done.twin, bf16[432,128]{1,0:T(8,128)(2,1)S(1)} %collective-permute-done.1.border, ...), custom_call_target="tpu_custom_call" | custom-call | tf_op jit(solution)/shard_map/pallas_call | solution.py:472
  43.3 13.2 %all_to_all.16 = f16[16,48,128]{2,1,0:T(8,128)(2,1)S(1)} all-to-all(f16[16,48,128]{2,1,0:T(8,128)(2,1)S(1)} %multiply_convert_fusion), channel_id=1, replica_groups=mesh['tile'=64,'node'=16] {'node'}, dimensions={0} | all-to-all | bytes 393216 | tf_op jit(solution)/shard_map/all_to_all | solution.py:475
  56.6 3.1 %shard_map.104 = f32[16,40,128]{2,1,0:T(8,128)S(1)} custom-call(f32[16,48,128]{2,1,0:T(8,128)S(1)} %convert_multiply_fusion.pressure, f32[512,256]{1,0:T(8,128)S(1)} %get-tuple-element.32.slope, f32[8,512,384]{2,1,0:T(8,128)S(1)} %get-tuple-element.33.fields, bf16[96,512]{1,0:T(8,128)(2,1)S(1)} %get-tuple-element.34.fh, ...), custom_call_target="tpu_custom_call" | custom-call | tf_op jit(solution)/shard_map/pallas_call | solution.py:476
  59.7 12.5 %all_to_all.17 = f16[16,40,128]{2,1,0:T(8,128)(2,1)S(1)} all-to-all(f16[16,40,128]{2,1,0:T(8,128)(2,1)S(1)} %convert_element_type.14), channel_id=1, replica_groups=mesh['tile'=64,'node'=16] {'node'}, dimensions={0} | all-to-all | bytes 327680 | tf_op jit(solution)/shard_map/all_to_all | solution.py:487
  72.3 0.6 fusion
  (5 shorter events, 0.1 us)
Async XLA Ops:
  1.5 9.6 %collective-permute-start.1 = (bf16[432,128]{1,0:T(8,128)(2,1)S(1)}, bf16[432,128]{1,0:T(8,128)(2,1)S(1)}, u32[]{:S(2)}, u32[]{:S(2)}) collective-permute-start(bf16[432,128]{1,0:T(8,128)(2,1)S(1)} %get-tuple-element.24.packed), channel_id=1, source_target_pairs={{16,32},{32,16},{48,64},{64,48},{80,96},{96,80},{112,128},{128,112... | collective-permute-start | bytes 331784 | tf_op jit(solution)/shard_map/ppermute | solution.py:429
  8.9 3.2 %collective-permute-start = (bf16[432,128]{1,0:T(8,128)(2,1)S(1)}, bf16[432,128]{1,0:T(8,128)(2,1)S(1)}, u32[]{:S(2)}, u32[]{:S(2)}) collective-permute-start(bf16[432,128]{1,0:T(8,128)(2,1)S(1)} %get-tuple-element.24.packed), channel_id=1, source_target_pairs={{0,16},{16,0},{32,48},{48,32},{64,80},{80,64},{96,112},{112,96},{1... | collective-permute-start | bytes 331784 | tf_op jit(solution)/shard_map/ppermute | solution.py:454

commit v8 on v7

--- a/solution.py
+++ b/solution.py
@@ -72,7 +72,10 @@
     return (lane < radius) | ((lane >= half) & (lane < half + radius))
 
 
-def spectrum_kernel(radius, node, freq_in, mask_in, target_in, packed_ref, wanted_ref, fh_ref, fl_ref, freq, mask, raw, sems):
+def spectrum_kernel(
+    radius, node, freq_in, mask_in, target_in, taps_in, wave_hi_in, wave_lo_in,
+    packed_ref, wanted_ref, fh_ref, fl_ref, taps, wave_hi, wave_lo, turns_ref, freq, mask, raw, sems,
+):
     rows, cols = mask.shape
     count = freq.shape[0]
     terms, share = raw.shape[0], raw.shape[1]
@@ -81,14 +84,19 @@
     at = jnp.where(mirrored, rows + rows // 2 - share - own * share, own * share)
     at = pl.multiple_of(at, share)
     moves = [(freq_in, freq), (mask_in, mask), (target_in.at[:, pl.ds(at, share), :], raw)]
+    moves += [(taps_in, taps), (wave_hi_in, wave_hi), (wave_lo_in, wave_lo)]
     copies = [pltpu.make_async_copy(source, goal, sems.at[i]) for i, (source, goal) in enumerate(moves)]
     for copy in copies:
         copy.start()
     copies[0].wait()
     line = lax.broadcasted_iota(jnp.int32, (2 * count, 128), 0)
     f_freq = jnp.zeros((2 * count, 128), jnp.int32)
+    lane = lanes((8, 256))
+    turns = jnp.zeros((8, 256), jnp.int32)
     for i in range(count):
         f_freq = jnp.where((line == i) | (line == i + count), freq[i], f_freq)
+        turns = jnp.where((lane == i) | (lane == i + count) | (lane == i + 2 * count), freq[i], turns)
+    turns_ref[...] = turns
     f_full = jnp.concatenate([f_freq] * (rows // 128), 1)
     f_row = lax.broadcasted_iota(jnp.int32, (2 * count, rows), 0)
     turn = f_full * (2 * lanes((2 * count, rows)) + 1) + jnp.where(f_row >= count, rows // 2, 0)
@@ -109,38 +117,30 @@
     high, low = parts_of(mm3(f_parts, parts_of(mask[...])) * (1.0 / math.sqrt(rows)))
     packed_ref[0 : 2 * count, :] = high
     packed_ref[2 * count : 4 * count, :] = low
+    for copy in copies[3:]:
+        copy.wait()
 
 
 def tables_kernel(
-    node, freq_in, index_in, node_weights_in, chaos_in, weights_in, taps_in, wave_hi_in, wave_lo_in,
-    u_ref, cs_ref, gr_ref, gi_ref, wave_hi, wave_lo, scalars_ref,
-    freq, index, node_weights, chaos, weights, taps, sems,
+    node, turns_ref, index_in, node_weights_in, chaos_in, weights_in, taps, wave_hi, wave_lo,
+    u_ref, cs_ref, gr_ref, gi_ref, scalars_ref,
+    index, node_weights, chaos, weights, sems,
 ):
     rows = u_ref.shape[0]
-    count = freq.shape[0]
-    kernels, tap_count = taps.shape[1], taps.shape[4]
+    kernels, count, tap_count = taps.shape[1], taps.shape[3], taps.shape[4]
     span = wave_hi.shape[0]
     radius = (tap_count - 1) // 2
     nodes = index.shape[1]
     moves = [
-        (freq_in, freq),
         (index_in, index),
         (node_weights_in, node_weights),
         (chaos_in, chaos),
         (weights_in, weights),
-        (wave_hi_in, wave_hi),
-        (wave_lo_in, wave_lo),
-        (taps_in, taps),
     ]
     copies = [pltpu.make_async_copy(source, goal, sems.at[i]) for i, (source, goal) in enumerate(moves)]
     for copy in copies:
         copy.start()
-    for copy in copies[:4]:
-        copy.wait()
-    lane = lanes((8, 256))
-    turns = jnp.zeros((8, 256), jnp.int32)
-    for i in range(count):
-        turns = jnp.where((lane == i) | (lane == i + count) | (lane == i + 2 * count), freq[i], turns)
+    turns = turns_ref[...]
     quarter = rows // 2
     steps = lax.broadcasted_iota(jnp.int32, (8, 256), 0)
 
@@ -170,6 +170,8 @@
             high, low = parts_of(table)
             both = jnp.where(lane < 2 * count, high.astype(f32), low.astype(f32))
             cs_ref[start + i * first : start + (i + 1) * first, :] = both[:, : 3 * count].astype(bf16)
+    for copy in copies[:3]:
+        copy.wait()
     for n in range(nodes):
         poly = []
         for axis in range(2):
@@ -188,7 +190,7 @@
     scalars_ref[15:16, :] = jnp.full((1, 128), dose, f32)
     for j in range(len(degrees)):
         scalars_ref[16 * nodes + j : 16 * nodes + j + 1, :] = jnp.full((1, 128), chaos[j], f32)
-    for copy in copies[4:]:
+    for copy in copies[3:]:
         copy.wait()
     side = [jnp.concatenate([w[span - radius : span], w[0 : tap_count - radius]], 0) for w in (wave_hi, wave_lo)]
     scale = jnp.sqrt(weights[...]) * (1.0 / (span * math.sqrt(count)))
@@ -409,49 +411,48 @@
     inside = [(i, i ^ 1) for i in range(tiles) if i ^ 1 < tiles]
     across = [(i, ((i + 1) ^ 1) - 1) for i in range(tiles) if 0 <= ((i + 1) ^ 1) - 1 < tiles]
     wave_hi, wave_lo = (jnp.asarray(w) for w in column_waves(span))
-    packed, wanted, fh, fl = call(
+    packed, wanted, fh, fl, staged, wave_hi, wave_lo, turns = call(
         functools.partial(spectrum_kernel, radius),
         8,
-        [smem] + [hbm] * 3,
+        [smem] + [hbm] * 6,
         [
             shape_of(4 * count + half * terms, cols, dtype=bf16),
             shape_of(terms, share, cols, dtype=bf16),
             shape_of(2 * count, rows, dtype=bf16),
             shape_of(2 * count, rows, dtype=bf16),
+            shape_of(*taps.shape),
+            shape_of(span, 2 * span, dtype=bf16),
+            shape_of(span, 2 * span, dtype=bf16),
+            shape_of(8, 256, dtype=jnp.int32),
         ],
         [
             pltpu.SMEM(freq.shape, jnp.int32),
             pltpu.VMEM(mask.shape, f32),
             pltpu.VMEM((terms, share, cols), bf16),
-            pltpu.SemaphoreType.DMA((3,)),
-        ],
-    )(node, *kept(freq, mask, target))
+            pltpu.SemaphoreType.DMA((6,)),
+        ],
+    )(node, *kept(freq, mask, target, taps, wave_hi, wave_lo))
     border = lax.ppermute(packed, "tile", across)
-    u, cs, gr, gi, wave_hi, wave_lo, scalars = call(
+    twin = lax.ppermute(packed, "tile", inside)
+    u, cs, gr, gi, scalars = call(
         tables_kernel,
         16,
-        [smem] + [hbm] * 8,
+        [smem, vmem] + [hbm] * 4 + [vmem] + [vmem] * 2,
         [
             shape_of(rows, 384, dtype=bf16),
             shape_of(rows, 3 * count, dtype=bf16),
             shape_of(kernels, count, span),
             shape_of(kernels, count, span),
-            shape_of(span, 2 * span, dtype=bf16),
-            shape_of(span, 2 * span, dtype=bf16),
             shape_of(16 * nodes + 16, 128),
         ],
         [
-            pltpu.SMEM(freq.shape, jnp.int32),
             pltpu.SMEM((2, nodes), jnp.int32),
             pltpu.SMEM((nodes,), f32),
             pltpu.SMEM(chaos.shape, f32),
             pltpu.VMEM(weights.shape, f32),
-            pltpu.VMEM(taps.shape, f32),
-            pltpu.SemaphoreType.DMA((8,)),
-        ],
-    )(node, *kept(freq, node_index.T, node_weights, chaos, weights, taps, wave_hi, wave_lo))
-    ready, scalars = lax.optimization_barrier((packed, scalars))
-    twin = lax.ppermute(ready, "tile", inside)
+            pltpu.SemaphoreType.DMA((4,)),
+        ],
+    )(node, turns, *kept(node_index.T, node_weights, chaos, weights), staged, wave_hi, wave_lo)
     image, slope, fields = call(
         functools.partial(forward_kernel, radius, tiles),
         20,

time: 73.2 us -> 72.7 us (level)
    ppermute x1, waiting for transfers between devices: 1.03 us -> 0.01 us  [local(): twin = lax.ppermute(packed, 'tile', inside)]
  transfers between devices with their start and end apart: 2 -> 2, of which waited for: 2 -> 1; matrix products, arithmetic and copies ran while one was open for 0% -> 0% of each run, Pallas kernels for 3% -> 2%
where the time goes in v8:
time: 72.7 us; the launch traced here: 71.8 us
  blocking collectives  53.3 us (73%)
  Pallas kernels  9.51 us (13%)
  starting transfers between devices  7.48 us (10%)
  other arithmetic  0.78 us (1%)
    all_to_all x1, blocking collectives, local(): images = lax.all_to_all(image, 'node', 0, 0)  27.2 us
    all_to_all x1, blocking collectives, local(): lax.all_to_all((pressure * 8192.0).astype(jnp.float16), 'node', 0, 0)  13.6 us
    all_to_all x1, blocking collectives, local(): lax.all_to_all(spread.astype(jnp.float16), 'node', 0, 0).astype(f32)  12.5 us
    ppermute x1, starting transfers between devices, local(): border = lax.ppermute(packed, 'tile', across)  5.56 us
    pallas_call x1, Pallas kernels, local(): call(functools.partial(backward_kernel, radius), 16, [vmem] * 10, [shape_...  3.18 us
    pallas_call x1, Pallas kernels, local(): call(functools.partial(forward_kernel, radius, tiles), 20, [smem] + [vmem...  2.47 us
    ppermute x1, starting transfers between devices, local(): twin = lax.ppermute(packed, 'tile', inside)  1.92 us
    pallas_call x1, Pallas kernels, local(): call(functools.partial(spectrum_kernel, radius), 8, [smem] + [hbm] * 6, [...  1.51 us
  transfers between devices with their start and end apart: 2, of which 1 were waited for; matrix products, arithmetic and copies ran while one was open for 0% of the time, Pallas kernels for 2%

profile of v8, /device:TPU:112, one launch (start us, length us, event | category | flops | bytes accessed | tf_op | source)
XLA Modules:
  0.0 71.8 jit_solution(8911679053149786402)
XLA Ops:
  0.0 1.5 %shard_map.100 = (bf16[432,128]{1,0:T(8,128)(2,1)S(1)}, bf16[15,32,128]{2,1,0:T(8,128)(2,1)S(1)}, bf16[96,512]{1,0:T(8,128)(2,1)S(1)}, bf16[96,512]{1,0:T(8,128)...) custom-call(s32[1]{0:T(128)} %bitcast.1.node, ...), custom_call_target="tpu_custom_call" | custom-call | tf_op jit(solution)/shard_map/pallas_call | solution.py:414
  1.5 5.6 %collective-permute-start.1 = (bf16[432,128]{1,0:T(8,128)(2,1)S(1)}, bf16[432,128]{1,0:T(8,128)(2,1)S(1)}, u32[]{:S(2)}, u32[]{:S(2)}) collective-permute-start(bf16[432,128]{1,0:T(8,128)(2,1)S(1)} %get-tuple-element.26.packed), channel_id=1, source_target_pairs={{16,32},{32,16},{48,64},{64,48},{80,96},{96,80},{112,128},{128,112... | collective-permute-start | bytes 331784 | tf_op jit(solution)/shard_map/ppermute | solution.py:435
  7.1 1.9 %collective-permute-start = (bf16[432,128]{1,0:T(8,128)(2,1)S(1)}, bf16[432,128]{1,0:T(8,128)(2,1)S(1)}, u32[]{:S(2)}, u32[]{:S(2)}) collective-permute-start(bf16[432,128]{1,0:T(8,128)(2,1)S(1)} %get-tuple-element.26.packed), channel_id=1, source_target_pairs={{0,16},{16,0},{32,48},{48,32},{64,80},{80,64},{96,112},{112,96},{1... | collective-permute-start | bytes 331784 | tf_op jit(solution)/shard_map/ppermute | solution.py:436
  9.0 1.5 %shard_map.101 = (bf16[512,384]{1,0:T(8,128)(2,1)S(1)}, bf16[512,144]{1,0:T(8,128)(2,1)S(1)}, f32[8,48,256]{2,1,0:T(8,128)S(1)}, f32[8,48,256]{2,1,0:T(8,128)S(1)}, f32[272,128]{1,0:T(8,128)S(1)}) custom-call(s32[1]{0:T(128)} %bitcast.1.node, s32[8,256]{1,0:T(8,128)S(1)} %get-tuple-element.21.turns_ref, s32[2,16]{1,0:T(2,128)} %bitcast.5, ...), custom_call_target="tpu_custom_call" | custom-call | tf_op jit(solution)/shard_map/pallas_call | solution.py:437
  10.5 0.6 collective-permute-done.1.border
  11.1 0.0 collective-permute-done.twin
  11.1 2.5 %shard_map.102 = (bf16[16,48,128]{2,1,0:T(8,128)(2,1)S(1)}, f32[512,256]{1,0:T(8,128)S(1)}, f32[8,512,384]{2,1,0:T(8,128)S(1)}) custom-call(s32[1]{0:T(128)} %bitcast.tile, f32[272,128]{1,0:T(8,128)S(1)} %get-tuple-element.25.scalars, bf16[432,128]{1,0:T(8,128)(2,1)S(1)} %get-tuple-element.26.packed, bf16[432,128]{1,0:T(8,128)(2,1)S(1)} %collective-permute-done.twin, ...), custom_call_target="tpu_custom_call" | custom-call | tf_op jit(solution)/shard_map/pallas_call | solution.py:456
  13.6 27.2 %all_to_all.15.images = bf16[16,48,128]{2,1,0:T(8,128)(2,1)S(1)} all-to-all(bf16[16,48,128]{2,1,0:T(8,128)(2,1)S(1)} %get-tuple-element.30), channel_id=1, replica_groups=mesh['tile'=64,'node'=16] {'node'}, dimensions={0} | all-to-all | bytes 393216 | tf_op jit(solution)/shard_map/all_to_all | solution.py:472
  40.8 0.9 %shard_map.103 = f32[16,48,128]{2,1,0:T(8,128)S(1)} custom-call(s32[1]{0:T(128)} %bitcast.tile, bf16[16,48,128]{2,1,0:T(8,128)(2,1)S(1)} %all_to_all.15.images, bf16[15,32,128]{2,1,0:T(8,128)(2,1)S(1)} %get-tuple-element.31.wanted, bf16[432,128]{1,0:T(8,128)(2,1)S(1)} %collective-permute-done.twin, bf16[432,128]{1,0:T(8,128)(2,1)S(1)} %collective-permute-done.1.border, ...), custom_call_target="tpu_custom_call" | custom-call | tf_op jit(solution)/shard_map/pallas_call | solution.py:473
  41.8 13.6 %all_to_all.16 = f16[16,48,128]{2,1,0:T(8,128)(2,1)S(1)} all-to-all(f16[16,48,128]{2,1,0:T(8,128)(2,1)S(1)} %multiply_convert_fusion), channel_id=1, replica_groups=mesh['tile'=64,'node'=16] {'node'}, dimensions={0} | all-to-all | bytes 393216 | tf_op jit(solution)/shard_map/all_to_all | solution.py:476
  55.4 3.2 %shard_map.104 = f32[16,40,128]{2,1,0:T(8,128)S(1)} custom-call(f32[16,48,128]{2,1,0:T(8,128)S(1)} %convert_multiply_fusion.pressure, f32[512,256]{1,0:T(8,128)S(1)} %get-tuple-element.32.slope, f32[8,512,384]{2,1,0:T(8,128)S(1)} %get-tuple-element.33.fields, bf16[96,512]{1,0:T(8,128)(2,1)S(1)} %get-tuple-element.34.fh, ...), custom_call_target="tpu_custom_call" | custom-call | tf_op jit(solution)/shard_map/pallas_call | solution.py:477
  58.7 12.5 %all_to_all.17 = f16[16,40,128]{2,1,0:T(8,128)(2,1)S(1)} all-to-all(f16[16,40,128]{2,1,0:T(8,128)(2,1)S(1)} %convert_element_type.14), channel_id=1, replica_groups=mesh['tile'=64,'node'=16] {'node'}, dimensions={0} | all-to-all | bytes 327680 | tf_op jit(solution)/shard_map/all_to_all | solution.py:488
  71.2 0.6 fusion
  (5 shorter events, 0.1 us)
Async XLA Ops:
  1.5 9.6 %collective-permute-start.1 = (bf16[432,128]{1,0:T(8,128)(2,1)S(1)}, bf16[432,128]{1,0:T(8,128)(2,1)S(1)}, u32[]{:S(2)}, u32[]{:S(2)}) collective-permute-start(bf16[432,128]{1,0:T(8,128)(2,1)S(1)} %get-tuple-element.26.packed), channel_id=1, source_target_pairs={{16,32},{32,16},{48,64},{64,48},{80,96},{96,80},{112,128},{128,112... | collective-permute-start | bytes 331784 | tf_op jit(solution)/shard_map/ppermute | solution.py:435
  7.1 4.0 %collective-permute-start = (bf16[432,128]{1,0:T(8,128)(2,1)S(1)}, bf16[432,128]{1,0:T(8,128)(2,1)S(1)}, u32[]{:S(2)}, u32[]{:S(2)}) collective-permute-start(bf16[432,128]{1,0:T(8,128)(2,1)S(1)} %get-tuple-element.26.packed), channel_id=1, source_target_pairs={{0,16},{16,0},{32,48},{48,32},{64,80},{80,64},{96,112},{112,96},{1... | collective-permute-start | bytes 331784 | tf_op jit(solution)/shard_map/ppermute | solution.py:436

commit v9 on v8

--- a/solution.py
+++ b/solution.py
@@ -203,7 +203,7 @@
 
 
 def forward_kernel(
-    radius, tiles, tile, scalars, packed, twin, border, gr, gi, cs, wave_hi, wave_lo,
+    radius, tiles, tile, scalars, packed, border, twin, gr, gi, cs, wave_hi, wave_lo,
     image_ref, slope_ref, fields_ref, bh, bl, x, total,
 ):
     kernels, count, span = gr.shape
@@ -282,7 +282,7 @@
                 image_ref[n, 0:share, :] = rows_n.astype(bf16)
 
 
-def middle_kernel(radius, offset, tile, images, wanted, twin, border, scalars, pressure_ref):
+def middle_kernel(radius, offset, tile, images, wanted, border, twin, scalars, pressure_ref):
     nodes, slab, cols = images.shape
     share = wanted.shape[1]
     step = slab - share
@@ -432,8 +432,8 @@
             pltpu.SemaphoreType.DMA((6,)),
         ],
     )(node, *kept(freq, mask, target, taps, wave_hi, wave_lo))
+    twin = lax.ppermute(packed, "tile", inside)
     border = lax.ppermute(packed, "tile", across)
-    twin = lax.ppermute(packed, "tile", inside)
     u, cs, gr, gi, scalars = call(
         tables_kernel,
         16,
@@ -468,11 +468,11 @@
             pltpu.VMEM((kernels // 2, 2, 3 * count, 6 * cols), bf16),
             pltpu.VMEM((rows, 2 * cols), f32),
         ],
-    )(tile, scalars, packed, twin, border, gr, gi, cs, wave_hi, wave_lo)
+    )(tile, scalars, packed, border, twin, gr, gi, cs, wave_hi, wave_lo)
     images = lax.all_to_all(image, "node", 0, 0)
     (pressure,) = call(
         functools.partial(middle_kernel, radius, 4 * count), 8, [smem] + [vmem] * 5, [shape_of(nodes, slab, cols)]
-    )(tile, images, wanted, twin, border, scalars)
+    )(tile, images, wanted, border, twin, scalars)
     pressure = lax.all_to_all((pressure * 8192.0).astype(jnp.float16), "node", 0, 0).astype(f32) * (1.0 / 8192.0)
     (spread,) = call(
         functools.partial(backward_kernel, radius),

time: 72.7 us -> 73.3 us (level)
  the two profiles are of different devices: /device:TPU:112 before, /device:TPU:80 now
where the time goes in v9:
time: 73.3 us; the launch traced here: 73 us
  blocking collectives  51.6 us (70%)
  Pallas kernels  9.51 us (13%)
  starting transfers between devices  7.25 us (10%)
  waiting for transfers between devices  3.75 us (5%)
  other arithmetic  0.78 us (1%)
    all_to_all x1, blocking collectives, local(): images = lax.all_to_all(image, 'node', 0, 0)  26.9 us
    all_to_all x1, blocking collectives, local(): lax.all_to_all(spread.astype(jnp.float16), 'node', 0, 0).astype(f32)  12.4 us
    all_to_all x1, blocking collectives, local(): lax.all_to_all((pressure * 8192.0).astype(jnp.float16), 'node', 0, 0)  12.3 us
    ppermute x1, starting transfers between devices, local(): border = lax.ppermute(packed, 'tile', across)  5.33 us
    ppermute x1, waiting for transfers between devices, local(): border = lax.ppermute(packed, 'tile', across)  3.75 us
    pallas_call x1, Pallas kernels, local(): call(functools.partial(backward_kernel, radius), 16, [vmem] * 10, [shape_...  3.18 us
    pallas_call x1, Pallas kernels, local(): call(functools.partial(forward_kernel, radius, tiles), 20, [smem] + [vmem...  2.47 us
    ppermute x1, starting transfers between devices, local(): twin = lax.ppermute(packed, 'tile', inside)  1.92 us
  transfers between devices with their start and end apart: 2, of which 1 were waited for; matrix products, arithmetic and copies ran while one was open for 0% of the time, Pallas kernels for 2%

profile of v9, /device:TPU:80, one launch (start us, length us, event | category | flops | bytes accessed | tf_op | source)
XLA Modules:
  0.0 73.0 jit_solution(7447710622925904171)
XLA Ops:
  0.0 1.5 %shard_map.100 = (bf16[432,128]{1,0:T(8,128)(2,1)S(1)}, bf16[15,32,128]{2,1,0:T(8,128)(2,1)S(1)}, bf16[96,512]{1,0:T(8,128)(2,1)S(1)}, bf16[96,512]{1,0:T(8,128)...) custom-call(s32[1]{0:T(128)} %bitcast.1.node, ...), custom_call_target="tpu_custom_call" | custom-call | tf_op jit(solution)/shard_map/pallas_call | solution.py:414
  1.5 1.9 %collective-permute-start.1 = (bf16[432,128]{1,0:T(8,128)(2,1)S(1)}, bf16[432,128]{1,0:T(8,128)(2,1)S(1)}, u32[]{:S(2)}, u32[]{:S(2)}) collective-permute-start(bf16[432,128]{1,0:T(8,128)(2,1)S(1)} %get-tuple-element.26.packed), channel_id=1, source_target_pairs={{0,16},{16,0},{32,48},{48,32},{64,80},{80,64},{96,112},{112,96},{1... | collective-permute-start | bytes 331784 | tf_op jit(solution)/shard_map/ppermute | solution.py:435
  3.4 5.3 %collective-permute-start = (bf16[432,128]{1,0:T(8,128)(2,1)S(1)}, bf16[432,128]{1,0:T(8,128)(2,1)S(1)}, u32[]{:S(2)}, u32[]{:S(2)}) collective-permute-start(bf16[432,128]{1,0:T(8,128)(2,1)S(1)} %get-tuple-element.26.packed), channel_id=1, source_target_pairs={{16,32},{32,16},{48,64},{64,48},{80,96},{96,80},{112,128},{128,112... | collective-permute-start | bytes 331784 | tf_op jit(solution)/shard_map/ppermute | solution.py:436
  8.8 1.5 %shard_map.101 = (bf16[512,384]{1,0:T(8,128)(2,1)S(1)}, bf16[512,144]{1,0:T(8,128)(2,1)S(1)}, f32[8,48,256]{2,1,0:T(8,128)S(1)}, f32[8,48,256]{2,1,0:T(8,128)S(1)}, f32[272,128]{1,0:T(8,128)S(1)}) custom-call(s32[1]{0:T(128)} %bitcast.1.node, s32[8,256]{1,0:T(8,128)S(1)} %get-tuple-element.21.turns_ref, s32[2,16]{1,0:T(2,128)} %bitcast.5, ...), custom_call_target="tpu_custom_call" | custom-call | tf_op jit(solution)/shard_map/pallas_call | solution.py:437
  10.3 0.0 collective-permute-done.1.twin
  10.3 3.7 %collective-permute-done.border = bf16[432,128]{1,0:T(8,128)(2,1)S(1)} collective-permute-done((bf16[432,128]{1,0:T(8,128)(2,1)S(1)}, bf16[432,128]{1,0:T(8,128)(2,1)S(1)}, u32[]{:S(2)}, u32[]{:S(2)}) %collective-permute-start) | collective-permute-done | bytes 110624 | tf_op jit(solution)/shard_map/ppermute | solution.py:436
  14.0 2.5 %shard_map.102 = (bf16[16,48,128]{2,1,0:T(8,128)(2,1)S(1)}, f32[512,256]{1,0:T(8,128)S(1)}, f32[8,512,384]{2,1,0:T(8,128)S(1)}) custom-call(s32[1]{0:T(128)} %bitcast.tile, f32[272,128]{1,0:T(8,128)S(1)} %get-tuple-element.25.scalars, bf16[432,128]{1,0:T(8,128)(2,1)S(1)} %get-tuple-element.26.packed, bf16[432,128]{1,0:T(8,128)(2,1)S(1)} %collective-permute-done.border, ...), custom_call_target="tpu_custom_call" | custom-call | tf_op jit(solution)/shard_map/pallas_call | solution.py:456
  16.5 26.9 %all_to_all.15.images = bf16[16,48,128]{2,1,0:T(8,128)(2,1)S(1)} all-to-all(bf16[16,48,128]{2,1,0:T(8,128)(2,1)S(1)} %get-tuple-element.30), channel_id=1, replica_groups=mesh['tile'=64,'node'=16] {'node'}, dimensions={0} | all-to-all | bytes 393216 | tf_op jit(solution)/shard_map/all_to_all | solution.py:472
  43.4 0.9 %shard_map.103 = f32[16,48,128]{2,1,0:T(8,128)S(1)} custom-call(s32[1]{0:T(128)} %bitcast.tile, bf16[16,48,128]{2,1,0:T(8,128)(2,1)S(1)} %all_to_all.15.images, bf16[15,32,128]{2,1,0:T(8,128)(2,1)S(1)} %get-tuple-element.31.wanted, bf16[432,128]{1,0:T(8,128)(2,1)S(1)} %collective-permute-done.border, bf16[432,128]{1,0:T(8,128)(2,1)S(1)} %collective-permute-done.1.twin, ...), custom_call_target="tpu_custom_call" | custom-call | tf_op jit(solution)/shard_map/pallas_call | solution.py:473
  44.3 12.3 %all_to_all.16 = f16[16,48,128]{2,1,0:T(8,128)(2,1)S(1)} all-to-all(f16[16,48,128]{2,1,0:T(8,128)(2,1)S(1)} %multiply_convert_fusion), channel_id=1, replica_groups=mesh['tile'=64,'node'=16] {'node'}, dimensions={0} | all-to-all | bytes 393216 | tf_op jit(solution)/shard_map/all_to_all | solution.py:476
  56.7 3.2 %shard_map.104 = f32[16,40,128]{2,1,0:T(8,128)S(1)} custom-call(f32[16,48,128]{2,1,0:T(8,128)S(1)} %convert_multiply_fusion.pressure, f32[512,256]{1,0:T(8,128)S(1)} %get-tuple-element.32.slope, f32[8,512,384]{2,1,0:T(8,128)S(1)} %get-tuple-element.33.fields, bf16[96,512]{1,0:T(8,128)(2,1)S(1)} %get-tuple-element.34.fh, ...), custom_call_target="tpu_custom_call" | custom-call | tf_op jit(solution)/shard_map/pallas_call | solution.py:477
  59.9 12.4 %all_to_all.17 = f16[16,40,128]{2,1,0:T(8,128)(2,1)S(1)} all-to-all(f16[16,40,128]{2,1,0:T(8,128)(2,1)S(1)} %convert_element_type.14), channel_id=1, replica_groups=mesh['tile'=64,'node'=16] {'node'}, dimensions={0} | all-to-all | bytes 327680 | tf_op jit(solution)/shard_map/all_to_all | solution.py:488
  72.4 0.6 fusion
  (5 shorter events, 0.1 us)
Async XLA Ops:
  1.5 8.7 %collective-permute-start.1 = (bf16[432,128]{1,0:T(8,128)(2,1)S(1)}, bf16[432,128]{1,0:T(8,128)(2,1)S(1)}, u32[]{:S(2)}, u32[]{:S(2)}) collective-permute-start(bf16[432,128]{1,0:T(8,128)(2,1)S(1)} %get-tuple-element.26.packed), channel_id=1, source_target_pairs={{0,16},{16,0},{32,48},{48,32},{64,80},{80,64},{96,112},{112,96},{1... | collective-permute-start | bytes 331784 | tf_op jit(solution)/shard_map/ppermute | solution.py:435
  3.4 10.6 %collective-permute-start = (bf16[432,128]{1,0:T(8,128)(2,1)S(1)}, bf16[432,128]{1,0:T(8,128)(2,1)S(1)}, u32[]{:S(2)}, u32[]{:S(2)}) collective-permute-start(bf16[432,128]{1,0:T(8,128)(2,1)S(1)} %get-tuple-element.26.packed), channel_id=1, source_target_pairs={{16,32},{32,16},{48,64},{64,48},{80,96},{96,80},{112,128},{128,112... | collective-permute-start | bytes 331784 | tf_op jit(solution)/shard_map/ppermute | solution.py:436

commit v10 on v9

--- a/solution.py
+++ b/solution.py
@@ -203,7 +203,7 @@
 
 
 def forward_kernel(
-    radius, tiles, tile, scalars, packed, border, twin, gr, gi, cs, wave_hi, wave_lo,
+    radius, tiles, tile, scalars, packed, after, before, gr, gi, cs, wave_hi, wave_lo,
     image_ref, slope_ref, fields_ref, bh, bl, x, total,
 ):
     kernels, count, span = gr.shape
@@ -211,12 +211,11 @@
     rows = slope_ref.shape[0]
     share = rows // nodes
     half = share // 2
-    even = lax.rem(tile[0], 2) == 0
-    near = (lanes((2 * count, cols)) < 2 * radius) == even
+    near = lanes((2 * count, cols)) < 2 * radius
     pair = []
     for part in range(2):
         at = pl.ds(2 * part * count, 2 * count)
-        beyond = jnp.where(near, twin[at, :].astype(f32), border[at, :].astype(f32))
+        beyond = jnp.where(near, after[at, :].astype(f32), before[at, :].astype(f32))
         pair.append(jnp.concatenate([packed[at, :], beyond.astype(bf16)], 1))
     wave = (wave_hi[...], wave_lo[...])
     prod = mm3(pair, wave)
@@ -282,11 +281,11 @@
                 image_ref[n, 0:share, :] = rows_n.astype(bf16)
 
 
-def middle_kernel(radius, offset, tile, images, wanted, border, twin, scalars, pressure_ref):
+def middle_kernel(radius, offset, images, wanted, after, before, scalars, pressure_ref):
     nodes, slab, cols = images.shape
     share = wanted.shape[1]
     step = slab - share
-    near = right_lanes((step, cols), radius) == (lax.rem(tile[0], 2) == 0)
+    near = right_lanes((step, cols), radius)
     for first in range(0, slab, step):
         image = [images[n, first : first + step, :].astype(f32) for n in range(nodes)]
         pressure = [None] * nodes
@@ -299,7 +298,7 @@
                 goal = wanted[j, first : first + step, :].astype(f32)
             else:
                 at = pl.ds(offset + j * step, step)
-                goal = jnp.where(near, twin[at, :].astype(f32), border[at, :].astype(f32))
+                goal = jnp.where(near, after[at, :].astype(f32), before[at, :].astype(f32))
             mixed = scalars[16 * nodes + j : 16 * nodes + j + 1, :] * jnp.tanh(coefficient - goal)
             for n in range(nodes):
                 term = weight[n] * mixed
@@ -408,8 +407,8 @@
     share = rows // nodes
     half = share // 2
     slab = share + half
-    inside = [(i, i ^ 1) for i in range(tiles) if i ^ 1 < tiles]
-    across = [(i, ((i + 1) ^ 1) - 1) for i in range(tiles) if 0 <= ((i + 1) ^ 1) - 1 < tiles]
+    up = [(i, i + 1) for i in range(tiles - 1)]
+    down = [(i + 1, i) for i in range(tiles - 1)]
     wave_hi, wave_lo = (jnp.asarray(w) for w in column_waves(span))
     packed, wanted, fh, fl, staged, wave_hi, wave_lo, turns = call(
         functools.partial(spectrum_kernel, radius),
@@ -432,8 +431,8 @@
             pltpu.SemaphoreType.DMA((6,)),
         ],
     )(node, *kept(freq, mask, target, taps, wave_hi, wave_lo))
-    twin = lax.ppermute(packed, "tile", inside)
-    border = lax.ppermute(packed, "tile", across)
+    before = lax.ppermute(packed, "tile", up)
+    after = lax.ppermute(packed, "tile", down)
     u, cs, gr, gi, scalars = call(
         tables_kernel,
         16,
@@ -468,11 +467,11 @@
             pltpu.VMEM((kernels // 2, 2, 3 * count, 6 * cols), bf16),
             pltpu.VMEM((rows, 2 * cols), f32),
         ],
-    )(tile, scalars, packed, border, twin, gr, gi, cs, wave_hi, wave_lo)
+    )(tile, scalars, packed, after, before, gr, gi, cs, wave_hi, wave_lo)
     images = lax.all_to_all(image, "node", 0, 0)
     (pressure,) = call(
-        functools.partial(middle_kernel, radius, 4 * count), 8, [smem] + [vmem] * 5, [shape_of(nodes, slab, cols)]
-    )(tile, images, wanted, border, twin, scalars)
+        functools.partial(middle_kernel, radius, 4 * count), 8, [vmem] * 5, [shape_of(nodes, slab, cols)]
+    )(images, wanted, after, before, scalars)
     pressure = lax.all_to_all((pressure * 8192.0).astype(jnp.float16), "node", 0, 0).astype(f32) * (1.0 / 8192.0)
     (spread,) = call(
         functools.partial(backward_kernel, radius),

time: 73.3 us -> 73.3 us (level)
  the two profiles are of different devices: /device:TPU:80 before, /device:TPU:47 now
where the time goes in v10:
time: 73.3 us; the launch traced here: 73 us
  blocking collectives  47.2 us (64%)
  Pallas kernels  9.51 us (13%)
  starting transfers between devices  7.94 us (11%)
  waiting for transfers between devices  7.54 us (10%)
  other arithmetic  0.78 us (1%)
    all_to_all x1, blocking collectives, local(): images = lax.all_to_all(image, 'node', 0, 0)  25.6 us
    all_to_all x1, blocking collectives, local(): lax.all_to_all((pressure * 8192.0).astype(jnp.float16), 'node', 0, 0)  10.8 us
    all_to_all x1, blocking collectives, local(): lax.all_to_all(spread.astype(jnp.float16), 'node', 0, 0).astype(f32)  10.7 us
    ppermute x1, waiting for transfers between devices, local(): after = lax.ppermute(packed, 'tile', down)  7.54 us
    ppermute x1, starting transfers between devices, local(): before = lax.ppermute(packed, 'tile', up)  6.02 us
    pallas_call x1, Pallas kernels, local(): call(functools.partial(backward_kernel, radius), 16, [vmem] * 10, [shape_...  3.18 us
    pallas_call x1, Pallas kernels, local(): call(functools.partial(forward_kernel, radius, tiles), 20, [smem] + [vmem...  2.46 us
    ppermute x1, starting transfers between devices, local(): after = lax.ppermute(packed, 'tile', down)  1.92 us
  transfers between devices with their start and end apart: 2, of which 1 were waited for; matrix products, arithmetic and copies ran while one was open for 0% of the time, Pallas kernels for 2%

profile of v10, /device:TPU:47, one launch (start us, length us, event | category | flops | bytes accessed | tf_op | source)
XLA Modules:
  0.0 73.0 jit_solution(6497168767095583509)
XLA Ops:
  0.0 1.5 %shard_map.100 = (bf16[432,128]{1,0:T(8,128)(2,1)S(1)}, bf16[15,32,128]{2,1,0:T(8,128)(2,1)S(1)}, bf16[96,512]{1,0:T(8,128)(2,1)S(1)}, bf16[96,512]{1,0:T(8,128)...) custom-call(s32[1]{0:T(128)} %bitcast.1.node, ...), custom_call_target="tpu_custom_call" | custom-call | tf_op jit(solution)/shard_map/pallas_call | solution.py:413
  1.5 6.0 %collective-permute-start.1 = (bf16[432,128]{1,0:T(8,128)(2,1)S(1)}, bf16[432,128]{1,0:T(8,128)(2,1)S(1)}, u32[]{:S(2)}, u32[]{:S(2)}) collective-permute-start(bf16[432,128]{1,0:T(8,128)(2,1)S(1)} %get-tuple-element.26.packed), channel_id=1, source_target_pairs={{0,16},{16,32},{32,48},{48,64},{64,80},{80,96},{96,112},{112,128},... | collective-permute-start | bytes 331784 | tf_op jit(solution)/shard_map/ppermute | solution.py:434
  7.5 1.9 %collective-permute-start = (bf16[432,128]{1,0:T(8,128)(2,1)S(1)}, bf16[432,128]{1,0:T(8,128)(2,1)S(1)}, u32[]{:S(2)}, u32[]{:S(2)}) collective-permute-start(bf16[432,128]{1,0:T(8,128)(2,1)S(1)} %get-tuple-element.26.packed), channel_id=1, source_target_pairs={{16,0},{32,16},{48,32},{64,48},{80,64},{96,80},{112,96},{128,112},... | collective-permute-start | bytes 331784 | tf_op jit(solution)/shard_map/ppermute | solution.py:435
  9.5 1.5 %shard_map.101 = (bf16[512,384]{1,0:T(8,128)(2,1)S(1)}, bf16[512,144]{1,0:T(8,128)(2,1)S(1)}, f32[8,48,256]{2,1,0:T(8,128)S(1)}, f32[8,48,256]{2,1,0:T(8,128)S(1)}, f32[272,128]{1,0:T(8,128)S(1)}) custom-call(s32[1]{0:T(128)} %bitcast.1.node, s32[8,256]{1,0:T(8,128)S(1)} %get-tuple-element.21.turns_ref, s32[2,16]{1,0:T(2,128)} %bitcast.5, ...), custom_call_target="tpu_custom_call" | custom-call | tf_op jit(solution)/shard_map/pallas_call | solution.py:436
  11.0 0.0 collective-permute-done.1.before
  11.0 7.5 %collective-permute-done.after = bf16[432,128]{1,0:T(8,128)(2,1)S(1)} collective-permute-done((bf16[432,128]{1,0:T(8,128)(2,1)S(1)}, bf16[432,128]{1,0:T(8,128)(2,1)S(1)}, u32[]{:S(2)}, u32[]{:S(2)}) %collective-permute-start) | collective-permute-done | bytes 110624 | tf_op jit(solution)/shard_map/ppermute | solution.py:435
  18.5 2.5 %shard_map.102 = (bf16[16,48,128]{2,1,0:T(8,128)(2,1)S(1)}, f32[512,256]{1,0:T(8,128)S(1)}, f32[8,512,384]{2,1,0:T(8,128)S(1)}) custom-call(s32[1]{0:T(128)} %bitcast.tile, f32[272,128]{1,0:T(8,128)S(1)} %get-tuple-element.25.scalars, bf16[432,128]{1,0:T(8,128)(2,1)S(1)} %get-tuple-element.26.packed, bf16[432,128]{1,0:T(8,128)(2,1)S(1)} %collective-permute-done.after, ...), custom_call_target="tpu_custom_call" | custom-call | tf_op jit(solution)/shard_map/pallas_call | solution.py:455
  21.0 25.6 %all_to_all.15.images = bf16[16,48,128]{2,1,0:T(8,128)(2,1)S(1)} all-to-all(bf16[16,48,128]{2,1,0:T(8,128)(2,1)S(1)} %get-tuple-element.30), channel_id=1, replica_groups=mesh['tile'=64,'node'=16] {'node'}, dimensions={0} | all-to-all | bytes 393216 | tf_op jit(solution)/shard_map/all_to_all | solution.py:471
  46.6 0.9 %shard_map.103 = f32[16,48,128]{2,1,0:T(8,128)S(1)} custom-call(bf16[16,48,128]{2,1,0:T(8,128)(2,1)S(1)} %all_to_all.15.images, bf16[15,32,128]{2,1,0:T(8,128)(2,1)S(1)} %get-tuple-element.31.wanted, bf16[432,128]{1,0:T(8,128)(2,1)S(1)} %collective-permute-done.after, bf16[432,128]{1,0:T(8,128)(2,1)S(1)} %collective-permute-done.1.before, ...), custom_call_target="tpu_custom_call" | custom-call | tf_op jit(solution)/shard_map/pallas_call | solution.py:472
  47.5 10.8 %all_to_all.16 = f16[16,48,128]{2,1,0:T(8,128)(2,1)S(1)} all-to-all(f16[16,48,128]{2,1,0:T(8,128)(2,1)S(1)} %multiply_convert_fusion), channel_id=1, replica_groups=mesh['tile'=64,'node'=16] {'node'}, dimensions={0} | all-to-all | bytes 393216 | tf_op jit(solution)/shard_map/all_to_all | solution.py:475
  58.4 3.2 %shard_map.104 = f32[16,40,128]{2,1,0:T(8,128)S(1)} custom-call(f32[16,48,128]{2,1,0:T(8,128)S(1)} %convert_multiply_fusion.pressure, f32[512,256]{1,0:T(8,128)S(1)} %get-tuple-element.32.slope, f32[8,512,384]{2,1,0:T(8,128)S(1)} %get-tuple-element.33.fields, bf16[96,512]{1,0:T(8,128)(2,1)S(1)} %get-tuple-element.34.fh, ...), custom_call_target="tpu_custom_call" | custom-call | tf_op jit(solution)/shard_map/pallas_call | solution.py:476
  61.6 10.7 %all_to_all.17 = f16[16,40,128]{2,1,0:T(8,128)(2,1)S(1)} all-to-all(f16[16,40,128]{2,1,0:T(8,128)(2,1)S(1)} %convert_element_type.14), channel_id=1, replica_groups=mesh['tile'=64,'node'=16] {'node'}, dimensions={0} | all-to-all | bytes 327680 | tf_op jit(solution)/shard_map/all_to_all | solution.py:487
  72.4 0.6 fusion
  (5 shorter events, 0.1 us)
Async XLA Ops:
  1.5 9.4 %collective-permute-start.1 = (bf16[432,128]{1,0:T(8,128)(2,1)S(1)}, bf16[432,128]{1,0:T(8,128)(2,1)S(1)}, u32[]{:S(2)}, u32[]{:S(2)}) collective-permute-start(bf16[432,128]{1,0:T(8,128)(2,1)S(1)} %get-tuple-element.26.packed), channel_id=1, source_target_pairs={{0,16},{16,32},{32,48},{48,64},{64,80},{80,96},{96,112},{112,128},... | collective-permute-start | bytes 331784 | tf_op jit(solution)/shard_map/ppermute | solution.py:434
  7.5 11.0 %collective-permute-start = (bf16[432,128]{1,0:T(8,128)(2,1)S(1)}, bf16[432,128]{1,0:T(8,128)(2,1)S(1)}, u32[]{:S(2)}, u32[]{:S(2)}) collective-permute-start(bf16[432,128]{1,0:T(8,128)(2,1)S(1)} %get-tuple-element.26.packed), channel_id=1, source_target_pairs={{16,0},{32,16},{48,32},{64,48},{80,64},{96,80},{112,96},{128,112},... | collective-permute-start | bytes 331784 | tf_op jit(solution)/shard_map/ppermute | solution.py:435

commit v11 on v7

--- a/solution.py
+++ b/solution.py
@@ -427,6 +427,7 @@
         ],
     )(node, *kept(freq, mask, target))
     border = lax.ppermute(packed, "tile", across)
+    twin = lax.ppermute(packed, "tile", inside)
     u, cs, gr, gi, wave_hi, wave_lo, scalars = call(
         tables_kernel,
         16,
@@ -450,8 +451,6 @@
             pltpu.SemaphoreType.DMA((8,)),
         ],
     )(node, *kept(freq, node_index.T, node_weights, chaos, weights, taps, wave_hi, wave_lo))
-    ready, scalars = lax.optimization_barrier((packed, scalars))
-    twin = lax.ppermute(ready, "tile", inside)
     image, slope, fields = call(
         functools.partial(forward_kernel, radius, tiles),
         20,

time: 73.2 us -> 72.8 us (level)
  waiting for transfers between devices: 1.28 us -> 0.25 us
    ppermute x1, waiting for transfers between devices: 1.03 us -> 0.01 us  [local(): twin = lax.ppermute(packed, 'tile', inside)]
  transfers between devices with their start and end apart: 2 -> 2, of which waited for: 2 -> 1; matrix products, arithmetic and copies ran while one was open for 0% -> 0% of each run, Pallas kernels for 3% -> 3%
where the time goes in v11:
time: 72.8 us; the launch traced here: 71.9 us
  blocking collectives  53.7 us (74%)
  Pallas kernels  9.66 us (13%)
  starting transfers between devices  7.48 us (10%)
  other arithmetic  0.78 us (1%)
    all_to_all x1, blocking collectives, local(): images = lax.all_to_all(image, 'node', 0, 0)  28 us
    all_to_all x1, blocking collectives, local(): lax.all_to_all((pressure * 8192.0).astype(jnp.float16), 'node', 0, 0)  13.2 us
    all_to_all x1, blocking collectives, local(): lax.all_to_all(spread.astype(jnp.float16), 'node', 0, 0).astype(f32)  12.4 us
    ppermute x1, starting transfers between devices, local(): border = lax.ppermute(packed, 'tile', across)  5.56 us
    pallas_call x1, Pallas kernels, local(): call(functools.partial(backward_kernel, radius), 16, [vmem] * 10, [shape_...  3.13 us
    pallas_call x1, Pallas kernels, local(): call(functools.partial(forward_kernel, radius, tiles), 20, [smem] + [vmem...  2.4 us
    ppermute x1, starting transfers between devices, local(): twin = lax.ppermute(packed, 'tile', inside)  1.92 us
    pallas_call x1, Pallas kernels, local(): call(tables_kernel, 16, [smem] + [hbm] * 8, [shape_of(rows, 384, dtype=bf...  1.83 us
  transfers between devices with their start and end apart: 2, of which 1 were waited for; matrix products, arithmetic and copies ran while one was open for 0% of the time, Pallas kernels for 3%

profile of v11, /device:TPU:112, one launch (start us, length us, event | category | flops | bytes accessed | tf_op | source)
XLA Modules:
  0.0 71.9 jit_solution(18110053582696530075)
XLA Ops:
  0.0 1.5 %shard_map.101 = (bf16[432,128]{1,0:T(8,128)(2,1)S(1)}, bf16[15,32,128]{2,1,0:T(8,128)(2,1)S(1)}, bf16[96,512]{1,0:T(8,128)(2,1)S(1)}, bf16[96,512]{1,0:T(8,128)(2,1)S(1)}) custom-call(s32[1]{0:T(128)} %bitcast.1.node, s32[48]{0:T(128)} %freq_in.3, f32[512,128]{1,0:T(8,128)} %mask_in.1, bf16[15,512,128]{2,1,0:T(8,128)(2,1)} %target_in.1), custom_call_target="tpu_custom_call" | custom-call | tf_op jit(solution)/shard_map/pallas_call | solution.py:412
  1.5 5.6 %collective-permute-start.1 = (bf16[432,128]{1,0:T(8,128)(2,1)S(1)}, bf16[432,128]{1,0:T(8,128)(2,1)S(1)}, u32[]{:S(2)}, u32[]{:S(2)}) collective-permute-start(bf16[432,128]{1,0:T(8,128)(2,1)S(1)} %get-tuple-element.20.packed), channel_id=1, source_target_pairs={{16,32},{32,16},{48,64},{64,48},{80,96},{96,80},{112,128},{128,112... | collective-permute-start | bytes 331784 | tf_op jit(solution)/shard_map/ppermute | solution.py:429
  7.1 1.9 %collective-permute-start = (bf16[432,128]{1,0:T(8,128)(2,1)S(1)}, bf16[432,128]{1,0:T(8,128)(2,1)S(1)}, u32[]{:S(2)}, u32[]{:S(2)}) collective-permute-start(bf16[432,128]{1,0:T(8,128)(2,1)S(1)} %get-tuple-element.20.packed), channel_id=1, source_target_pairs={{0,16},{16,0},{32,48},{48,32},{64,80},{80,64},{96,112},{112,96},{1... | collective-permute-start | bytes 331784 | tf_op jit(solution)/shard_map/ppermute | solution.py:430
  9.0 1.8 %shard_map.100 = (bf16[512,384]{1,0:T(8,128)(2,1)S(1)}, bf16[512,144]{1,0:T(8,128)(2,1)S(1)}, f32[8,48,256]{2,1,0:T(8,128)S(1)}, f32[8,48,256]{2,1,0:T(8,128)S(1...) custom-call(s32[1]{0:T(128)} %bitcast.1.node, s32[48]{0:T(128)} %freq_in.3, ...), custom_call_target="tpu_custom_call" | custom-call | tf_op jit(solution)/shard_map/pallas_call | solution.py:431
  10.8 0.2 collective-permute-done.1.border
  11.1 0.0 collective-permute-done.twin
  11.1 2.4 %shard_map.102 = (bf16[16,48,128]{2,1,0:T(8,128)(2,1)S(1)}, f32[512,256]{1,0:T(8,128)S(1)}, f32[8,512,384]{2,1,0:T(8,128)S(1)}) custom-call(s32[1]{0:T(128)} %bitcast.tile, f32[272,128]{1,0:T(8,128)S(1)} %get-tuple-element.19.scalars, bf16[432,128]{1,0:T(8,128)(2,1)S(1)} %get-tuple-element.20.packed, bf16[432,128]{1,0:T(8,128)(2,1)S(1)} %collective-permute-done.twin, ...), custom_call_target="tpu_custom_call" | custom-call | tf_op jit(solution)/shard_map/pallas_call | solution.py:454
  13.5 28.0 %all_to_all.15.images = bf16[16,48,128]{2,1,0:T(8,128)(2,1)S(1)} all-to-all(bf16[16,48,128]{2,1,0:T(8,128)(2,1)S(1)} %get-tuple-element.26), channel_id=1, replica_groups=mesh['tile'=64,'node'=16] {'node'}, dimensions={0} | all-to-all | bytes 393216 | tf_op jit(solution)/shard_map/all_to_all | solution.py:470
  41.5 0.8 %shard_map.103 = f32[16,48,128]{2,1,0:T(8,128)S(1)} custom-call(s32[1]{0:T(128)} %bitcast.tile, bf16[16,48,128]{2,1,0:T(8,128)(2,1)S(1)} %all_to_all.15.images, bf16[15,32,128]{2,1,0:T(8,128)(2,1)S(1)} %get-tuple-element.27.wanted, bf16[432,128]{1,0:T(8,128)(2,1)S(1)} %collective-permute-done.twin, bf16[432,128]{1,0:T(8,128)(2,1)S(1)} %collective-permute-done.1.border, ...), custom_call_target="tpu_custom_call" | custom-call | tf_op jit(solution)/shard_map/pallas_call | solution.py:471
  42.4 13.2 %all_to_all.16 = f16[16,48,128]{2,1,0:T(8,128)(2,1)S(1)} all-to-all(f16[16,48,128]{2,1,0:T(8,128)(2,1)S(1)} %multiply_convert_fusion), channel_id=1, replica_groups=mesh['tile'=64,'node'=16] {'node'}, dimensions={0} | all-to-all | bytes 393216 | tf_op jit(solution)/shard_map/all_to_all | solution.py:474
  55.6 3.1 %shard_map.104 = f32[16,40,128]{2,1,0:T(8,128)S(1)} custom-call(f32[16,48,128]{2,1,0:T(8,128)S(1)} %convert_multiply_fusion.pressure, f32[512,256]{1,0:T(8,128)S(1)} %get-tuple-element.28.slope, f32[8,512,384]{2,1,0:T(8,128)S(1)} %get-tuple-element.29.fields, bf16[96,512]{1,0:T(8,128)(2,1)S(1)} %get-tuple-element.30.fh, ...), custom_call_target="tpu_custom_call" | custom-call | tf_op jit(solution)/shard_map/pallas_call | solution.py:475
  58.8 12.4 %all_to_all.17 = f16[16,40,128]{2,1,0:T(8,128)(2,1)S(1)} all-to-all(f16[16,40,128]{2,1,0:T(8,128)(2,1)S(1)} %convert_element_type.14), channel_id=1, replica_groups=mesh['tile'=64,'node'=16] {'node'}, dimensions={0} | all-to-all | bytes 327680 | tf_op jit(solution)/shard_map/all_to_all | solution.py:486
  71.3 0.6 fusion
  (5 shorter events, 0.1 us)
Async XLA Ops:
  1.5 9.6 %collective-permute-start.1 = (bf16[432,128]{1,0:T(8,128)(2,1)S(1)}, bf16[432,128]{1,0:T(8,128)(2,1)S(1)}, u32[]{:S(2)}, u32[]{:S(2)}) collective-permute-start(bf16[432,128]{1,0:T(8,128)(2,1)S(1)} %get-tuple-element.20.packed), channel_id=1, source_target_pairs={{16,32},{32,16},{48,64},{64,48},{80,96},{96,80},{112,128},{128,112... | collective-permute-start | bytes 331784 | tf_op jit(solution)/shard_map/ppermute | solution.py:429
  7.1 4.0 %collective-permute-start = (bf16[432,128]{1,0:T(8,128)(2,1)S(1)}, bf16[432,128]{1,0:T(8,128)(2,1)S(1)}, u32[]{:S(2)}, u32[]{:S(2)}) collective-permute-start(bf16[432,128]{1,0:T(8,128)(2,1)S(1)} %get-tuple-element.20.packed), channel_id=1, source_target_pairs={{0,16},{16,0},{32,48},{48,32},{64,80},{80,64},{96,112},{112,96},{1... | collective-permute-start | bytes 331784 | tf_op jit(solution)/shard_map/ppermute | solution.py:430
